TPU v7x, 32 devices: a whole 2x2x4 slice. The times are simulated.
32 devices in a mesh: group: 2 (over y), section: 4 (over z), ctx: 2 (over core), head: 2 (over x).
Axes of the slice: x: 2, y: 2, z: 4, core: 2. Of those that a mesh axis runs over, the one named last changes fastest.
Arguments:
- queries: bfloat16 [2048, 48, 128], P(('group', 'section'), 'head'), parts along dimension 0, may hold values from -6 to 6
- slice_kv: bfloat16 [2048, 2, 128], P(('group', 'section')), parts along dimension 0, may hold values from -6 to 6
- cache_keys: bfloat16 [8, 16, 128, 128], P(('group', 'section'), 'ctx'), parts along dimension 0
- cache_values: bfloat16 [8, 16, 128, 128], P(('group', 'section'), 'ctx'), parts along dimension 0, may hold values from -6 to 6
- block_table: int32 [8, 16], P('group'), parts along dimension 0, may hold values from 0 to 15, each once within a row
- slice_index: int32 [8], P('group'), parts along dimension 0, may hold values from 0 to 3, as said below
- out_weight: bfloat16 [48, 128, 6144], P('head', 'section', 'ctx'), may hold values from -0.078125 to 0.078125
Outputs:
- mixed: bfloat16 [2048, 6144], P(('group', 'section'), ('ctx', 'head')), parts along dimension 0
There are 2 independent parts, one for each index of `group`. A program takes and returns all parts, laid end to end along the dimension named above; an argument that names none is the same for every part. Nothing has to cross between parts.
Inputs may be any that keep to these rules, and one draw needn't show every extreme that they name: `slice_index`: every value appears once; the sections s and s + 4 / 2 (for s < 2) hold slice indices that sum to 3.
All inputs are finite; a program needn't handle non-finite values.
Results may differ from a plain program's by a relative error of at most 0.018.
Values may be sent and summed in bfloat16 or wider, within the bound.
No kernel may reach another device: no remote copies, remote signals or barrier semaphores. Data moves between devices by JAX's collectives and lax.ppermute only.
A program may use at most 64 MiB of HBM per device.

v0:
```python
import functools
import math

import jax
import jax.numpy as jnp
from jax import lax
from jax.experimental import pallas as pl
from jax.experimental.pallas import tpu as pltpu
from jax.sharding import PartitionSpec as P


BPS = 4

negative_floor = -1e30
column_chunks = 2


def attend_kernel(ids_ref, table_ref, index_ref, q_ref, *refs, first, pieces, block_len):
    if first:
        own_ref, kl_ref, vl_ref, kr_ref, vr_ref = refs[:5]
        out_refs = refs[5:-4]
        k_s, vt_s, m_s, acc_s = refs[-4:]
    else:
        k_s, vt_s = refs[:2]
        out_refs = refs[2:-2]
        m_s, acc_s = refs[-2:]
    heads, tokens, head_dim = q_ref.shape
    pool = table_ref.shape[1]
    section = ids_ref[0]
    ctx = ids_ref[1]
    slice_len = k_s.shape[0] - pool * block_len
    steps = index_ref[section] + 1
    width = BPS * block_len
    factor = math.log2(math.e) / math.sqrt(head_dim)

    if first:
        local_pool = kl_ref.shape[0]
        k_s[:slice_len, :] = own_ref[0]
        vt_s[:head_dim, :slice_len] = own_ref[1].T
        vt_s[head_dim:, :] = jnp.ones((vt_s.shape[0] - head_dim, vt_s.shape[1]), vt_s.dtype)

        @pl.loop(0, steps * BPS)
        def _(j):
            place = lax.rem(table_ref[section, j] + pool - ctx * local_pool, pool)
            rows = pl.ds(pl.multiple_of(slice_len + j * block_len, block_len), block_len)

            @pl.when(place < local_pool)
            def _():
                k_s[rows, :] = kl_ref[place]
                vt_s[:head_dim, rows] = vl_ref[place].T

            @pl.when(place >= local_pool)
            def _():
                k_s[rows, :] = kr_ref[place - local_pool]
                vt_s[:head_dim, rows] = vr_ref[place - local_pool].T

    q = q_ref[...].reshape(heads * tokens, head_dim)

    def scores(keys):
        return lax.dot_general(
            keys, q, (((1,), (1,)), ((), ())), preferred_element_type=jnp.float32
        )

    shape = (slice_len, heads * tokens)
    token = lax.rem(lax.broadcasted_iota(jnp.int32, shape, 1), tokens) + ctx * tokens
    s = jnp.where(
        lax.broadcasted_iota(jnp.int32, shape, 0) <= token, scores(k_s[:slice_len, :]), negative_floor
    )
    m = jnp.max(s, axis=0, keepdims=True)
    p = jnp.exp2(s * factor - m * factor).astype(jnp.bfloat16)
    m_s[...] = jnp.broadcast_to(m, m_s.shape)
    acc_s[...] = jnp.dot(vt_s[:, :slice_len], p, preferred_element_type=jnp.float32)

    @pl.loop(0, steps)
    def _(j):
        rows = pl.ds(pl.multiple_of(slice_len + j * width, block_len), width)
        s = scores(k_s[rows, :])
        before = m_s[:1, :]
        m = jnp.maximum(before, jnp.max(s, axis=0, keepdims=True))
        p = jnp.exp2(s * factor - m * factor).astype(jnp.bfloat16)
        rescale = jnp.exp2((before - m) * factor)
        m_s[...] = jnp.broadcast_to(m, m_s.shape)
        acc_s[...] = acc_s[...] * rescale + jnp.dot(
            vt_s[:, rows], p, preferred_element_type=jnp.float32
        )

    acc_s[:head_dim, :] = acc_s[:head_dim, :] / acc_s[head_dim : head_dim + 1, :]
    if pieces == 1:
        out_refs[0][...] = acc_s[:head_dim, :].astype(jnp.bfloat16)
    else:
        piece = head_dim // pieces
        for k in range(pieces):
            rows = pl.ds(pl.multiple_of(lax.rem(section + k, pieces) * piece, piece), piece)
            for h in range(heads):
                out_refs[k][h * piece : (h + 1) * piece, :] = acc_s[
                    rows, h * tokens : (h + 1) * tokens
                ].astype(jnp.bfloat16)


def attend(ids, block_table, slice_index, q, arrays, block_len, first_head, heads, pieces, first):
    tokens, head_dim = q.shape[1:]
    whole = lambda a: pl.BlockSpec(a.shape, lambda g, *_: (0,) * a.ndim)
    pool = block_table.shape[1]
    if first:
        keys = arrays[0].shape[1] + pool * arrays[1].shape[1]
        packed = [
            jax.ShapeDtypeStruct((keys, head_dim), jnp.bfloat16),
            jax.ShapeDtypeStruct((head_dim + 16, keys), jnp.bfloat16),
        ]
    else:
        packed = []
    if pieces == 1:
        out_shape = [jax.ShapeDtypeStruct((head_dim, heads * tokens), jnp.bfloat16)]
    else:
        out_shape = [
            jax.ShapeDtypeStruct((heads * head_dim // pieces, tokens), jnp.bfloat16)
        ] * pieces
    block = first_head // heads
    outs = pl.pallas_call(
        functools.partial(attend_kernel, first=first, pieces=pieces, block_len=block_len),
        out_shape=out_shape + packed,
        grid_spec=pltpu.PrefetchScalarGridSpec(
            num_scalar_prefetch=3,
            grid=(1,),
            in_specs=[pl.BlockSpec((heads, tokens, head_dim), lambda g, *_: (block, 0, 0))]
            + [whole(a) for a in arrays],
            out_specs=[whole(a) for a in out_shape + packed],
            scratch_shapes=[
                pltpu.VMEM((8, heads * tokens), jnp.float32),
                pltpu.VMEM((head_dim + 16, heads * tokens), jnp.float32),
            ],
        ),
        compiler_params=pltpu.CompilerParams(dimension_semantics=("arbitrary",)),
        name="attend",
    )(ids, block_table, slice_index, q, *arrays)
    return list(outs[: len(out_shape)]), list(outs[len(out_shape) :])


def project_kernel(ids_ref, *refs, sections, parts):
    near = refs[: sections * parts]
    far = refs[sections * parts : 2 * sections * parts]
    w_refs = refs[2 * sections * parts : 2 * sections * parts + 6]
    out_refs = refs[2 * sections * parts + 6 : -1]
    a_s = refs[-1]
    rows, tokens = near[0].shape
    all_rows = rows * parts
    half = all_rows // 2
    group = ids_ref[3]

    @pl.when(pl.program_id(0) == 0)
    def _():
        for k in range(sections):
            at = slice(k * tokens, (k + 1) * tokens)
            for i in range(parts):
                a_s[at, i * rows : (i + 1) * rows] = near[k * parts + i][...].T
                place = all_rows + lax.rem(i + group, parts) * rows
                a_s[at, pl.ds(pl.multiple_of(place, rows), rows)] = far[k * parts + i][...].T

    a = a_s[...]
    for side in range(2):
        own, one, two = w_refs[3 * side : 3 * side + 3]
        out = jnp.dot(a[:, :all_rows], own[...], preferred_element_type=jnp.float32)
        out = out + jnp.dot(
            a[:, all_rows : all_rows + half], one[...], preferred_element_type=jnp.float32
        )
        out = out + jnp.dot(
            a[:, all_rows + half :], two[...], preferred_element_type=jnp.float32
        )
        for k in range(sections):
            out_refs[k][side] = out[k * tokens : (k + 1) * tokens].astype(jnp.bfloat16)


def project(ids, near, far, weights, chunk, columns):
    sections, parts = len(near), len(near[0])
    rows, tokens = near[0][0].shape
    tile = math.gcd(columns, 256)
    per_chunk = columns // tile
    per_half = weights[3].shape[1] // tile
    base = chunk * per_chunk
    flat = [a for both in (near, far) for k in both for a in k]
    here = lambda n, ids: (0, base + n)
    start = lambda n, ids: (0, n)
    return pl.pallas_call(
        functools.partial(project_kernel, sections=sections, parts=parts),
        out_shape=[jax.ShapeDtypeStruct((2, tokens, columns), jnp.bfloat16)] * sections,
        grid_spec=pltpu.PrefetchScalarGridSpec(
            num_scalar_prefetch=1,
            grid=(per_chunk,),
            in_specs=[pl.BlockSpec(a.shape, lambda n, ids: (0, 0)) for a in flat]
            + [
                pl.BlockSpec(
                    (weights[0].shape[0], tile), lambda n, ids: (0, ids[2] * per_half + base + n)
                )
            ]
            + [
                pl.BlockSpec((w.shape[0], tile), here if w is weights[3] else start)
                for w in weights[1:]
            ],
            out_specs=[pl.BlockSpec((2, tokens, tile), lambda n, ids: (0, 0, n))] * sections,
            scratch_shapes=[pltpu.VMEM((sections * tokens, 2 * parts * rows), jnp.bfloat16)],
        ),
        compiler_params=pltpu.CompilerParams(dimension_semantics=("arbitrary",)),
        name="project",
    )(ids, *flat, *weights)


def combine_kernel(ids_ref, own, up, down, twin, cross_up, cross_down, *rest):
    out = rest[-1]
    tokens = own.shape[0]
    f32 = lambda ref: ref[...].astype(jnp.float32)
    ctx = ids_ref[1]
    here = pl.ds(pl.multiple_of(ctx * tokens, tokens), tokens)
    there = pl.ds(pl.multiple_of((1 - ctx) * tokens, tokens), tokens)
    out[here, :] = (f32(own) + f32(up) + f32(down)).astype(jnp.bfloat16)
    out[there, :] = (f32(twin) + f32(cross_up) + f32(cross_down)).astype(jnp.bfloat16)


def combine(ids, own, up, down, twin, cross_up, cross_down, before, chunk, chunks):
    tokens, columns = twin.shape
    flat = [own, up, down, twin, cross_up, cross_down]
    specs = [
        pl.BlockSpec((None, tokens, columns), lambda g, ids: (0, 0, 0))
        if a.ndim == 3
        else pl.BlockSpec((tokens, columns), lambda g, ids: (0, 0))
        for a in flat
    ]
    args = flat
    aliases = {}
    if before is not None:
        specs = specs + [pl.BlockSpec(memory_space=pl.ANY)]
        args = flat + [before]
        aliases = {7: 0}
    return pl.pallas_call(
        combine_kernel,
        out_shape=jax.ShapeDtypeStruct((2 * tokens, columns * chunks), jnp.bfloat16),
        grid_spec=pltpu.PrefetchScalarGridSpec(
            num_scalar_prefetch=1,
            grid=(1,),
            in_specs=specs,
            out_specs=pl.BlockSpec((2 * tokens, columns), lambda g, ids: (0, chunk)),
        ),
        input_output_aliases=aliases,
        name="combine",
    )(ids, *args)


swap = [(0, 1), (1, 0)]


def add_rounded(*values):
    total = values[0].astype(jnp.float32)
    for value in values[1:]:
        total = total + value.astype(jnp.float32)
    return total.astype(jnp.bfloat16)


def line_reduce(partial):
    count = len(partial)
    up = down = None
    for t in range(1, count):
        send_up = partial[t] if up is None else add_rounded(partial[t], up)
        send_down = partial[count - t] if down is None else add_rounded(partial[count - t], down)
        ups = [(z, z + 1) for z in range(t)]
        downs = [(count - 1 - z, count - 2 - z) for z in range(t)]
        if t + 1 < count:
            up = lax.ppermute(send_up, "section", ups)
            down = lax.ppermute(send_down, "section", downs)
    crossed = lambda pairs: [(2 * i + c, 2 * j + 1 - c) for i, j in pairs for c in range(2)]
    twin = lax.ppermute(partial[0][1], "ctx", swap)
    return (
        partial[0],
        lax.ppermute(send_up[0], "section", ups),
        lax.ppermute(send_down[0], "section", downs),
        twin,
        lax.ppermute(send_up[1], ("section", "ctx"), crossed(ups)),
        lax.ppermute(send_down[1], ("section", "ctx"), crossed(downs)),
    )


def on_device(queries, slice_kv, cache_keys, cache_values, block_table, slice_index, out_weight):
    slice_len, heads, head_dim = queries.shape
    section_count = lax.axis_size("section")
    ctx_count = lax.axis_size("ctx")
    head_count = lax.axis_size("head")
    group_count = lax.axis_size("group")
    section = lax.axis_index("section")
    ctx = lax.axis_index("ctx")
    head = lax.axis_index("head")
    group = lax.axis_index("group")
    ids = jnp.stack([section, ctx, head, group]).astype(jnp.int32)
    tokens = slice_len // ctx_count
    block_len = cache_keys.shape[2]
    piece = head_dim // section_count
    width = out_weight.shape[2]
    w_local = out_weight.reshape(heads * piece, width)
    out_columns = width // head_count
    pairs = (
        head_count == 2
        and group_count == 2
        and piece % 16 == 0
        and heads % 2 == 0
        and out_columns % (128 * column_chunks) == 0
    )

    keys_far = lax.ppermute(cache_keys[0], "ctx", swap)
    values_far = lax.ppermute(cache_values[0], "ctx", swap)
    own_queries = lax.dynamic_slice_in_dim(queries, ctx * tokens, tokens, 0)
    q = jnp.swapaxes(own_queries, 0, 1)
    own = jnp.swapaxes(slice_kv, 0, 1)
    blocks = [own, cache_keys[0], cache_values[0], keys_far, values_far]
    if pairs:
        parts = 2
        columns = out_columns // column_chunks
        half_rows = w_local.shape[0] // 2
        w_one, w_two, twin_kept, twin_one, twin_two = ([None] * column_chunks for _ in range(5))
        for chunk in range(column_chunks):
            sent = lax.dynamic_slice(
                w_local,
                (group * half_rows, (1 - head) * out_columns + chunk * columns),
                (half_rows, columns),
            )
            w_one[chunk] = lax.ppermute(sent, "head", swap)
        w_kept = lax.dynamic_slice_in_dim(w_local, head * out_columns, out_columns, 1)
        twin_kept = lax.ppermute(w_kept, "ctx", swap)
        near = [[None] * parts for _ in range(section_count)]
        far = [[None] * parts for _ in range(section_count)]
        arrays = blocks
        for i in range(parts):
            made, packed = attend(
                ids, block_table, slice_index, q, arrays, block_len, i * (heads // parts),
                heads // parts, section_count, i == 0,
            )
            if i == 0:
                arrays = packed
            near[0][i] = made[0]
            for k in shift_order(section_count):
                near[k][i] = lax.ppermute(
                    made[k],
                    "section",
                    [(z, (z + k) % section_count) for z in range(section_count)],
                )
            for k in range(section_count):
                far[k][i] = lax.ppermute(near[k][i], "head", swap)
        for chunk in range(column_chunks):
            w_two[chunk] = lax.ppermute(w_one[chunk], "group", swap)
            twin_one[chunk] = lax.ppermute(w_one[chunk], "ctx", swap)
            twin_two[chunk] = lax.ppermute(w_two[chunk], "ctx", swap)
        out = None
        for chunk in range(column_chunks):
            weights = [w_local, w_one[chunk], w_two[chunk], twin_kept, twin_one[chunk], twin_two[chunk]]
            partial = project(ids, near, far, weights, chunk, columns)
            out = combine(ids, *line_reduce(partial), out, chunk, column_chunks)
        return out

    attended = attend(ids, block_table, slice_index, q, blocks, block_len, 0, heads, 1, True)[0][0]
    by_section = attended.reshape(section_count, piece, heads, tokens).transpose(0, 3, 2, 1)
    by_section = by_section.reshape(section_count, tokens, heads * piece)
    by_section = lax.all_gather(by_section, "ctx", axis=1, tiled=True)
    rows = lax.all_to_all(by_section, "section", 0, 0)
    rows = rows.reshape(section_count * slice_len, heads * piece)
    rows = lax.all_gather(rows, "head", axis=1, tiled=True)
    weights = lax.all_to_all(w_local, "head", split_axis=1, concat_axis=0, tiled=True)
    partial = jnp.dot(rows, weights, preferred_element_type=jnp.float32).astype(jnp.bfloat16)
    return lax.psum_scatter(partial, "section", scatter_dimension=0, tiled=True)


def shift_order(sections):
    return sorted(range(1, sections), key=lambda k: min(k, sections - k))


def solution(mesh):
    placed = (
        P(("group", "section"), "head", None),
        P(("group", "section"), None, None),
        P(("group", "section"), "ctx", None, None),
        P(("group", "section"), "ctx", None, None),
        P("group", None),
        P("group"),
        P("head", "section", "ctx"),
    )

    return jax.shard_map(
        on_device,
        mesh=mesh,
        in_specs=placed,
        out_specs=P(("group", "section"), ("ctx", "head")),
        check_vma=False,
    )
```

profile of v0, /device:TPU:0, one launch (start us, length us, event | category | flops | bytes accessed | tf_op | source)
XLA Modules:
  0.0 165.0 jit_solution(4058695445388814136)
XLA Ops:
  0.0 3.4 %constant_dynamic-slice_fusion = bf16[768,1536]{1,0:T(8,128)(2,1)} fusion(bf16[768,3072]{1,0:T(8,128)(2,1)} %bitcast.33, s32[]{:T(128)S(6)} %select_n.19), kind=kLoop, calls=%fused_computation.25 | loop fusion | bytes 4718596 | tf_op jit(solution)/shard_map/dynamic_slice | solution.py:323
  6.0 2.5 %collective-permute-start.30 = (bf16[384,768]{1,0:T(8,128)(2,1)S(1)}, bf16[384,768]{1,0:T(8,128)(2,1)S(1)}, u32[]{:S(2)}, u32[]{:S(2)}) collective-permute-start(bf16[384,768]{1,0:T(8,128)(2,1)S(1)} %get-tuple-element.41), channel_id=1, source_target_pairs={{0,1},{1,0},{2,3},{3,2},{4,5},{5,4},{6,7},{7,6},{8,9},{9,8},{10,11... | collective-permute-start | bytes 1769480 | tf_op jit(solution)/shard_map/ppermute | solution.py:322
  12.3 9.1 %attend.2 = (bf16[384,128]{1,0:T(8,128)(2,1)}, bf16[384,128]{1,0:T(8,128)(2,1)}, bf16[384,128]{1,0:T(8,128)(2,1)}, bf16[384,128]{1,0:T(8,128)(2,1)}, bf16[2304,1...) custom-call(s32[4]{0:T(128)} %pad_add_fusion.ids_ref, s32[4,16]{1,0:T(4,128)} %table_ref.3, s32[4]{0:T(128)} %index_ref.3, ...), custom_call_target="tpu_custom_call" | custom-call | tf_op jit(solution)/shard_map/attend/pallas_call | solution.py:119
  21.4 3.7 %collective-permute-start.2 = (bf16[384,128]{1,0:T(8,128)(2,1)}, bf16[384,128]{1,0:T(8,128)(2,1)S(1)}, u32[]{:S(2)}, u32[]{:S(2)}) collective-permute-start(bf16[384,128]{1,0:T(8,128)(2,1)} %get-tuple-element.27), channel_id=1, source_target_pairs={{0,4},{4,8},{8,12},{12,0},{1,5},{5,9},{9,13},{13,1},{2,6},{6,10},{... | collective-permute-start | bytes 294920 | tf_op jit(solution)/shard_map/ppermute | solution.py:337
  25.1 7.7 %attend.3 = (bf16[384,128]{1,0:T(8,128)(2,1)}, bf16[384,128]{1,0:T(8,128)(2,1)}, bf16[384,128]{1,0:T(8,128)(2,1)}, bf16[384,128]{1,0:T(8,128)(2,1)}) custom-call(s32[4]{0:T(128)} %pad_add_fusion.ids_ref, s32[4,16]{1,0:T(4,128)} %table_ref.3, s32[4]{0:T(128)} %index_ref.3, bf16[24,128,128]{2,1,0:T(8,128)(2,1)} %bitcast.38, ...), custom_call_target="tpu_custom_call" | custom-call | tf_op jit(solution)/shard_map/attend/pallas_call | solution.py:119
  34.2 4.1 %collective-permute-start.4 = (bf16[384,128]{1,0:T(8,128)(2,1)}, bf16[384,128]{1,0:T(8,128)(2,1)S(1)}, u32[]{:S(2)}, u32[]{:S(2)}) collective-permute-start(bf16[384,128]{1,0:T(8,128)(2,1)} %get-tuple-element.29), channel_id=1, source_target_pairs={{0,8},{4,12},{8,0},{12,4},{1,9},{5,13},{9,1},{13,5},{2,10},{6,14},... | collective-permute-start | bytes 294920 | tf_op jit(solution)/shard_map/ppermute | solution.py:337
  40.5 5.4 %collective-permute-done.4.refs_4_ = bf16[384,128]{1,0:T(8,128)(2,1)S(1)} collective-permute-done((bf16[384,128]{1,0:T(8,128)(2,1)}, bf16[384,128]{1,0:T(8,128)(2,1)S(1)}, u32[]{:S(2)}, u32[]{:S(2)}) %collective-permute-start.4) | collective-permute-done | bytes 98336 | tf_op jit(solution)/shard_map/ppermute | solution.py:337
  45.9 2.7 %collective-permute-start.6 = (bf16[384,128]{1,0:T(8,128)(2,1)}, bf16[384,128]{1,0:T(8,128)(2,1)S(1)}, u32[]{:S(2)}, u32[]{:S(2)}) collective-permute-start(bf16[384,128]{1,0:T(8,128)(2,1)} %get-tuple-element.31), channel_id=1, source_target_pairs={{0,12},{4,0},{8,4},{12,8},{1,13},{5,1},{9,5},{13,9},{2,14},{6,2},{... | collective-permute-start | bytes 294920 | tf_op jit(solution)/shard_map/ppermute | solution.py:337
  69.3 2.4 %collective-permute-done.14.refs_14_ = bf16[384,128]{1,0:T(8,128)(2,1)S(1)} collective-permute-done((bf16[384,128]{1,0:T(8,128)(2,1)S(1)}, bf16[384,128]{1,0:T(8,128)(2,1)S(1)}, u32[]{:S(2)}, u32[]{:S(2)}) %collective-permute-start.14) | collective-permute-done | bytes 98336 | tf_op jit(solution)/shard_map/ppermute | solution.py:343
  73.2 3.1 %collective-permute-done.15.refs_15_ = bf16[384,128]{1,0:T(8,128)(2,1)S(1)} collective-permute-done((bf16[384,128]{1,0:T(8,128)(2,1)S(1)}, bf16[384,128]{1,0:T(8,128)(2,1)S(1)}, u32[]{:S(2)}, u32[]{:S(2)}) %collective-permute-start.15) | collective-permute-done | bytes 98336 | tf_op jit(solution)/shard_map/ppermute | solution.py:343
  78.5 7.7 %project.3 = (bf16[2,128,768]{2,1,0:T(8,128)(2,1)}, bf16[2,128,768]{2,1,0:T(8,128)(2,1)}, bf16[2,128,768]{2,1,0:T(8,128)(2,1)}, bf16[2,128,768]{2,1,0:T(8,128)(2,1)}) custom-call(s32[4]{0:T(128)} %pad_add_fusion.ids_ref, bf16[384,128]{1,0:T(8,128)(2,1)} %get-tuple-element.23.refs_0_, bf16[384,128]{1,0:T(8,128)(2,1)} %get-tuple-element.26.refs_1_, ...), custom_call_target="tpu_custom_call" | custom-call | tf_op jit(solution)/shard_map/project/pallas_call | solution.py:183
  87.7 2.5 %collective-permute-start.34 = (bf16[2,128,768]{2,1,0:T(8,128)(2,1)}, bf16[2,128,768]{2,1,0:T(8,128)(2,1)}, u32[]{:S(2)}, u32[]{:S(2)}) collective-permute-start(bf16[2,128,768]{2,1,0:T(8,128)(2,1)} %get-tuple-element.40), channel_id=1, source_target_pairs={{0,4},{1,5},{2,6},{3,7},{16,20},{17,21},{18,22},{19,23}} | collective-permute-start | bytes 1179656 | tf_op jit(solution)/shard_map/ppermute | solution.py:266
  90.2 7.7 %project.2 = (bf16[2,128,768]{2,1,0:T(8,128)(2,1)}, bf16[2,128,768]{2,1,0:T(8,128)(2,1)}, bf16[2,128,768]{2,1,0:T(8,128)(2,1)}, bf16[2,128,768]{2,1,0:T(8,128)(2,1)}) custom-call(s32[4]{0:T(128)} %pad_add_fusion.ids_ref, bf16[384,128]{1,0:T(8,128)(2,1)} %get-tuple-element.23.refs_0_, bf16[384,128]{1,0:T(8,128)(2,1)} %get-tuple-element.26.refs_1_, ...), custom_call_target="tpu_custom_call" | custom-call | tf_op jit(solution)/shard_map/project/pallas_call | solution.py:183
  101.5 2.7 %collective-permute-start.35 = (bf16[2,128,768]{2,1,0:T(8,128)(2,1)S(1)}, bf16[2,128,768]{2,1,0:T(8,128)(2,1)S(1)}, u32[]{:S(2)}, u32[]{:S(2)}) collective-permute-start(bf16[2,128,768]{2,1,0:T(8,128)(2,1)S(1)} %get-tuple-element.48), channel_id=1, source_target_pairs={{0,4},{4,8},{1,5},{5,9},{2,6},{6,10},{3,7},{7,11},{16,20},{20,24},... | collective-permute-start | bytes 1179656 | tf_op jit(solution)/shard_map/ppermute | solution.py:266
  104.9 4.9 %collective-permute-done.21 = bf16[2,128,768]{2,1,0:T(8,128)(2,1)S(1)} collective-permute-done((bf16[2,128,768]{2,1,0:T(8,128)(2,1)}, bf16[2,128,768]{2,1,0:T(8,128)(2,1)S(1)}, u32[]{:S(2)}, u32[]{:S(2)}) %collective-permute-start.21) | collective-permute-done | bytes 393248 | tf_op jit(solution)/shard_map/ppermute | solution.py:266
  110.0 4.4 %collective-permute-start.22 = (bf16[2,128,768]{2,1,0:T(8,128)(2,1)S(1)}, bf16[2,128,768]{2,1,0:T(8,128)(2,1)S(1)}, u32[]{:S(2)}, u32[]{:S(2)}) collective-permute-start(bf16[2,128,768]{2,1,0:T(8,128)(2,1)S(1)} %get-tuple-element.54), channel_id=1, source_target_pairs={{0,4},{4,8},{1,5},{5,9},{2,6},{6,10},{3,7},{7,11},{16,20},{20,24},... | collective-permute-start | bytes 1179656 | tf_op jit(solution)/shard_map/ppermute | solution.py:266
  118.3 4.5 %collective-permute-start.36 = (bf16[128,768]{1,0:T(8,128)(2,1)S(1)}, bf16[128,768]{1,0:T(8,128)(2,1)S(1)}, u32[]{:S(2)}, u32[]{:S(2)}) collective-permute-start(bf16[128,768]{1,0:T(8,128)(2,1)S(1)} %get-tuple-element.46), channel_id=1, source_target_pairs={{0,4},{4,8},{8,12},{1,5},{5,9},{9,13},{2,6},{6,10},{10,14},{3,7},{... | collective-permute-start | bytes 589832 | tf_op jit(solution)/shard_map/ppermute | solution.py:272
  126.6 11.1 %collective-permute-start.41 = (bf16[128,768]{1,0:T(8,128)(2,1)S(1)}, bf16[128,768]{1,0:T(8,128)(2,1)}, u32[]{:S(2)}, u32[]{:S(2)}) collective-permute-start(bf16[128,768]{1,0:T(8,128)(2,1)S(1)} %get-tuple-element.45), channel_id=1, source_target_pairs={{0,6},{2,4},{4,10},{6,8},{8,14},{10,12},{1,7},{3,5},{5,11},{7,9},{... | collective-permute-start | bytes 589832 | tf_op jit(solution)/shard_map/ppermute | solution.py:275
  140.8 2.4 %collective-permute-start.27 = (bf16[128,768]{1,0:T(8,128)(2,1)}, bf16[128,768]{1,0:T(8,128)(2,1)S(1)}, u32[]{:S(2)}, u32[]{:S(2)}) collective-permute-start(bf16[128,768]{1,0:T(8,128)(2,1)} %slice_bitcast_fusion.9), channel_id=1, source_target_pairs={{0,2},{2,0},{1,3},{3,1},{4,6},{6,4},{5,7},{7,5},{8,10},{10,8},{9,1... | collective-permute-start | bytes 589832 | tf_op jit(solution)/shard_map/ppermute | solution.py:269
  143.3 4.2 %collective-permute-start.23 = (bf16[128,768]{1,0:T(8,128)(2,1)}, bf16[128,768]{1,0:T(8,128)(2,1)S(1)}, u32[]{:S(2)}, u32[]{:S(2)}) collective-permute-start(bf16[128,768]{1,0:T(8,128)(2,1)} %get-tuple-element.52), channel_id=1, source_target_pairs={{0,4},{4,8},{8,12},{1,5},{5,9},{9,13},{2,6},{6,10},{10,14},{3,7},{... | collective-permute-start | bytes 589832 | tf_op jit(solution)/shard_map/ppermute | solution.py:272
  148.8 4.1 %collective-permute-start.28 = (bf16[128,768]{1,0:T(8,128)(2,1)}, bf16[128,768]{1,0:T(8,128)(2,1)S(1)}, u32[]{:S(2)}, u32[]{:S(2)}) collective-permute-start(bf16[128,768]{1,0:T(8,128)(2,1)} %get-tuple-element.51), channel_id=1, source_target_pairs={{0,6},{2,4},{4,10},{6,8},{8,14},{10,12},{1,7},{3,5},{5,11},{7,9},{... | collective-permute-start | bytes 589832 | tf_op jit(solution)/shard_map/ppermute | solution.py:275
  154.2 2.9 %combine.2.rest_0_ = bf16[256,1536]{1,0:T(8,128)(2,1)} custom-call(s32[4]{0:T(128)} %pad_add_fusion.ids_ref, bf16[2,128,768]{2,1,0:T(8,128)(2,1)} %get-tuple-element.37.own, bf16[128,768]{1,0:T(8,128)(2,1)} %copy-done.29, bf16[128,768]{1,0:T(8,128)(2,1)} %copy-done.30, bf16[128,768]{1,0:T(8,128)(2,1)} %copy-done.28, ...), custom_call_target="tpu_custom_call" | custom-call | tf_op jit(solution)/shard_map/combine/pallas_call | solution.py:233
  158.4 3.1 %collective-permute-done.29.cross_down = bf16[128,768]{1,0:T(8,128)(2,1)S(1)} collective-permute-done((bf16[128,768]{1,0:T(8,128)(2,1)}, bf16[128,768]{1,0:T(8,128)(2,1)S(1)}, u32[]{:S(2)}, u32[]{:S(2)}) %collective-permute-start.29) | collective-permute-done | bytes 196640 | tf_op jit(solution)/shard_map/ppermute | solution.py:276
  162.1 2.9 %combine.3 = bf16[256,1536]{1,0:T(8,128)(2,1)} custom-call(s32[4]{0:T(128)} %pad_add_fusion.ids_ref, bf16[2,128,768]{2,1,0:T(8,128)(2,1)} %get-tuple-element.33.own, bf16[128,768]{1,0:T(8,128)(2,1)} %copy-done.32, bf16[128,768]{1,0:T(8,128)(2,1)} %copy-done.34, bf16[128,768]{1,0:T(8,128)(2,1)} %copy-done.31, ...), custom_call_target="tpu_custom_call", output_to_operand_aliasing={{}: (7, {})} | custom-call | tf_op jit(solution)/shard_map/combine/pallas_call | solution.py:233
  (160 shorter events, 55.2 us)
Async XLA Ops:
  3.4 75.1 %collective-permute-start.18 = (bf16[768,1536]{1,0:T(8,128)(2,1)}, bf16[768,1536]{1,0:T(8,128)(2,1)}, u32[]{:S(2)}, u32[]{:S(2)}) collective-permute-start(bf16[768,1536]{1,0:T(8,128)(2,1)} %constant_dynamic-slice_fusion), channel_id=1, source_target_pairs={{0,2},{2,0},{1,3},{3,1},{4,6},{6,4},{5,7},{7,5},{8,10},{10,8},{9,1... | collective-permute-start | bytes 7077896 | tf_op jit(solution)/shard_map/ppermute | solution.py:324
  6.0 28.1 %collective-permute-start.30 = (bf16[384,768]{1,0:T(8,128)(2,1)S(1)}, bf16[384,768]{1,0:T(8,128)(2,1)S(1)}, u32[]{:S(2)}, u32[]{:S(2)}) collective-permute-start(bf16[384,768]{1,0:T(8,128)(2,1)S(1)} %get-tuple-element.41), channel_id=1, source_target_pairs={{0,1},{1,0},{2,3},{3,2},{4,5},{5,4},{6,7},{7,6},{8,9},{9,8},{10,11... | collective-permute-start | bytes 1769480 | tf_op jit(solution)/shard_map/ppermute | solution.py:322
  8.5 40.1 %collective-permute-start.16 = (bf16[384,768]{1,0:T(8,128)(2,1)}, bf16[384,768]{1,0:T(8,128)(2,1)S(1)}, u32[]{:S(2)}, u32[]{:S(2)}) collective-permute-start(bf16[384,768]{1,0:T(8,128)(2,1)} %get-tuple-element.42), channel_id=1, source_target_pairs={{0,1},{1,0},{2,3},{3,2},{4,5},{5,4},{6,7},{7,6},{8,9},{9,8},{10,11... | collective-permute-start | bytes 1769480 | tf_op jit(solution)/shard_map/ppermute | solution.py:322
  21.4 12.7 %collective-permute-start.2 = (bf16[384,128]{1,0:T(8,128)(2,1)}, bf16[384,128]{1,0:T(8,128)(2,1)S(1)}, u32[]{:S(2)}, u32[]{:S(2)}) collective-permute-start(bf16[384,128]{1,0:T(8,128)(2,1)} %get-tuple-element.27), channel_id=1, source_target_pairs={{0,4},{4,8},{8,12},{12,0},{1,5},{5,9},{9,13},{13,1},{2,6},{6,10},{... | collective-permute-start | bytes 294920 | tf_op jit(solution)/shard_map/ppermute | solution.py:337
  34.1 35.1 %collective-permute-start.31 = (bf16[384,768]{1,0:T(8,128)(2,1)S(1)}, bf16[384,768]{1,0:T(8,128)(2,1)S(1)}, u32[]{:S(2)}, u32[]{:S(2)}) collective-permute-start(bf16[384,768]{1,0:T(8,128)(2,1)S(1)} %collective-permute-done.30.refs_17_), channel_id=1, source_target_pairs={{0,16},{16,0},{1,17},{17,1},{2,18},{18,2},{3,19},{19,3},{4,20},{20... | collective-permute-start | bytes 1769480 | tf_op jit(solution)/shard_map/ppermute | solution.py:345
  34.2 11.7 %collective-permute-start.4 = (bf16[384,128]{1,0:T(8,128)(2,1)}, bf16[384,128]{1,0:T(8,128)(2,1)S(1)}, u32[]{:S(2)}, u32[]{:S(2)}) collective-permute-start(bf16[384,128]{1,0:T(8,128)(2,1)} %get-tuple-element.29), channel_id=1, source_target_pairs={{0,8},{4,12},{8,0},{12,4},{1,9},{5,13},{9,1},{13,5},{2,10},{6,14},... | collective-permute-start | bytes 294920 | tf_op jit(solution)/shard_map/ppermute | solution.py:337
  48.6 27.7 %collective-permute-start.17 = (bf16[384,768]{1,0:T(8,128)(2,1)S(1)}, bf16[384,768]{1,0:T(8,128)(2,1)}, u32[]{:S(2)}, u32[]{:S(2)}) collective-permute-start(bf16[384,768]{1,0:T(8,128)(2,1)S(1)} %collective-permute-done.16.refs_17_), channel_id=1, source_target_pairs={{0,16},{16,0},{1,17},{17,1},{2,18},{18,2},{3,19},{19,3},{4,20},{20... | collective-permute-start | bytes 1769480 | tf_op jit(solution)/shard_map/ppermute | solution.py:345
  76.3 13.9 %collective-permute-start.19 = (bf16[384,768]{1,0:T(8,128)(2,1)S(1)}, bf16[384,768]{1,0:T(8,128)(2,1)}, u32[]{:S(2)}, u32[]{:S(2)}) collective-permute-start(bf16[384,768]{1,0:T(8,128)(2,1)S(1)} %collective-permute-done.16.refs_17_), channel_id=1, source_target_pairs={{0,2},{2,0},{1,3},{3,1},{4,6},{6,4},{5,7},{7,5},{8,10},{10,8},{9,1... | collective-permute-start | bytes 1769480 | tf_op jit(solution)/shard_map/ppermute | solution.py:346
  76.3 13.9 %collective-permute-start.20 = (bf16[384,768]{1,0:T(8,128)(2,1)}, bf16[384,768]{1,0:T(8,128)(2,1)}, u32[]{:S(2)}, u32[]{:S(2)}) collective-permute-start(bf16[384,768]{1,0:T(8,128)(2,1)} %collective-permute-done.17.refs_18_), channel_id=1, source_target_pairs={{0,2},{2,0},{1,3},{3,1},{4,6},{6,4},{5,7},{7,5},{8,10},{10,8},{9,1... | collective-permute-start | bytes 1769480 | tf_op jit(solution)/shard_map/ppermute | solution.py:347
  86.3 13.9 %collective-permute-start.37 = (bf16[2,128,768]{2,1,0:T(8,128)(2,1)}, bf16[2,128,768]{2,1,0:T(8,128)(2,1)}, u32[]{:S(2)}, u32[]{:S(2)}) collective-permute-start(bf16[2,128,768]{2,1,0:T(8,128)(2,1)} %get-tuple-element.38), channel_id=1, source_target_pairs={{12,8},{13,9},{14,10},{15,11},{28,24},{29,25},{30,26},{31,27}} | collective-permute-start | bytes 1179656 | tf_op jit(solution)/shard_map/ppermute | solution.py:267
  87.7 12.4 %collective-permute-start.34 = (bf16[2,128,768]{2,1,0:T(8,128)(2,1)}, bf16[2,128,768]{2,1,0:T(8,128)(2,1)}, u32[]{:S(2)}, u32[]{:S(2)}) collective-permute-start(bf16[2,128,768]{2,1,0:T(8,128)(2,1)} %get-tuple-element.40), channel_id=1, source_target_pairs={{0,4},{1,5},{2,6},{3,7},{16,20},{17,21},{18,22},{19,23}} | collective-permute-start | bytes 1179656 | tf_op jit(solution)/shard_map/ppermute | solution.py:266
  98.7 11.1 %collective-permute-start.21 = (bf16[2,128,768]{2,1,0:T(8,128)(2,1)}, bf16[2,128,768]{2,1,0:T(8,128)(2,1)S(1)}, u32[]{:S(2)}, u32[]{:S(2)}) collective-permute-start(bf16[2,128,768]{2,1,0:T(8,128)(2,1)} %get-tuple-element.36), channel_id=1, source_target_pairs={{0,4},{1,5},{2,6},{3,7},{16,20},{17,21},{18,22},{19,23}} | collective-permute-start | bytes 1179656 | tf_op jit(solution)/shard_map/ppermute | solution.py:266
  100.1 40.7 %collective-permute-start.40 = (bf16[128,768]{1,0:T(8,128)(2,1)S(1)}, bf16[128,768]{1,0:T(8,128)(2,1)S(1)}, u32[]{:S(2)}, u32[]{:S(2)}) collective-permute-start(bf16[128,768]{1,0:T(8,128)(2,1)S(1)} %slice_bitcast_fusion.8), channel_id=1, source_target_pairs={{0,2},{2,0},{1,3},{3,1},{4,6},{6,4},{5,7},{7,5},{8,10},{10,8},{9,1... | collective-permute-start | bytes 589832 | tf_op jit(solution)/shard_map/ppermute | solution.py:269
  101.5 16.7 %collective-permute-start.35 = (bf16[2,128,768]{2,1,0:T(8,128)(2,1)S(1)}, bf16[2,128,768]{2,1,0:T(8,128)(2,1)S(1)}, u32[]{:S(2)}, u32[]{:S(2)}) collective-permute-start(bf16[2,128,768]{2,1,0:T(8,128)(2,1)S(1)} %get-tuple-element.48), channel_id=1, source_target_pairs={{0,4},{4,8},{1,5},{5,9},{2,6},{6,10},{3,7},{7,11},{16,20},{20,24},... | collective-permute-start | bytes 1179656 | tf_op jit(solution)/shard_map/ppermute | solution.py:266
  110.0 16.6 %collective-permute-start.22 = (bf16[2,128,768]{2,1,0:T(8,128)(2,1)S(1)}, bf16[2,128,768]{2,1,0:T(8,128)(2,1)S(1)}, u32[]{:S(2)}, u32[]{:S(2)}) collective-permute-start(bf16[2,128,768]{2,1,0:T(8,128)(2,1)S(1)} %get-tuple-element.54), channel_id=1, source_target_pairs={{0,4},{4,8},{1,5},{5,9},{2,6},{6,10},{3,7},{7,11},{16,20},{20,24},... | collective-permute-start | bytes 1179656 | tf_op jit(solution)/shard_map/ppermute | solution.py:266
  114.4 24.2 %collective-permute-start.25 = (bf16[2,128,768]{2,1,0:T(8,128)(2,1)S(1)}, bf16[2,128,768]{2,1,0:T(8,128)(2,1)S(1)}, u32[]{:S(2)}, u32[]{:S(2)}) collective-permute-start(bf16[2,128,768]{2,1,0:T(8,128)(2,1)S(1)} %get-tuple-element.53), channel_id=1, source_target_pairs={{12,8},{8,4},{13,9},{9,5},{14,10},{10,6},{15,11},{11,7},{28,24},{2... | collective-permute-start | bytes 1179656 | tf_op jit(solution)/shard_map/ppermute | solution.py:267
  118.3 25.0 %collective-permute-start.36 = (bf16[128,768]{1,0:T(8,128)(2,1)S(1)}, bf16[128,768]{1,0:T(8,128)(2,1)S(1)}, u32[]{:S(2)}, u32[]{:S(2)}) collective-permute-start(bf16[128,768]{1,0:T(8,128)(2,1)S(1)} %get-tuple-element.46), channel_id=1, source_target_pairs={{0,4},{4,8},{8,12},{1,5},{5,9},{9,13},{2,6},{6,10},{10,14},{3,7},{... | collective-permute-start | bytes 589832 | tf_op jit(solution)/shard_map/ppermute | solution.py:272
  123.0 24.5 %collective-permute-start.39 = (bf16[128,768]{1,0:T(8,128)(2,1)S(1)}, bf16[128,768]{1,0:T(8,128)(2,1)S(1)}, u32[]{:S(2)}, u32[]{:S(2)}) collective-permute-start(bf16[128,768]{1,0:T(8,128)(2,1)S(1)} %get-tuple-element.44), channel_id=1, source_target_pairs={{12,8},{8,4},{4,0},{13,9},{9,5},{5,1},{14,10},{10,6},{6,2},{15,11}... | collective-permute-start | bytes 589832 | tf_op jit(solution)/shard_map/ppermute | solution.py:273
  126.6 22.2 %collective-permute-start.41 = (bf16[128,768]{1,0:T(8,128)(2,1)S(1)}, bf16[128,768]{1,0:T(8,128)(2,1)}, u32[]{:S(2)}, u32[]{:S(2)}) collective-permute-start(bf16[128,768]{1,0:T(8,128)(2,1)S(1)} %get-tuple-element.45), channel_id=1, source_target_pairs={{0,6},{2,4},{4,10},{6,8},{8,14},{10,12},{1,7},{3,5},{5,11},{7,9},{... | collective-permute-start | bytes 589832 | tf_op jit(solution)/shard_map/ppermute | solution.py:275
  138.6 14.3 %collective-permute-start.42 = (bf16[128,768]{1,0:T(8,128)(2,1)S(1)}, bf16[128,768]{1,0:T(8,128)(2,1)S(1)}, u32[]{:S(2)}, u32[]{:S(2)}) collective-permute-start(bf16[128,768]{1,0:T(8,128)(2,1)S(1)} %get-tuple-element.43), channel_id=1, source_target_pairs={{12,10},{14,8},{8,6},{10,4},{4,2},{6,0},{13,11},{15,9},{9,7},{11,5... | collective-permute-start | bytes 589832 | tf_op jit(solution)/shard_map/ppermute | solution.py:276
  140.8 16.3 %collective-permute-start.27 = (bf16[128,768]{1,0:T(8,128)(2,1)}, bf16[128,768]{1,0:T(8,128)(2,1)S(1)}, u32[]{:S(2)}, u32[]{:S(2)}) collective-permute-start(bf16[128,768]{1,0:T(8,128)(2,1)} %slice_bitcast_fusion.9), channel_id=1, source_target_pairs={{0,2},{2,0},{1,3},{3,1},{4,6},{6,4},{5,7},{7,5},{8,10},{10,8},{9,1... | collective-permute-start | bytes 589832 | tf_op jit(solution)/shard_map/ppermute | solution.py:269
  143.3 13.9 %collective-permute-start.23 = (bf16[128,768]{1,0:T(8,128)(2,1)}, bf16[128,768]{1,0:T(8,128)(2,1)S(1)}, u32[]{:S(2)}, u32[]{:S(2)}) collective-permute-start(bf16[128,768]{1,0:T(8,128)(2,1)} %get-tuple-element.52), channel_id=1, source_target_pairs={{0,4},{4,8},{8,12},{1,5},{5,9},{9,13},{2,6},{6,10},{10,14},{3,7},{... | collective-permute-start | bytes 589832 | tf_op jit(solution)/shard_map/ppermute | solution.py:272
  147.5 9.7 %collective-permute-start.26 = (bf16[128,768]{1,0:T(8,128)(2,1)}, bf16[128,768]{1,0:T(8,128)(2,1)S(1)}, u32[]{:S(2)}, u32[]{:S(2)}) collective-permute-start(bf16[128,768]{1,0:T(8,128)(2,1)} %get-tuple-element.50), channel_id=1, source_target_pairs={{12,8},{8,4},{4,0},{13,9},{9,5},{5,1},{14,10},{10,6},{6,2},{15,11}... | collective-permute-start | bytes 589832 | tf_op jit(solution)/shard_map/ppermute | solution.py:273
  148.8 9.6 %collective-permute-start.28 = (bf16[128,768]{1,0:T(8,128)(2,1)}, bf16[128,768]{1,0:T(8,128)(2,1)S(1)}, u32[]{:S(2)}, u32[]{:S(2)}) collective-permute-start(bf16[128,768]{1,0:T(8,128)(2,1)} %get-tuple-element.51), channel_id=1, source_target_pairs={{0,6},{2,4},{4,10},{6,8},{8,14},{10,12},{1,7},{3,5},{5,11},{7,9},{... | collective-permute-start | bytes 589832 | tf_op jit(solution)/shard_map/ppermute | solution.py:275
  (56 other events, 611.3 us)
where the time goes:
time: 166 us; the launch traced here: 165 us
  starting transfers between devices  74.9 us (45%)
  Pallas kernels  38 us (23%)
  waiting for transfers between devices  35.5 us (21%)
  local copies, waits for them, and re-layouts  13.6 us (8%)
  other arithmetic  2.4 us (1%)
    pallas_call x2, Pallas kernels, attend(): pl.pallas_call(functools.partial(attend_kernel, first=first, pieces=piece...  16.8 us
    pallas_call x2, Pallas kernels, project(): pl.pallas_call(functools.partial(project_kernel, sections=sections, parts...  15.4 us
    ppermute x2, starting transfers between devices, line_reduce(): lax.ppermute(send_up[1], ('section', 'ctx'), crossed(ups))  15.2 us
    ppermute x6, starting transfers between devices, on_device(): lax.ppermute(made[k], 'section', [(z, (z + k) % section_count) for z in r...  12.8 us
    ppermute x8, starting transfers between devices, on_device(): far[k][i] = lax.ppermute(near[k][i], 'head', swap)  11.9 us
    ppermute x8, waiting for transfers between devices, on_device(): far[k][i] = lax.ppermute(near[k][i], 'head', swap)  11.7 us
    ppermute x4, starting transfers between devices, line_reduce(): up = lax.ppermute(send_up, 'section', ups)  10.9 us
    ppermute x6, waiting for transfers between devices, on_device(): lax.ppermute(made[k], 'section', [(z, (z + k) % section_count) for z in r...  10 us
  transfers between devices with their start and end apart: 43, of which 16 were waited for; matrix products, arithmetic and copies ran while one was open for 6% of the time, Pallas kernels for 21%

commit v1 on v0

--- a/solution.py
+++ b/solution.py
@@ -175,11 +175,11 @@
     rows, tokens = near[0][0].shape
     tile = math.gcd(columns, 256)
     per_chunk = columns // tile
-    per_half = weights[3].shape[1] // tile
+    per_half = weights[0].shape[1] // 2 // tile
     base = chunk * per_chunk
     flat = [a for both in (near, far) for k in both for a in k]
-    here = lambda n, ids: (0, base + n)
-    start = lambda n, ids: (0, n)
+    local = lambda n, ids: (0, ids[2] * per_half + base + n)
+    sent = lambda n, ids: (0, n)
     return pl.pallas_call(
         functools.partial(project_kernel, sections=sections, parts=parts),
         out_shape=[jax.ShapeDtypeStruct((2, tokens, columns), jnp.bfloat16)] * sections,
@@ -188,13 +188,8 @@
             grid=(per_chunk,),
             in_specs=[pl.BlockSpec(a.shape, lambda n, ids: (0, 0)) for a in flat]
             + [
-                pl.BlockSpec(
-                    (weights[0].shape[0], tile), lambda n, ids: (0, ids[2] * per_half + base + n)
-                )
-            ]
-            + [
-                pl.BlockSpec((w.shape[0], tile), here if w is weights[3] else start)
-                for w in weights[1:]
+                pl.BlockSpec((w.shape[0], tile), sent if i % 3 else local)
+                for i, w in enumerate(weights)
             ],
             out_specs=[pl.BlockSpec((2, tokens, tile), lambda n, ids: (0, 0, n))] * sections,
             scratch_shapes=[pltpu.VMEM((sections * tokens, 2 * parts * rows), jnp.bfloat16)],
@@ -312,7 +307,7 @@
         parts = 2
         columns = out_columns // column_chunks
         half_rows = w_local.shape[0] // 2
-        w_one, w_two, twin_kept, twin_one, twin_two = ([None] * column_chunks for _ in range(5))
+        w_one, w_two, twin_one, twin_two = ([None] * column_chunks for _ in range(4))
         for chunk in range(column_chunks):
             sent = lax.dynamic_slice(
                 w_local,
@@ -320,8 +315,7 @@
                 (half_rows, columns),
             )
             w_one[chunk] = lax.ppermute(sent, "head", swap)
-        w_kept = lax.dynamic_slice_in_dim(w_local, head * out_columns, out_columns, 1)
-        twin_kept = lax.ppermute(w_kept, "ctx", swap)
+        twin_local = lax.ppermute(w_local, "ctx", swap)
         near = [[None] * parts for _ in range(section_count)]
         far = [[None] * parts for _ in range(section_count)]
         arrays = blocks
@@ -339,17 +333,24 @@
                     "section",
                     [(z, (z + k) % section_count) for z in range(section_count)],
                 )
-            for k in range(section_count):
+            for k in sum(shift_sets(section_count), []):
                 far[k][i] = lax.ppermute(near[k][i], "head", swap)
         for chunk in range(column_chunks):
             w_two[chunk] = lax.ppermute(w_one[chunk], "group", swap)
             twin_one[chunk] = lax.ppermute(w_one[chunk], "ctx", swap)
             twin_two[chunk] = lax.ppermute(w_two[chunk], "ctx", swap)
+        partial = [[None] * section_count for _ in range(column_chunks)]
+        for shifts in shift_sets(section_count):
+            for chunk in range(column_chunks):
+                weights = [w_local, w_one[chunk], w_two[chunk], twin_local, twin_one[chunk], twin_two[chunk]]
+                made = project(
+                    ids, [near[k] for k in shifts], [far[k] for k in shifts], weights, chunk, columns
+                )
+                for k, value in zip(shifts, made):
+                    partial[chunk][k] = value
         out = None
         for chunk in range(column_chunks):
-            weights = [w_local, w_one[chunk], w_two[chunk], twin_kept, twin_one[chunk], twin_two[chunk]]
-            partial = project(ids, near, far, weights, chunk, columns)
-            out = combine(ids, *line_reduce(partial), out, chunk, column_chunks)
+            out = combine(ids, *line_reduce(partial[chunk]), out, chunk, column_chunks)
         return out
 
     attended = attend(ids, block_table, slice_index, q, blocks, block_len, 0, heads, 1, True)[0][0]
@@ -368,6 +369,11 @@
     return sorted(range(1, sections), key=lambda k: min(k, sections - k))
 
 
+def shift_sets(sections):
+    first = sorted({1, sections - 1})
+    return [first, [k for k in range(1, sections) if k not in first] + [0]]
+
+
 def solution(mesh):
     placed = (
         P(("group", "section"), "head", None),

time: 166 us -> 177 us (1.066)
  waiting for transfers between devices: 35.5 us -> 48.7 us
  starting transfers between devices: 74.9 us -> 64.9 us
  Pallas kernels: 38 us -> 47.8 us
  local copies, waits for them, and re-layouts: 13.6 us -> 11 us
    ppermute x2, waiting for transfers between devices: 0.01 us -> 22.1 us  [on_device(): w_one[chunk] = lax.ppermute(sent, 'head', swap)]
    pallas_call x2 -> x4, Pallas kernels: 15.4 us -> 25.2 us  [project(): pl.pallas_call(functools.partial(project_kernel, sections=sections, parts...]
    ppermute x2, starting transfers between devices: 15.2 us -> 7.21 us  [line_reduce(): lax.ppermute(send_up[1], ('section', 'ctx'), crossed(ups))]
    ppermute x8, waiting for transfers between devices: 11.7 us -> 6.76 us  [on_device(): far[k][i] = lax.ppermute(near[k][i], 'head', swap)]
    ppermute x2, starting transfers between devices: 0.01 us -> 3.82 us  [on_device(): w_two[chunk] = lax.ppermute(w_one[chunk], 'group', swap)]
    dynamic_slice x1 -> x0, local copies, waits for them, and re-layouts: 3.36 us -> none  [on_device(): lax.dynamic_slice_in_dim(w_local, head * out_columns, out_columns, 1)]
    ppermute x8, starting transfers between devices: 11.9 us -> 8.74 us  [on_device(): far[k][i] = lax.ppermute(near[k][i], 'head', swap)]
    ppermute x6, waiting for transfers between devices: 10 us -> 7.16 us  [on_device(): lax.ppermute(made[k], 'section', [(z, (z + k) % section_count) for z in r...]
  transfers between devices with their start and end apart: 43 -> 43, of which waited for: 16 -> 12; matrix products, arithmetic and copies ran while one was open for 6% -> 7% of each run, Pallas kernels for 21% -> 25%
where the time goes in v1:
time: 177 us; the launch traced here: 176 us
  starting transfers between devices  64.9 us (37%)
  waiting for transfers between devices  48.7 us (28%)
  Pallas kernels  47.8 us (27%)
  local copies, waits for them, and re-layouts  11 us (6%)
  other arithmetic  3.51 us (2%)
    pallas_call x4, Pallas kernels, project(): pl.pallas_call(functools.partial(project_kernel, sections=sections, parts...  25.2 us
    ppermute x2, waiting for transfers between devices, on_device(): w_one[chunk] = lax.ppermute(sent, 'head', swap)  22.1 us
    pallas_call x2, Pallas kernels, attend(): pl.pallas_call(functools.partial(attend_kernel, first=first, pieces=piece...  16.9 us
    ppermute x4, starting transfers between devices, line_reduce(): up = lax.ppermute(send_up, 'section', ups)  12.3 us
    ppermute x6, starting transfers between devices, on_device(): lax.ppermute(made[k], 'section', [(z, (z + k) % section_count) for z in r...  9.96 us
    ppermute x2, starting transfers between devices, line_reduce(): lax.ppermute(send_up[0], 'section', ups)  8.83 us
    ppermute x8, starting transfers between devices, on_device(): far[k][i] = lax.ppermute(near[k][i], 'head', swap)  8.74 us
    ppermute x4, waiting for transfers between devices, line_reduce(): up = lax.ppermute(send_up, 'section', ups)  8.07 us
  transfers between devices with their start and end apart: 43, of which 12 were waited for; matrix products, arithmetic and copies ran while one was open for 7% of the time, Pallas kernels for 25%

profile of v1, /device:TPU:0, one launch (start us, length us, event | category | flops | bytes accessed | tf_op | source)
XLA Modules:
  0.0 176.4 jit_solution(6509406301546755981)
XLA Ops:
  2.7 2.6 %collective-permute-start.8 = (bf16[384,768]{1,0:T(8,128)(2,1)S(1)}, bf16[384,768]{1,0:T(8,128)(2,1)S(1)}, u32[]{:S(2)}, u32[]{:S(2)}) collective-permute-start(bf16[384,768]{1,0:T(8,128)(2,1)S(1)} %get-tuple-element.42), channel_id=1, source_target_pairs={{0,1},{1,0},{2,3},{3,2},{4,5},{5,4},{6,7},{7,6},{8,9},{9,8},{10,11... | collective-permute-start | bytes 1769480 | tf_op jit(solution)/shard_map/ppermute | solution.py:317
  5.8 13.6 %collective-permute-done.8.refs_9_ = bf16[384,768]{1,0:T(8,128)(2,1)S(1)} collective-permute-done((bf16[384,768]{1,0:T(8,128)(2,1)S(1)}, bf16[384,768]{1,0:T(8,128)(2,1)S(1)}, u32[]{:S(2)}, u32[]{:S(2)}) %collective-permute-start.8) | collective-permute-done | bytes 589856 | tf_op jit(solution)/shard_map/ppermute | solution.py:317
  23.3 8.4 %collective-permute-done.30.refs_9_ = bf16[384,768]{1,0:T(8,128)(2,1)S(1)} collective-permute-done((bf16[384,768]{1,0:T(8,128)(2,1)}, bf16[384,768]{1,0:T(8,128)(2,1)S(1)}, u32[]{:S(2)}, u32[]{:S(2)}) %collective-permute-start.30) | collective-permute-done | bytes 589856 | tf_op jit(solution)/shard_map/ppermute | solution.py:317
  34.2 9.2 %attend.2 = (bf16[384,128]{1,0:T(8,128)(2,1)}, bf16[384,128]{1,0:T(8,128)(2,1)}, bf16[384,128]{1,0:T(8,128)(2,1)}, bf16[384,128]{1,0:T(8,128)(2,1)}, bf16[2304,1...) custom-call(s32[4]{0:T(128)} %pad_add_fusion.ids_ref, s32[4,16]{1,0:T(4,128)} %table_ref.3, s32[4]{0:T(128)} %index_ref.3, ...), custom_call_target="tpu_custom_call" | custom-call | tf_op jit(solution)/shard_map/attend/pallas_call | solution.py:119
  43.4 3.2 %collective-permute-start.13 = (bf16[384,128]{1,0:T(8,128)(2,1)}, bf16[384,128]{1,0:T(8,128)(2,1)S(1)}, u32[]{:S(2)}, u32[]{:S(2)}) collective-permute-start(bf16[384,128]{1,0:T(8,128)(2,1)} %get-tuple-element.30), channel_id=1, source_target_pairs={{0,4},{4,8},{8,12},{12,0},{1,5},{5,9},{9,13},{13,1},{2,6},{6,10},{... | collective-permute-start | bytes 294920 | tf_op jit(solution)/shard_map/ppermute | solution.py:331
  46.6 7.7 %attend.3 = (bf16[384,128]{1,0:T(8,128)(2,1)}, bf16[384,128]{1,0:T(8,128)(2,1)}, bf16[384,128]{1,0:T(8,128)(2,1)}, bf16[384,128]{1,0:T(8,128)(2,1)}) custom-call(s32[4]{0:T(128)} %pad_add_fusion.ids_ref, s32[4,16]{1,0:T(4,128)} %table_ref.3, s32[4]{0:T(128)} %index_ref.3, bf16[24,128,128]{2,1,0:T(8,128)(2,1)} %bitcast.40, ...), custom_call_target="tpu_custom_call" | custom-call | tf_op jit(solution)/shard_map/attend/pallas_call | solution.py:119
  55.6 2.5 %collective-permute-start.15 = (bf16[384,128]{1,0:T(8,128)(2,1)}, bf16[384,128]{1,0:T(8,128)(2,1)S(1)}, u32[]{:S(2)}, u32[]{:S(2)}) collective-permute-start(bf16[384,128]{1,0:T(8,128)(2,1)} %get-tuple-element.32), channel_id=1, source_target_pairs={{0,12},{4,0},{8,4},{12,8},{1,13},{5,1},{9,5},{13,9},{2,14},{6,2},{... | collective-permute-start | bytes 294920 | tf_op jit(solution)/shard_map/ppermute | solution.py:331
  58.1 3.5 %collective-permute-done.14.refs_1_ = bf16[384,128]{1,0:T(8,128)(2,1)S(1)} collective-permute-done((bf16[384,128]{1,0:T(8,128)(2,1)}, bf16[384,128]{1,0:T(8,128)(2,1)S(1)}, u32[]{:S(2)}, u32[]{:S(2)}) %collective-permute-start.14) | collective-permute-done | bytes 98336 | tf_op jit(solution)/shard_map/ppermute | solution.py:331
  63.2 3.3 %collective-permute-done.16.refs_3_ = bf16[384,128]{1,0:T(8,128)(2,1)S(1)} collective-permute-done((bf16[384,128]{1,0:T(8,128)(2,1)}, bf16[384,128]{1,0:T(8,128)(2,1)S(1)}, u32[]{:S(2)}, u32[]{:S(2)}) %collective-permute-start.16) | collective-permute-done | bytes 98336 | tf_op jit(solution)/shard_map/ppermute | solution.py:331
  73.6 3.6 %collective-permute-done.20.refs_7_ = bf16[384,128]{1,0:T(8,128)(2,1)S(1)} collective-permute-done((bf16[384,128]{1,0:T(8,128)(2,1)S(1)}, bf16[384,128]{1,0:T(8,128)(2,1)S(1)}, u32[]{:S(2)}, u32[]{:S(2)}) %collective-permute-start.20) | collective-permute-done | bytes 98336 | tf_op jit(solution)/shard_map/ppermute | solution.py:337
  82.7 6.3 %project.5 = (bf16[2,128,768]{2,1,0:T(8,128)(2,1)}, bf16[2,128,768]{2,1,0:T(8,128)(2,1)}) custom-call(s32[4]{0:T(128)} %pad_add_fusion.ids_ref, bf16[384,128]{1,0:T(8,128)(2,1)} %copy-done.7, bf16[384,128]{1,0:T(8,128)(2,1)} %copy-done.8, bf16[384,128]{1,0:T(8,128)(2,1)} %copy-done.9, bf16[384,128]{1,0:T(8,128)(2,1)} %copy-done.10, ...), custom_call_target="tpu_custom_call" | custom-call | tf_op jit(solution)/shard_map/project/pallas_call | solution.py:183
  90.0 3.9 %collective-permute-start.21 = (bf16[2,128,768]{2,1,0:T(8,128)(2,1)}, bf16[2,128,768]{2,1,0:T(8,128)(2,1)S(1)}, u32[]{:S(2)}, u32[]{:S(2)}) collective-permute-start(bf16[2,128,768]{2,1,0:T(8,128)(2,1)} %get-tuple-element.36), channel_id=1, source_target_pairs={{0,4},{1,5},{2,6},{3,7},{16,20},{17,21},{18,22},{19,23}} | collective-permute-start | bytes 1179656 | tf_op jit(solution)/shard_map/ppermute | solution.py:261
  96.6 6.3 %project.7 = (bf16[2,128,768]{2,1,0:T(8,128)(2,1)}, bf16[2,128,768]{2,1,0:T(8,128)(2,1)}) custom-call(s32[4]{0:T(128)} %pad_add_fusion.ids_ref, bf16[384,128]{1,0:T(8,128)(2,1)} %copy-done.7, bf16[384,128]{1,0:T(8,128)(2,1)} %copy-done.8, bf16[384,128]{1,0:T(8,128)(2,1)} %copy-done.9, bf16[384,128]{1,0:T(8,128)(2,1)} %copy-done.10, ...), custom_call_target="tpu_custom_call" | custom-call | tf_op jit(solution)/shard_map/project/pallas_call | solution.py:183
  106.3 6.2 %project.6 = (bf16[2,128,768]{2,1,0:T(8,128)(2,1)}, bf16[2,128,768]{2,1,0:T(8,128)(2,1)}) custom-call(s32[4]{0:T(128)} %pad_add_fusion.ids_ref, bf16[384,128]{1,0:T(8,128)(2,1)} %collective-permute-done.2.refs_0_, bf16[384,128]{1,0:T(8,128)(2,1)} %collective-permute-done.3.refs_1_, bf16[384,128]{1,0:T(8,128)(2,1)} %get-tuple-element.27.refs_2_, ...), custom_call_target="tpu_custom_call" | custom-call | tf_op jit(solution)/shard_map/project/pallas_call | solution.py:183
  114.2 6.4 %project.4 = (bf16[2,128,768]{2,1,0:T(8,128)(2,1)}, bf16[2,128,768]{2,1,0:T(8,128)(2,1)}) custom-call(s32[4]{0:T(128)} %pad_add_fusion.ids_ref, bf16[384,128]{1,0:T(8,128)(2,1)} %collective-permute-done.2.refs_0_, bf16[384,128]{1,0:T(8,128)(2,1)} %collective-permute-done.3.refs_1_, bf16[384,128]{1,0:T(8,128)(2,1)} %get-tuple-element.27.refs_2_, ...), custom_call_target="tpu_custom_call" | custom-call | tf_op jit(solution)/shard_map/project/pallas_call | solution.py:183
  127.5 5.0 %collective-permute-start.35 = (bf16[2,128,768]{2,1,0:T(8,128)(2,1)S(1)}, bf16[2,128,768]{2,1,0:T(8,128)(2,1)S(1)}, u32[]{:S(2)}, u32[]{:S(2)}) collective-permute-start(bf16[2,128,768]{2,1,0:T(8,128)(2,1)S(1)} %get-tuple-element.48), channel_id=1, source_target_pairs={{0,4},{4,8},{1,5},{5,9},{2,6},{6,10},{3,7},{7,11},{16,20},{20,24},... | collective-permute-start | bytes 1179656 | tf_op jit(solution)/shard_map/ppermute | solution.py:261
  134.2 7.2 %collective-permute-done.35 = bf16[2,128,768]{2,1,0:T(8,128)(2,1)S(1)} collective-permute-done((bf16[2,128,768]{2,1,0:T(8,128)(2,1)S(1)}, bf16[2,128,768]{2,1,0:T(8,128)(2,1)S(1)}, u32[]{:S(2)}, u32[]{:S(2)}) %collective-permute-start.35) | collective-permute-done | bytes 393248 | tf_op jit(solution)/shard_map/ppermute | solution.py:261
  141.7 4.4 %collective-permute-start.36 = (bf16[128,768]{1,0:T(8,128)(2,1)S(1)}, bf16[128,768]{1,0:T(8,128)(2,1)S(1)}, u32[]{:S(2)}, u32[]{:S(2)}) collective-permute-start(bf16[128,768]{1,0:T(8,128)(2,1)S(1)} %get-tuple-element.46), channel_id=1, source_target_pairs={{0,4},{4,8},{8,12},{1,5},{5,9},{9,13},{2,6},{6,10},{10,14},{3,7},{... | collective-permute-start | bytes 589832 | tf_op jit(solution)/shard_map/ppermute | solution.py:267
  147.4 3.2 %collective-permute-start.41 = (bf16[128,768]{1,0:T(8,128)(2,1)S(1)}, bf16[128,768]{1,0:T(8,128)(2,1)S(1)}, u32[]{:S(2)}, u32[]{:S(2)}) collective-permute-start(bf16[128,768]{1,0:T(8,128)(2,1)S(1)} %get-tuple-element.45), channel_id=1, source_target_pairs={{0,6},{2,4},{4,10},{6,8},{8,14},{10,12},{1,7},{3,5},{5,11},{7,9},{... | collective-permute-start | bytes 589832 | tf_op jit(solution)/shard_map/ppermute | solution.py:270
  154.2 4.4 %collective-permute-start.23 = (bf16[128,768]{1,0:T(8,128)(2,1)}, bf16[128,768]{1,0:T(8,128)(2,1)S(1)}, u32[]{:S(2)}, u32[]{:S(2)}) collective-permute-start(bf16[128,768]{1,0:T(8,128)(2,1)} %get-tuple-element.52), channel_id=1, source_target_pairs={{0,4},{4,8},{8,12},{1,5},{5,9},{9,13},{2,6},{6,10},{10,14},{3,7},{... | collective-permute-start | bytes 589832 | tf_op jit(solution)/shard_map/ppermute | solution.py:267
  160.0 4.0 %collective-permute-start.28 = (bf16[128,768]{1,0:T(8,128)(2,1)S(1)}, bf16[128,768]{1,0:T(8,128)(2,1)S(1)}, u32[]{:S(2)}, u32[]{:S(2)}) collective-permute-start(bf16[128,768]{1,0:T(8,128)(2,1)S(1)} %get-tuple-element.51), channel_id=1, source_target_pairs={{0,6},{2,4},{4,10},{6,8},{8,14},{10,12},{1,7},{3,5},{5,11},{7,9},{... | collective-permute-start | bytes 589832 | tf_op jit(solution)/shard_map/ppermute | solution.py:270
  165.3 2.9 %combine.2.rest_0_ = bf16[256,1536]{1,0:T(8,128)(2,1)} custom-call(s32[4]{0:T(128)} %pad_add_fusion.ids_ref, bf16[2,128,768]{2,1,0:T(8,128)(2,1)} %get-tuple-element.37.own, bf16[128,768]{1,0:T(8,128)(2,1)} %copy-done.21, bf16[128,768]{1,0:T(8,128)(2,1)} %copy-done.23, bf16[128,768]{1,0:T(8,128)(2,1)} %collective-permute-done.40.twin, ...), custom_call_target="tpu_custom_call" | custom-call | tf_op jit(solution)/shard_map/combine/pallas_call | solution.py:228
  169.2 3.6 %collective-permute-done.29.cross_down = bf16[128,768]{1,0:T(8,128)(2,1)S(1)} collective-permute-done((bf16[128,768]{1,0:T(8,128)(2,1)}, bf16[128,768]{1,0:T(8,128)(2,1)S(1)}, u32[]{:S(2)}, u32[]{:S(2)}) %collective-permute-start.29) | collective-permute-done | bytes 196640 | tf_op jit(solution)/shard_map/ppermute | solution.py:271
  173.5 2.9 %combine.3 = bf16[256,1536]{1,0:T(8,128)(2,1)} custom-call(s32[4]{0:T(128)} %pad_add_fusion.ids_ref, bf16[2,128,768]{2,1,0:T(8,128)(2,1)} %get-tuple-element.29.own, bf16[128,768]{1,0:T(8,128)(2,1)} %copy-done.25, bf16[128,768]{1,0:T(8,128)(2,1)} %copy-done.27, bf16[128,768]{1,0:T(8,128)(2,1)} %copy-done.22, ...), custom_call_target="tpu_custom_call", output_to_operand_aliasing={{}: (7, {})} | custom-call | tf_op jit(solution)/shard_map/combine/pallas_call | solution.py:228
  (147 shorter events, 51.6 us)
Async XLA Ops:
  0.0 81.5 %collective-permute-start.10 = (bf16[768,3072]{1,0:T(8,128)(2,1)}, bf16[768,3072]{1,0:T(8,128)(2,1)}, u32[]{:S(2)}, u32[]{:S(2)}) collective-permute-start(bf16[768,3072]{1,0:T(8,128)(2,1)} %bitcast.33), channel_id=1, source_target_pairs={{0,2},{2,0},{1,3},{3,1},{4,6},{6,4},{5,7},{7,5},{8,10},{10,8},{9,1... | collective-permute-start | bytes 14155784 | tf_op jit(solution)/shard_map/ppermute | solution.py:318
  2.7 16.8 %collective-permute-start.8 = (bf16[384,768]{1,0:T(8,128)(2,1)S(1)}, bf16[384,768]{1,0:T(8,128)(2,1)S(1)}, u32[]{:S(2)}, u32[]{:S(2)}) collective-permute-start(bf16[384,768]{1,0:T(8,128)(2,1)S(1)} %get-tuple-element.42), channel_id=1, source_target_pairs={{0,1},{1,0},{2,3},{3,2},{4,5},{5,4},{6,7},{7,6},{8,9},{9,8},{10,11... | collective-permute-start | bytes 1769480 | tf_op jit(solution)/shard_map/ppermute | solution.py:317
  5.3 26.5 %collective-permute-start.30 = (bf16[384,768]{1,0:T(8,128)(2,1)}, bf16[384,768]{1,0:T(8,128)(2,1)S(1)}, u32[]{:S(2)}, u32[]{:S(2)}) collective-permute-start(bf16[384,768]{1,0:T(8,128)(2,1)} %get-tuple-element.41), channel_id=1, source_target_pairs={{0,1},{1,0},{2,3},{3,2},{4,5},{5,4},{6,7},{7,6},{8,9},{9,8},{10,11... | collective-permute-start | bytes 1769480 | tf_op jit(solution)/shard_map/ppermute | solution.py:317
  5.3 28.9 %collective-permute-start = (bf16[8,128,128]{2,1,0:T(8,128)(2,1)}, bf16[8,128,128]{2,1,0:T(8,128)(2,1)}, u32[]{:S(2)}, u32[]{:S(2)}) collective-permute-start(bf16[8,128,128]{2,1,0:T(8,128)(2,1)} %bitcast.42), channel_id=1, source_target_pairs={{0,2},{2,0},{1,3},{3,1},{4,6},{6,4},{5,7},{7,5},{8,10},{10,8},{9,1... | collective-permute-start | bytes 786440 | tf_op jit(solution)/shard_map/ppermute | solution.py:300
  5.4 28.8 %collective-permute-start.1 = (bf16[8,128,128]{2,1,0:T(8,128)(2,1)}, bf16[8,128,128]{2,1,0:T(8,128)(2,1)}, u32[]{:S(2)}, u32[]{:S(2)}) collective-permute-start(bf16[8,128,128]{2,1,0:T(8,128)(2,1)} %bitcast.44), channel_id=1, source_target_pairs={{0,2},{2,0},{1,3},{3,1},{4,6},{6,4},{5,7},{7,5},{8,10},{10,8},{9,1... | collective-permute-start | bytes 786440 | tf_op jit(solution)/shard_map/ppermute | solution.py:301
  19.5 51.7 %collective-permute-start.9 = (bf16[384,768]{1,0:T(8,128)(2,1)S(1)}, bf16[384,768]{1,0:T(8,128)(2,1)S(1)}, u32[]{:S(2)}, u32[]{:S(2)}) collective-permute-start(bf16[384,768]{1,0:T(8,128)(2,1)S(1)} %collective-permute-done.8.refs_9_), channel_id=1, source_target_pairs={{0,16},{16,0},{1,17},{17,1},{2,18},{18,2},{3,19},{19,3},{4,20},{20... | collective-permute-start | bytes 1769480 | tf_op jit(solution)/shard_map/ppermute | solution.py:339
  31.8 45.4 %collective-permute-start.31 = (bf16[384,768]{1,0:T(8,128)(2,1)S(1)}, bf16[384,768]{1,0:T(8,128)(2,1)}, u32[]{:S(2)}, u32[]{:S(2)}) collective-permute-start(bf16[384,768]{1,0:T(8,128)(2,1)S(1)} %collective-permute-done.30.refs_9_), channel_id=1, source_target_pairs={{0,16},{16,0},{1,17},{17,1},{2,18},{18,2},{3,19},{19,3},{4,20},{20... | collective-permute-start | bytes 1769480 | tf_op jit(solution)/shard_map/ppermute | solution.py:339
  43.4 12.2 %collective-permute-start.13 = (bf16[384,128]{1,0:T(8,128)(2,1)}, bf16[384,128]{1,0:T(8,128)(2,1)S(1)}, u32[]{:S(2)}, u32[]{:S(2)}) collective-permute-start(bf16[384,128]{1,0:T(8,128)(2,1)} %get-tuple-element.30), channel_id=1, source_target_pairs={{0,4},{4,8},{8,12},{12,0},{1,5},{5,9},{9,13},{13,1},{2,6},{6,10},{... | collective-permute-start | bytes 294920 | tf_op jit(solution)/shard_map/ppermute | solution.py:331
  77.2 17.4 %collective-permute-start.32 = (bf16[384,768]{1,0:T(8,128)(2,1)S(1)}, bf16[384,768]{1,0:T(8,128)(2,1)}, u32[]{:S(2)}, u32[]{:S(2)}) collective-permute-start(bf16[384,768]{1,0:T(8,128)(2,1)S(1)} %collective-permute-done.30.refs_9_), channel_id=1, source_target_pairs={{0,2},{2,0},{1,3},{3,1},{4,6},{6,4},{5,7},{7,5},{8,10},{10,8},{9,1... | collective-permute-start | bytes 1769480 | tf_op jit(solution)/shard_map/ppermute | solution.py:340
  77.2 18.9 %collective-permute-start.33 = (bf16[384,768]{1,0:T(8,128)(2,1)}, bf16[384,768]{1,0:T(8,128)(2,1)}, u32[]{:S(2)}, u32[]{:S(2)}) collective-permute-start(bf16[384,768]{1,0:T(8,128)(2,1)} %collective-permute-done.31.refs_10_), channel_id=1, source_target_pairs={{0,2},{2,0},{1,3},{3,1},{4,6},{6,4},{5,7},{7,5},{8,10},{10,8},{9,1... | collective-permute-start | bytes 1769480 | tf_op jit(solution)/shard_map/ppermute | solution.py:341
  77.7 11.2 %collective-permute-start.2 = (bf16[384,128]{1,0:T(8,128)(2,1)}, bf16[384,128]{1,0:T(8,128)(2,1)}, u32[]{:S(2)}, u32[]{:S(2)}) collective-permute-start(bf16[384,128]{1,0:T(8,128)(2,1)} %get-tuple-element.23), channel_id=1, source_target_pairs={{0,8},{4,12},{8,0},{12,4},{1,9},{5,13},{9,1},{13,5},{2,10},{6,14},... | collective-permute-start | bytes 294920 | tf_op jit(solution)/shard_map/ppermute | solution.py:331
  81.5 12.4 %collective-permute-start.6 = (bf16[384,128]{1,0:T(8,128)(2,1)}, bf16[384,128]{1,0:T(8,128)(2,1)}, u32[]{:S(2)}, u32[]{:S(2)}) collective-permute-start(bf16[384,128]{1,0:T(8,128)(2,1)} %get-tuple-element.27.refs_2_), channel_id=1, source_target_pairs={{0,1},{1,0},{2,3},{3,2},{4,5},{5,4},{6,7},{7,6},{8,9},{9,8},{10,11... | collective-permute-start | bytes 294920 | tf_op jit(solution)/shard_map/ppermute | solution.py:337
  89.0 31.7 %collective-permute-start.24 = (bf16[2,128,768]{2,1,0:T(8,128)(2,1)}, bf16[2,128,768]{2,1,0:T(8,128)(2,1)S(1)}, u32[]{:S(2)}, u32[]{:S(2)}) collective-permute-start(bf16[2,128,768]{2,1,0:T(8,128)(2,1)} %get-tuple-element.34), channel_id=1, source_target_pairs={{12,8},{13,9},{14,10},{15,11},{28,24},{29,25},{30,26},{31,27}} | collective-permute-start | bytes 1179656 | tf_op jit(solution)/shard_map/ppermute | solution.py:262
  90.0 30.6 %collective-permute-start.21 = (bf16[2,128,768]{2,1,0:T(8,128)(2,1)}, bf16[2,128,768]{2,1,0:T(8,128)(2,1)S(1)}, u32[]{:S(2)}, u32[]{:S(2)}) collective-permute-start(bf16[2,128,768]{2,1,0:T(8,128)(2,1)} %get-tuple-element.36), channel_id=1, source_target_pairs={{0,4},{1,5},{2,6},{3,7},{16,20},{17,21},{18,22},{19,23}} | collective-permute-start | bytes 1179656 | tf_op jit(solution)/shard_map/ppermute | solution.py:261
  102.9 22.6 %collective-permute-start.37 = (bf16[2,128,768]{2,1,0:T(8,128)(2,1)}, bf16[2,128,768]{2,1,0:T(8,128)(2,1)S(1)}, u32[]{:S(2)}, u32[]{:S(2)}) collective-permute-start(bf16[2,128,768]{2,1,0:T(8,128)(2,1)} %get-tuple-element.38), channel_id=1, source_target_pairs={{12,8},{13,9},{14,10},{15,11},{28,24},{29,25},{30,26},{31,27}} | collective-permute-start | bytes 1179656 | tf_op jit(solution)/shard_map/ppermute | solution.py:262
  103.6 21.9 %collective-permute-start.34 = (bf16[2,128,768]{2,1,0:T(8,128)(2,1)}, bf16[2,128,768]{2,1,0:T(8,128)(2,1)}, u32[]{:S(2)}, u32[]{:S(2)}) collective-permute-start(bf16[2,128,768]{2,1,0:T(8,128)(2,1)} %get-tuple-element.40), channel_id=1, source_target_pairs={{0,4},{1,5},{2,6},{3,7},{16,20},{17,21},{18,22},{19,23}} | collective-permute-start | bytes 1179656 | tf_op jit(solution)/shard_map/ppermute | solution.py:261
  114.2 38.6 %collective-permute-start.40 = (bf16[128,768]{1,0:T(8,128)(2,1)}, bf16[128,768]{1,0:T(8,128)(2,1)}, u32[]{:S(2)}, u32[]{:S(2)}) collective-permute-start(bf16[128,768]{1,0:T(8,128)(2,1)} %slice_bitcast_fusion.8), channel_id=1, source_target_pairs={{0,2},{2,0},{1,3},{3,1},{4,6},{6,4},{5,7},{7,5},{8,10},{10,8},{9,1... | collective-permute-start | bytes 589832 | tf_op jit(solution)/shard_map/ppermute | solution.py:264
  127.5 14.0 %collective-permute-start.35 = (bf16[2,128,768]{2,1,0:T(8,128)(2,1)S(1)}, bf16[2,128,768]{2,1,0:T(8,128)(2,1)S(1)}, u32[]{:S(2)}, u32[]{:S(2)}) collective-permute-start(bf16[2,128,768]{2,1,0:T(8,128)(2,1)S(1)} %get-tuple-element.48), channel_id=1, source_target_pairs={{0,4},{4,8},{1,5},{5,9},{2,6},{6,10},{3,7},{7,11},{16,20},{20,24},... | collective-permute-start | bytes 1179656 | tf_op jit(solution)/shard_map/ppermute | solution.py:261
  141.7 12.5 %collective-permute-start.36 = (bf16[128,768]{1,0:T(8,128)(2,1)S(1)}, bf16[128,768]{1,0:T(8,128)(2,1)S(1)}, u32[]{:S(2)}, u32[]{:S(2)}) collective-permute-start(bf16[128,768]{1,0:T(8,128)(2,1)S(1)} %get-tuple-element.46), channel_id=1, source_target_pairs={{0,4},{4,8},{8,12},{1,5},{5,9},{9,13},{2,6},{6,10},{10,14},{3,7},{... | collective-permute-start | bytes 589832 | tf_op jit(solution)/shard_map/ppermute | solution.py:267
  146.1 12.5 %collective-permute-start.39 = (bf16[128,768]{1,0:T(8,128)(2,1)S(1)}, bf16[128,768]{1,0:T(8,128)(2,1)S(1)}, u32[]{:S(2)}, u32[]{:S(2)}) collective-permute-start(bf16[128,768]{1,0:T(8,128)(2,1)S(1)} %get-tuple-element.44), channel_id=1, source_target_pairs={{12,8},{8,4},{4,0},{13,9},{9,5},{5,1},{14,10},{10,6},{6,2},{15,11}... | collective-permute-start | bytes 589832 | tf_op jit(solution)/shard_map/ppermute | solution.py:268
  147.4 12.5 %collective-permute-start.41 = (bf16[128,768]{1,0:T(8,128)(2,1)S(1)}, bf16[128,768]{1,0:T(8,128)(2,1)S(1)}, u32[]{:S(2)}, u32[]{:S(2)}) collective-permute-start(bf16[128,768]{1,0:T(8,128)(2,1)S(1)} %get-tuple-element.45), channel_id=1, source_target_pairs={{0,6},{2,4},{4,10},{6,8},{8,14},{10,12},{1,7},{3,5},{5,11},{7,9},{... | collective-permute-start | bytes 589832 | tf_op jit(solution)/shard_map/ppermute | solution.py:270
  150.6 13.3 %collective-permute-start.42 = (bf16[128,768]{1,0:T(8,128)(2,1)S(1)}, bf16[128,768]{1,0:T(8,128)(2,1)S(1)}, u32[]{:S(2)}, u32[]{:S(2)}) collective-permute-start(bf16[128,768]{1,0:T(8,128)(2,1)S(1)} %get-tuple-element.43), channel_id=1, source_target_pairs={{12,10},{14,8},{8,6},{10,4},{4,2},{6,0},{13,11},{15,9},{9,7},{11,5... | collective-permute-start | bytes 589832 | tf_op jit(solution)/shard_map/ppermute | solution.py:271
  152.7 15.5 %collective-permute-start.27 = (bf16[128,768]{1,0:T(8,128)(2,1)}, bf16[128,768]{1,0:T(8,128)(2,1)S(1)}, u32[]{:S(2)}, u32[]{:S(2)}) collective-permute-start(bf16[128,768]{1,0:T(8,128)(2,1)} %slice_bitcast_fusion.9), channel_id=1, source_target_pairs={{0,2},{2,0},{1,3},{3,1},{4,6},{6,4},{5,7},{7,5},{8,10},{10,8},{9,1... | collective-permute-start | bytes 589832 | tf_op jit(solution)/shard_map/ppermute | solution.py:264
  154.2 14.0 %collective-permute-start.23 = (bf16[128,768]{1,0:T(8,128)(2,1)}, bf16[128,768]{1,0:T(8,128)(2,1)S(1)}, u32[]{:S(2)}, u32[]{:S(2)}) collective-permute-start(bf16[128,768]{1,0:T(8,128)(2,1)} %get-tuple-element.52), channel_id=1, source_target_pairs={{0,4},{4,8},{8,12},{1,5},{5,9},{9,13},{2,6},{6,10},{10,14},{3,7},{... | collective-permute-start | bytes 589832 | tf_op jit(solution)/shard_map/ppermute | solution.py:267
  (50 other events, 561.5 us)

commit v2 on v0

v2 whole, which is shorter than its diff:
```python
import functools
import math

import jax
import jax.numpy as jnp
from jax import lax
from jax.experimental import pallas as pl
from jax.experimental.pallas import tpu as pltpu
from jax.sharding import PartitionSpec as P


BPS = 4

negative_floor = -1e30
chunk_parts = (3, 3, 3, 3)


def attend_kernel(ids_ref, table_ref, index_ref, q_ref, *refs, first, pieces, block_len):
    if first:
        own_ref, kl_ref, vl_ref, kr_ref, vr_ref = refs[:5]
        out_refs = refs[5:-4]
        k_s, vt_s, m_s, acc_s = refs[-4:]
    else:
        k_s, vt_s = refs[:2]
        out_refs = refs[2:-2]
        m_s, acc_s = refs[-2:]
    heads, tokens, head_dim = q_ref.shape
    pool = table_ref.shape[1]
    section = ids_ref[0]
    ctx = ids_ref[1]
    slice_len = k_s.shape[0] - pool * block_len
    steps = index_ref[section] + 1
    width = BPS * block_len
    factor = math.log2(math.e) / math.sqrt(head_dim)

    if first:
        local_pool = kl_ref.shape[0]
        k_s[:slice_len, :] = own_ref[0]
        vt_s[:head_dim, :slice_len] = own_ref[1].T
        vt_s[head_dim:, :] = jnp.ones((vt_s.shape[0] - head_dim, vt_s.shape[1]), vt_s.dtype)

        @pl.loop(0, steps * BPS)
        def _(j):
            place = lax.rem(table_ref[section, j] + pool - ctx * local_pool, pool)
            rows = pl.ds(pl.multiple_of(slice_len + j * block_len, block_len), block_len)

            @pl.when(place < local_pool)
            def _():
                k_s[rows, :] = kl_ref[place]
                vt_s[:head_dim, rows] = vl_ref[place].T

            @pl.when(place >= local_pool)
            def _():
                k_s[rows, :] = kr_ref[place - local_pool]
                vt_s[:head_dim, rows] = vr_ref[place - local_pool].T

    q = q_ref[...].reshape(heads * tokens, head_dim)

    def scores(keys):
        return lax.dot_general(
            keys, q, (((1,), (1,)), ((), ())), preferred_element_type=jnp.float32
        )

    shape = (slice_len, heads * tokens)
    token = lax.rem(lax.broadcasted_iota(jnp.int32, shape, 1), tokens) + ctx * tokens
    s = jnp.where(
        lax.broadcasted_iota(jnp.int32, shape, 0) <= token, scores(k_s[:slice_len, :]), negative_floor
    )
    m = jnp.max(s, axis=0, keepdims=True)
    p = jnp.exp2(s * factor - m * factor).astype(jnp.bfloat16)
    m_s[...] = jnp.broadcast_to(m, m_s.shape)
    acc_s[...] = jnp.dot(vt_s[:, :slice_len], p, preferred_element_type=jnp.float32)

    @pl.loop(0, steps)
    def _(j):
        rows = pl.ds(pl.multiple_of(slice_len + j * width, block_len), width)
        s = scores(k_s[rows, :])
        before = m_s[:1, :]
        m = jnp.maximum(before, jnp.max(s, axis=0, keepdims=True))
        p = jnp.exp2(s * factor - m * factor).astype(jnp.bfloat16)
        rescale = jnp.exp2((before - m) * factor)
        m_s[...] = jnp.broadcast_to(m, m_s.shape)
        acc_s[...] = acc_s[...] * rescale + jnp.dot(
            vt_s[:, rows], p, preferred_element_type=jnp.float32
        )

    acc_s[:head_dim, :] = acc_s[:head_dim, :] / acc_s[head_dim : head_dim + 1, :]
    if pieces == 1:
        out_refs[0][...] = acc_s[:head_dim, :].astype(jnp.bfloat16)
    else:
        piece = head_dim // pieces
        for k in range(pieces):
            rows = pl.ds(pl.multiple_of(lax.bitwise_xor(section, k) * piece, piece), piece)
            for h in range(heads):
                out_refs[k // 2][k % 2, h * piece : (h + 1) * piece, :] = acc_s[
                    rows, h * tokens : (h + 1) * tokens
                ].astype(jnp.bfloat16)


def attend(ids, block_table, slice_index, q, arrays, block_len, first_head, heads, pieces, first):
    tokens, head_dim = q.shape[1:]
    whole = lambda a: pl.BlockSpec(a.shape, lambda g, *_: (0,) * a.ndim)
    pool = block_table.shape[1]
    if first:
        keys = arrays[0].shape[1] + pool * arrays[1].shape[1]
        packed = [
            jax.ShapeDtypeStruct((keys, head_dim), jnp.bfloat16),
            jax.ShapeDtypeStruct((head_dim + 16, keys), jnp.bfloat16),
        ]
    else:
        packed = []
    if pieces == 1:
        out_shape = [jax.ShapeDtypeStruct((head_dim, heads * tokens), jnp.bfloat16)]
    else:
        out_shape = [
            jax.ShapeDtypeStruct((2, heads * head_dim // pieces, tokens), jnp.bfloat16)
        ] * (pieces // 2)
    block = first_head // heads
    outs = pl.pallas_call(
        functools.partial(attend_kernel, first=first, pieces=pieces, block_len=block_len),
        out_shape=out_shape + packed,
        grid_spec=pltpu.PrefetchScalarGridSpec(
            num_scalar_prefetch=3,
            grid=(1,),
            in_specs=[pl.BlockSpec((heads, tokens, head_dim), lambda g, *_: (block, 0, 0))]
            + [whole(a) for a in arrays],
            out_specs=[whole(a) for a in out_shape + packed],
            scratch_shapes=[
                pltpu.VMEM((8, heads * tokens), jnp.float32),
                pltpu.VMEM((head_dim + 16, heads * tokens), jnp.float32),
            ],
        ),
        compiler_params=pltpu.CompilerParams(dimension_semantics=("arbitrary",)),
        name="attend",
    )(ids, block_table, slice_index, q, *arrays)
    return list(outs[: len(out_shape)]), list(outs[len(out_shape) :])


def project_kernel(ids_ref, *refs, parts):
    a_refs = refs[: 4 * parts]
    w_refs = refs[4 * parts : 4 * parts + 4]
    w_pairs = refs[4 * parts + 2 : 4 * parts + 4]
    kept, sent, a_s, w_s = refs[4 * parts + 4 :]
    rows, tokens = a_refs[0].shape[1:]
    columns = kept.shape[2]
    ctx, head, group = ids_ref[1], ids_ref[2], ids_ref[3]
    local_rows = parts * rows
    for i in range(parts):
        place = local_rows + lax.rem(i + group, parts) * rows
        place = pl.ds(pl.multiple_of(place, rows), rows)
        for which in range(4):
            core = ctx if which % 2 == 0 else 1 - ctx
            at = pl.multiple_of((which // 2 * 2 + core) * tokens, tokens)
            at = pl.ds(at, tokens)
            a_s[at, i * rows : (i + 1) * rows] = a_refs[4 * i + which][0].T
            a_s[at, place] = a_refs[4 * i + which][1].T
    for side in range(2):
        at = slice(side * columns, (side + 1) * columns)
        w_s[:local_rows, at] = w_refs[side][...]
        half = head if side == 0 else 1 - head
        for j in range(2):
            w_s[local_rows + j * rows : local_rows + (j + 1) * rows, at] = w_pairs[j][half]
    out = jnp.dot(a_s[...], w_s[...], preferred_element_type=jnp.float32).astype(jnp.bfloat16)
    for k in range(2):
        at = slice(2 * k * tokens, 2 * (k + 1) * tokens)
        sent[k] = out[at, columns:]
        kept[k] = out[at, :columns]


def project(ids, pieces, w_local, w_pairs, base, columns):
    parts = len(pieces)
    rows, tokens = pieces[0][0].shape[1:]
    flat = [a for four in pieces for a in four]
    half = w_local.shape[1] // 2
    whole = lambda a: pl.BlockSpec(a.shape, lambda n, ids: (0,) * a.ndim)
    element = lambda f: pl.BlockSpec(
        (pl.Element(w_local.shape[0]), pl.Element(columns)), lambda n, ids: (0, f(ids))
    )
    shape = jax.ShapeDtypeStruct((2, 2 * tokens, columns), jnp.bfloat16)
    return pl.pallas_call(
        functools.partial(project_kernel, parts=parts),
        out_shape=[shape, shape],
        grid_spec=pltpu.PrefetchScalarGridSpec(
            num_scalar_prefetch=1,
            grid=(1,),
            in_specs=[whole(a) for a in flat]
            + [
                element(lambda ids: pl.multiple_of(ids[2] * half + base, 128)),
                element(lambda ids: pl.multiple_of((1 - ids[2]) * half + base, 128)),
            ]
            + [whole(w) for w in w_pairs],
            out_specs=[whole(shape), whole(shape)],
            scratch_shapes=[
                pltpu.VMEM((4 * tokens, 2 * parts * rows), jnp.bfloat16),
                pltpu.VMEM((2 * parts * rows, 2 * columns), jnp.bfloat16),
            ],
        ),
        compiler_params=pltpu.CompilerParams(dimension_semantics=("arbitrary",)),
        name="project",
    )(ids, *flat, w_local, w_local, *w_pairs)


swap = [(0, 1), (1, 0)]


def add_rounded(*values):
    total = values[0].astype(jnp.float32)
    for value in values[1:]:
        total = total + value.astype(jnp.float32)
    return total.astype(jnp.bfloat16)


def on_device(queries, slice_kv, cache_keys, cache_values, block_table, slice_index, out_weight):
    slice_len, heads, head_dim = queries.shape
    section_count = lax.axis_size("section")
    ctx_count = lax.axis_size("ctx")
    head_count = lax.axis_size("head")
    group_count = lax.axis_size("group")
    section = lax.axis_index("section")
    ctx = lax.axis_index("ctx")
    head = lax.axis_index("head")
    group = lax.axis_index("group")
    ids = jnp.stack([section, ctx, head, group]).astype(jnp.int32)
    tokens = slice_len // ctx_count
    block_len = cache_keys.shape[2]
    piece = head_dim // section_count
    width = out_weight.shape[2]
    w_local = out_weight.reshape(heads * piece, width)
    out_columns = width // head_count
    pairs = fits_pairs(head_count, group_count, section_count) and (
        piece % 16 == 0 and heads % 2 == 0 and out_columns % (128 * sum(chunk_parts)) == 0
    )

    keys_far = lax.ppermute(cache_keys[0], "ctx", swap)
    values_far = lax.ppermute(cache_values[0], "ctx", swap)
    own_queries = lax.dynamic_slice_in_dim(queries, ctx * tokens, tokens, 0)
    q = jnp.swapaxes(own_queries, 0, 1)
    own = jnp.swapaxes(slice_kv, 0, 1)
    blocks = [own, cache_keys[0], cache_values[0], keys_far, values_far]
    if pairs:
        parts = 2
        pair = [(z, z ^ 1) for z in range(section_count)]
        across = [(z, z ^ 2) for z in range(section_count)]
        widths = [out_columns * w // sum(chunk_parts) for w in chunk_parts]
        bases = [sum(widths[:j]) for j in range(len(widths))]
        half_rows = w_local.shape[0] // 2
        w_pairs = []
        for base, columns in zip(bases, widths):
            cut = lambda at: lax.dynamic_slice(w_local, (group * half_rows, at), (half_rows, columns))
            sent = jnp.stack([cut(base), cut(out_columns + base)])
            through_pair = lax.ppermute(sent, "section", pair)
            w_pairs.append((through_pair, lax.ppermute(through_pair, "group", swap)))
        arrays = blocks
        pieces = []
        for i in range(parts):
            (kept, sent), packed = attend(
                ids, block_table, slice_index, q, arrays, block_len, i * (heads // parts),
                heads // parts, section_count, i == 0,
            )
            if i == 0:
                arrays = packed
            far = lax.ppermute(sent, "section", across)
            kept_twin = lax.ppermute(kept, "ctx", swap)
            far_twin = lax.ppermute(far, "ctx", swap)
            pieces.append((kept, kept_twin, far, far_twin))
        out = []
        for j, (base, columns) in enumerate(zip(bases, widths)):
            kept, sent = project(ids, pieces, w_local, w_pairs[j], base, columns)
            other = lax.ppermute(sent, "head", swap)
            far = lax.ppermute(add_rounded(kept[1], other[1]), "section", across)
            out.append(add_rounded(kept[0], other[0], far))
        return jnp.concatenate(out, axis=1)

    attended = attend(ids, block_table, slice_index, q, blocks, block_len, 0, heads, 1, True)[0][0]
    by_section = attended.reshape(section_count, piece, heads, tokens).transpose(0, 3, 2, 1)
    by_section = by_section.reshape(section_count, tokens, heads * piece)
    by_section = lax.all_gather(by_section, "ctx", axis=1, tiled=True)
    rows = lax.all_to_all(by_section, "section", 0, 0)
    rows = rows.reshape(section_count * slice_len, heads * piece)
    rows = lax.all_gather(rows, "head", axis=1, tiled=True)
    weights = lax.all_to_all(w_local, "head", split_axis=1, concat_axis=0, tiled=True)
    partial = jnp.dot(rows, weights, preferred_element_type=jnp.float32).astype(jnp.bfloat16)
    return lax.psum_scatter(partial, "section", scatter_dimension=0, tiled=True)


def fits_pairs(head_count, group_count, section_count):
    return head_count == 2 and group_count == 2 and section_count == 4


def solution(mesh):
    placed = (
        P(("group", "section"), "head", None),
        P(("group", "section"), None, None),
        P(("group", "section"), "ctx", None, None),
        P(("group", "section"), "ctx", None, None),
        P("group", None),
        P("group"),
        P("head", "section", "ctx"),
    )

    return jax.shard_map(
        on_device,
        mesh=mesh,
        in_specs=placed,
        out_specs=P(("group", "section"), ("ctx", "head")),
        check_vma=False,
    )
```

time: 166 us -> 154 us (0.928)
  starting transfers between devices: 74.9 us -> 35.8 us
  waiting for transfers between devices: 35.5 us -> 67.5 us
  local copies, waits for them, and re-layouts: 13.6 us -> 4.6 us
  other arithmetic: 2.4 us -> 5.8 us
    ppermute x41 -> x22, starting transfers between devices: 74.4 us -> 35.3 us  [the longest x4 12 us: on_device(): through_pair = lax.ppermute(sent, 'section', pair)]
    ppermute x41 -> x22, waiting for transfers between devices: 35.5 us -> 67.5 us  [the longest x4 23.4 us: on_device(): far = lax.ppermute(add_rounded(kept[1], other[1]), 'section', across)]
    dynamic_slice x2 -> x0, local copies, waits for them, and re-layouts: 5.5 us -> none  [the longest x1 3.36 us: on_device(): lax.dynamic_slice_in_dim(w_local, head * out_columns, out_columns, 1)]
    unnamed x76 -> x30, local copies, waits for them, and re-layouts: 5.59 us -> 2.68 us
    squeeze x6 -> x0, local copies, waits for them, and re-layouts: 2.39 us -> none  [the longest x2 0.84 us: line_reduce(): send_up[1]]
    another operation x0 -> x4, other arithmetic: none -> 1.92 us  [on_device(): sent = jnp.stack([cut(base), cut(out_columns + base)])]
    another operation x0 -> x1, local copies, waits for them, and re-layouts: none -> 1.84 us  [on_device(): sent = jnp.stack([cut(base), cut(out_columns + base)])]
  transfers between devices with their start and end apart: 43 -> 24, of which waited for: 16 -> 13; matrix products, arithmetic and copies ran while one was open for 6% -> 6% of each run, Pallas kernels for 21% -> 26%
where the time goes in v2:
time: 154 us; the launch traced here: 153 us
  waiting for transfers between devices  67.5 us (44%)
  Pallas kernels  39.6 us (26%)
  starting transfers between devices  35.8 us (23%)
  other arithmetic  5.8 us (4%)
  local copies, waits for them, and re-layouts  4.6 us (3%)
    ppermute x4, waiting for transfers between devices, on_device(): far = lax.ppermute(add_rounded(kept[1], other[1]), 'section', across)  23.4 us
    pallas_call x4, Pallas kernels, project(): pl.pallas_call(functools.partial(project_kernel, parts=parts), out_shape=...  22.5 us
    ppermute x4, waiting for transfers between devices, on_device(): w_pairs.append((through_pair, lax.ppermute(through_pair, 'group', swap)))  18.2 us
    pallas_call x2, Pallas kernels, attend(): pl.pallas_call(functools.partial(attend_kernel, first=first, pieces=piece...  17.1 us
    ppermute x2, waiting for transfers between devices, on_device(): far = lax.ppermute(sent, 'section', across)  15 us
    ppermute x4, starting transfers between devices, on_device(): through_pair = lax.ppermute(sent, 'section', pair)  12 us
    ppermute x4, starting transfers between devices, on_device(): far = lax.ppermute(add_rounded(kept[1], other[1]), 'section', across)  9.94 us
    ppermute x4, waiting for transfers between devices, on_device(): through_pair = lax.ppermute(sent, 'section', pair)  8.93 us
  transfers between devices with their start and end apart: 24, of which 13 were waited for; matrix products, arithmetic and copies ran while one was open for 6% of the time, Pallas kernels for 26%

profile of v2, /device:TPU:0, one launch (start us, length us, event | category | flops | bytes accessed | tf_op | source)
XLA Modules:
  0.0 153.5 jit_solution(16447122470388511129)
XLA Ops:
  3.3 3.0 %collective-permute-start.12 = (bf16[2,384,384]{2,1,0:T(8,128)(2,1)}, bf16[2,384,384]{2,1,0:T(8,128)(2,1)}, u32[]{:S(2)}, u32[]{:S(2)}) collective-permute-start(bf16[2,384,384]{2,1,0:T(8,128)(2,1)} %pad_maximum_fusion.2), channel_id=1, source_target_pairs={{0,4},{4,0},{8,12},{12,8},{1,5},{5,1},{9,13},{13,9},{2,6},{6,2},{1... | collective-permute-start | bytes 1769480 | tf_op jit(solution)/shard_map/ppermute | solution.py:251
  10.5 9.2 %attend.2 = (bf16[2,384,128]{2,1,0:T(8,128)(2,1)}, bf16[2,384,128]{2,1,0:T(8,128)(2,1)}, bf16[2304,128]{1,0:T(8,128)(2,1)}, bf16[144,2304]{1,0:T(8,128)(2,1)}) custom-call(s32[4]{0:T(128)} %pad_add_fusion.ids_ref, s32[4,16]{1,0:T(4,128)} %table_ref.3, s32[4]{0:T(128)} %index_ref.3, bf16[24,128,128]{2,1,0:T(8,128)(2,1)} %bitcast.62, ...), custom_call_target="tpu_custom_call" | custom-call | tf_op jit(solution)/shard_map/attend/pallas_call | solution.py:119
  19.7 7.9 %attend.3 = (bf16[2,384,128]{2,1,0:T(8,128)(2,1)}, bf16[2,384,128]{2,1,0:T(8,128)(2,1)}) custom-call(s32[4]{0:T(128)} %pad_add_fusion.ids_ref, s32[4,16]{1,0:T(4,128)} %table_ref.3, s32[4]{0:T(128)} %index_ref.3, bf16[24,128,128]{2,1,0:T(8,128)(2,1)} %bitcast.63, bf16[2304,128]{1,0:T(8,128)(2,1)} %get-tuple-element.21.refs_0_, ...), custom_call_target="tpu_custom_call" | custom-call | tf_op jit(solution)/shard_map/attend/pallas_call | solution.py:119
  27.7 5.0 %collective-permute-start.20 = (bf16[2,384,384]{2,1,0:T(8,128)(2,1)S(1)}, bf16[2,384,384]{2,1,0:T(8,128)(2,1)S(1)}, u32[]{:S(2)}, u32[]{:S(2)}) collective-permute-start(bf16[2,384,384]{2,1,0:T(8,128)(2,1)S(1)} %pad_maximum_fusion.4), channel_id=1, source_target_pairs={{0,4},{4,0},{8,12},{12,8},{1,5},{5,1},{9,13},{13,9},{2,6},{6,2},{1... | collective-permute-start | bytes 1769480 | tf_op jit(solution)/shard_map/ppermute | solution.py:251
  32.8 5.5 %collective-permute-done.6.refs_6_ = bf16[2,384,128]{2,1,0:T(8,128)(2,1)S(1)} collective-permute-done((bf16[2,384,128]{2,1,0:T(8,128)(2,1)}, bf16[2,384,128]{2,1,0:T(8,128)(2,1)S(1)}, u32[]{:S(2)}, u32[]{:S(2)}) %collective-permute-start.6) | collective-permute-done | bytes 196640 | tf_op jit(solution)/shard_map/ppermute | solution.py:262
  38.3 2.3 %collective-permute-start.3 = (bf16[2,384,128]{2,1,0:T(8,128)(2,1)S(1)}, bf16[2,384,128]{2,1,0:T(8,128)(2,1)S(1)}, u32[]{:S(2)}, u32[]{:S(2)}) collective-permute-start(bf16[2,384,128]{2,1,0:T(8,128)(2,1)S(1)} %copy-done.13), channel_id=1, source_target_pairs={{0,8},{4,12},{8,0},{12,4},{1,9},{5,13},{9,1},{13,5},{2,10},{6,14},... | collective-permute-start | bytes 589832 | tf_op jit(solution)/shard_map/ppermute | solution.py:262
  40.5 4.0 %collective-permute-start.8 = (bf16[2,384,384]{2,1,0:T(8,128)(2,1)S(1)}, bf16[2,384,384]{2,1,0:T(8,128)(2,1)}, u32[]{:S(2)}, u32[]{:S(2)}) collective-permute-start(bf16[2,384,384]{2,1,0:T(8,128)(2,1)S(1)} %pad_maximum_fusion.1), channel_id=1, source_target_pairs={{0,4},{4,0},{8,12},{12,8},{1,5},{5,1},{9,13},{13,9},{2,6},{6,2},{1... | collective-permute-start | bytes 1769480 | tf_op jit(solution)/shard_map/ppermute | solution.py:251
  44.5 9.5 %collective-permute-done.3.refs_2_ = bf16[2,384,128]{2,1,0:T(8,128)(2,1)S(1)} collective-permute-done((bf16[2,384,128]{2,1,0:T(8,128)(2,1)S(1)}, bf16[2,384,128]{2,1,0:T(8,128)(2,1)S(1)}, u32[]{:S(2)}, u32[]{:S(2)}) %collective-permute-start.3) | collective-permute-done | bytes 196640 | tf_op jit(solution)/shard_map/ppermute | solution.py:262
  57.6 8.9 %collective-permute-done.8.refs_10_ = bf16[2,384,384]{2,1,0:T(8,128)(2,1)} collective-permute-done((bf16[2,384,384]{2,1,0:T(8,128)(2,1)S(1)}, bf16[2,384,384]{2,1,0:T(8,128)(2,1)}, u32[]{:S(2)}, u32[]{:S(2)}) %collective-permute-start.8) | collective-permute-done | bytes 589856 | tf_op jit(solution)/shard_map/ppermute | solution.py:251
  68.3 2.3 %collective-permute-done.13.refs_11_ = bf16[2,384,384]{2,1,0:T(8,128)(2,1)} collective-permute-done((bf16[2,384,384]{2,1,0:T(8,128)(2,1)}, bf16[2,384,384]{2,1,0:T(8,128)(2,1)}, u32[]{:S(2)}, u32[]{:S(2)}) %collective-permute-start.13) | collective-permute-done | bytes 589856 | tf_op jit(solution)/shard_map/ppermute | solution.py:252
  70.6 5.7 %project.5 = (bf16[2,256,384]{2,1,0:T(8,128)(2,1)}, bf16[2,256,384]{2,1,0:T(8,128)(2,1)}) custom-call(s32[4]{0:T(128)} %pad_add_fusion.ids_ref, bf16[2,384,128]{2,1,0:T(8,128)(2,1)} %get-tuple-element.19.refs_0_, bf16[2,384,128]{2,1,0:T(8,128)(2,1)} %copy-done.5, bf16[2,384,128]{2,1,0:T(8,128)(2,1)} %copy-done.4, bf16[2,384,128]{2,1,0:T(8,128)(2,1)} %copy-done.7, ...), custom_call_target="tpu_custom_call" | custom-call | tf_op jit(solution)/shard_map/project/pallas_call | solution.py:180
  77.8 5.4 %collective-permute-done.17.refs_11_ = bf16[2,384,384]{2,1,0:T(8,128)(2,1)} collective-permute-done((bf16[2,384,384]{2,1,0:T(8,128)(2,1)}, bf16[2,384,384]{2,1,0:T(8,128)(2,1)}, u32[]{:S(2)}, u32[]{:S(2)}) %collective-permute-start.17) | collective-permute-done | bytes 589856 | tf_op jit(solution)/shard_map/ppermute | solution.py:252
  83.2 5.6 %project.6 = (bf16[2,256,384]{2,1,0:T(8,128)(2,1)}, bf16[2,256,384]{2,1,0:T(8,128)(2,1)}) custom-call(s32[4]{0:T(128)} %pad_add_fusion.ids_ref, bf16[2,384,128]{2,1,0:T(8,128)(2,1)} %get-tuple-element.19.refs_0_, bf16[2,384,128]{2,1,0:T(8,128)(2,1)} %copy-done.5, bf16[2,384,128]{2,1,0:T(8,128)(2,1)} %copy-done.4, bf16[2,384,128]{2,1,0:T(8,128)(2,1)} %copy-done.7, ...), custom_call_target="tpu_custom_call" | custom-call | tf_op jit(solution)/shard_map/project/pallas_call | solution.py:180
  90.3 5.5 %collective-permute-done.21.refs_11_ = bf16[2,384,384]{2,1,0:T(8,128)(2,1)} collective-permute-done((bf16[2,384,384]{2,1,0:T(8,128)(2,1)S(1)}, bf16[2,384,384]{2,1,0:T(8,128)(2,1)}, u32[]{:S(2)}, u32[]{:S(2)}) %collective-permute-start.21) | collective-permute-done | bytes 589856 | tf_op jit(solution)/shard_map/ppermute | solution.py:252
  95.9 5.6 %project.7 = (bf16[2,256,384]{2,1,0:T(8,128)(2,1)}, bf16[2,256,384]{2,1,0:T(8,128)(2,1)}) custom-call(s32[4]{0:T(128)} %pad_add_fusion.ids_ref, bf16[2,384,128]{2,1,0:T(8,128)(2,1)} %get-tuple-element.19.refs_0_, bf16[2,384,128]{2,1,0:T(8,128)(2,1)} %copy-done.5, bf16[2,384,128]{2,1,0:T(8,128)(2,1)} %copy-done.4, bf16[2,384,128]{2,1,0:T(8,128)(2,1)} %copy-done.7, ...), custom_call_target="tpu_custom_call" | custom-call | tf_op jit(solution)/shard_map/project/pallas_call | solution.py:180
  103.0 4.9 %collective-permute-done.9.refs_11_ = bf16[2,384,384]{2,1,0:T(8,128)(2,1)} collective-permute-done((bf16[2,384,384]{2,1,0:T(8,128)(2,1)}, bf16[2,384,384]{2,1,0:T(8,128)(2,1)}, u32[]{:S(2)}, u32[]{:S(2)}) %collective-permute-start.9) | collective-permute-done | bytes 589856 | tf_op jit(solution)/shard_map/ppermute | solution.py:252
  108.0 5.6 %project.4 = (bf16[2,256,384]{2,1,0:T(8,128)(2,1)}, bf16[2,256,384]{2,1,0:T(8,128)(2,1)}) custom-call(s32[4]{0:T(128)} %pad_add_fusion.ids_ref, bf16[2,384,128]{2,1,0:T(8,128)(2,1)} %get-tuple-element.19.refs_0_, bf16[2,384,128]{2,1,0:T(8,128)(2,1)} %copy-done.5, bf16[2,384,128]{2,1,0:T(8,128)(2,1)} %copy-done.4, bf16[2,384,128]{2,1,0:T(8,128)(2,1)} %copy-done.7, ...), custom_call_target="tpu_custom_call" | custom-call | tf_op jit(solution)/shard_map/project/pallas_call | solution.py:180
  115.1 3.4 %collective-permute-start.15 = (bf16[256,384]{1,0:T(8,128)(2,1)S(1)}, bf16[256,384]{1,0:T(8,128)(2,1)S(1)}, u32[]{:S(2)}, u32[]{:S(2)}) collective-permute-start(bf16[256,384]{1,0:T(8,128)(2,1)S(1)} %fusion.5), channel_id=1, source_target_pairs={{0,8},{4,12},{8,0},{12,4},{1,9},{5,13},{9,1},{13,5},{2,10},{6,14},... | collective-permute-start | bytes 589832 | tf_op jit(solution)/shard_map/ppermute | solution.py:270
  119.7 3.0 %collective-permute-start.23 = (bf16[256,384]{1,0:T(8,128)(2,1)S(1)}, bf16[256,384]{1,0:T(8,128)(2,1)S(1)}, u32[]{:S(2)}, u32[]{:S(2)}) collective-permute-start(bf16[256,384]{1,0:T(8,128)(2,1)S(1)} %fusion.7), channel_id=1, source_target_pairs={{0,8},{4,12},{8,0},{12,4},{1,9},{5,13},{9,1},{13,5},{2,10},{6,14},... | collective-permute-start | bytes 589832 | tf_op jit(solution)/shard_map/ppermute | solution.py:270
  124.5 3.4 %collective-permute-start.11 = (bf16[256,384]{1,0:T(8,128)(2,1)S(1)}, bf16[256,384]{1,0:T(8,128)(2,1)S(1)}, u32[]{:S(2)}, u32[]{:S(2)}) collective-permute-start(bf16[256,384]{1,0:T(8,128)(2,1)S(1)} %fusion.4), channel_id=1, source_target_pairs={{0,8},{4,12},{8,0},{12,4},{1,9},{5,13},{9,1},{13,5},{2,10},{6,14},... | collective-permute-start | bytes 589832 | tf_op jit(solution)/shard_map/ppermute | solution.py:270
  127.9 13.1 %collective-permute-done.15 = bf16[256,384]{1,0:T(8,128)(2,1)S(1)} collective-permute-done((bf16[256,384]{1,0:T(8,128)(2,1)S(1)}, bf16[256,384]{1,0:T(8,128)(2,1)S(1)}, u32[]{:S(2)}, u32[]{:S(2)}) %collective-permute-start.15) | collective-permute-done | bytes 196640 | tf_op jit(solution)/shard_map/ppermute | solution.py:270
  141.1 4.1 %collective-permute-done.19 = bf16[256,384]{1,0:T(8,128)(2,1)S(1)} collective-permute-done((bf16[256,384]{1,0:T(8,128)(2,1)S(1)}, bf16[256,384]{1,0:T(8,128)(2,1)S(1)}, u32[]{:S(2)}, u32[]{:S(2)}) %collective-permute-start.19) | collective-permute-done | bytes 196640 | tf_op jit(solution)/shard_map/ppermute | solution.py:270
  146.2 3.2 %collective-permute-done.23 = bf16[256,384]{1,0:T(8,128)(2,1)S(1)} collective-permute-done((bf16[256,384]{1,0:T(8,128)(2,1)S(1)}, bf16[256,384]{1,0:T(8,128)(2,1)S(1)}, u32[]{:S(2)}, u32[]{:S(2)}) %collective-permute-start.23) | collective-permute-done | bytes 196640 | tf_op jit(solution)/shard_map/ppermute | solution.py:270
  149.5 3.0 %collective-permute-done.11 = bf16[256,384]{1,0:T(8,128)(2,1)S(1)} collective-permute-done((bf16[256,384]{1,0:T(8,128)(2,1)S(1)}, bf16[256,384]{1,0:T(8,128)(2,1)S(1)}, u32[]{:S(2)}, u32[]{:S(2)}) %collective-permute-start.11) | collective-permute-done | bytes 196640 | tf_op jit(solution)/shard_map/ppermute | solution.py:270
  (76 shorter events, 24.3 us)
Async XLA Ops:
  0.0 10.5 %collective-permute-start = (bf16[8,128,128]{2,1,0:T(8,128)(2,1)}, bf16[8,128,128]{2,1,0:T(8,128)(2,1)}, u32[]{:S(2)}, u32[]{:S(2)}) collective-permute-start(bf16[8,128,128]{2,1,0:T(8,128)(2,1)} %bitcast.65), channel_id=1, source_target_pairs={{0,2},{2,0},{1,3},{3,1},{4,6},{6,4},{5,7},{7,5},{8,10},{10,8},{9,1... | collective-permute-start | bytes 786440 | tf_op jit(solution)/shard_map/ppermute | solution.py:234
  0.5 10.0 %collective-permute-start.1 = (bf16[8,128,128]{2,1,0:T(8,128)(2,1)}, bf16[8,128,128]{2,1,0:T(8,128)(2,1)}, u32[]{:S(2)}, u32[]{:S(2)}) collective-permute-start(bf16[8,128,128]{2,1,0:T(8,128)(2,1)} %bitcast.67), channel_id=1, source_target_pairs={{0,2},{2,0},{1,3},{3,1},{4,6},{6,4},{5,7},{7,5},{8,10},{10,8},{9,1... | collective-permute-start | bytes 786440 | tf_op jit(solution)/shard_map/ppermute | solution.py:235
  3.3 50.7 %collective-permute-start.12 = (bf16[2,384,384]{2,1,0:T(8,128)(2,1)}, bf16[2,384,384]{2,1,0:T(8,128)(2,1)}, u32[]{:S(2)}, u32[]{:S(2)}) collective-permute-start(bf16[2,384,384]{2,1,0:T(8,128)(2,1)} %pad_maximum_fusion.2), channel_id=1, source_target_pairs={{0,4},{4,0},{8,12},{12,8},{1,5},{5,1},{9,13},{13,9},{2,6},{6,2},{1... | collective-permute-start | bytes 1769480 | tf_op jit(solution)/shard_map/ppermute | solution.py:251
  7.2 48.4 %collective-permute-start.16 = (bf16[2,384,384]{2,1,0:T(8,128)(2,1)}, bf16[2,384,384]{2,1,0:T(8,128)(2,1)}, u32[]{:S(2)}, u32[]{:S(2)}) collective-permute-start(bf16[2,384,384]{2,1,0:T(8,128)(2,1)} %pad_maximum_fusion.3), channel_id=1, source_target_pairs={{0,4},{4,0},{8,12},{12,8},{1,5},{5,1},{9,13},{13,9},{2,6},{6,2},{1... | collective-permute-start | bytes 1769480 | tf_op jit(solution)/shard_map/ppermute | solution.py:251
  27.6 10.7 %collective-permute-start.6 = (bf16[2,384,128]{2,1,0:T(8,128)(2,1)}, bf16[2,384,128]{2,1,0:T(8,128)(2,1)S(1)}, u32[]{:S(2)}, u32[]{:S(2)}) collective-permute-start(bf16[2,384,128]{2,1,0:T(8,128)(2,1)} %get-tuple-element.24), channel_id=1, source_target_pairs={{0,8},{4,12},{8,0},{12,4},{1,9},{5,13},{9,1},{13,5},{2,10},{6,14},... | collective-permute-start | bytes 589832 | tf_op jit(solution)/shard_map/ppermute | solution.py:262
  27.7 12.9 %collective-permute-start.5 = (bf16[2,384,128]{2,1,0:T(8,128)(2,1)}, bf16[2,384,128]{2,1,0:T(8,128)(2,1)S(1)}, u32[]{:S(2)}, u32[]{:S(2)}) collective-permute-start(bf16[2,384,128]{2,1,0:T(8,128)(2,1)} %get-tuple-element.23.refs_4_), channel_id=1, source_target_pairs={{0,2},{2,0},{1,3},{3,1},{4,6},{6,4},{5,7},{7,5},{8,10},{10,8},{9,1... | collective-permute-start | bytes 589832 | tf_op jit(solution)/shard_map/ppermute | solution.py:263
  27.7 28.8 %collective-permute-start.20 = (bf16[2,384,384]{2,1,0:T(8,128)(2,1)S(1)}, bf16[2,384,384]{2,1,0:T(8,128)(2,1)S(1)}, u32[]{:S(2)}, u32[]{:S(2)}) collective-permute-start(bf16[2,384,384]{2,1,0:T(8,128)(2,1)S(1)} %pad_maximum_fusion.4), channel_id=1, source_target_pairs={{0,4},{4,0},{8,12},{12,8},{1,5},{5,1},{9,13},{13,9},{2,6},{6,2},{1... | collective-permute-start | bytes 1769480 | tf_op jit(solution)/shard_map/ppermute | solution.py:251
  38.3 15.7 %collective-permute-start.3 = (bf16[2,384,128]{2,1,0:T(8,128)(2,1)S(1)}, bf16[2,384,128]{2,1,0:T(8,128)(2,1)S(1)}, u32[]{:S(2)}, u32[]{:S(2)}) collective-permute-start(bf16[2,384,128]{2,1,0:T(8,128)(2,1)S(1)} %copy-done.13), channel_id=1, source_target_pairs={{0,8},{4,12},{8,0},{12,4},{1,9},{5,13},{9,1},{13,5},{2,10},{6,14},... | collective-permute-start | bytes 589832 | tf_op jit(solution)/shard_map/ppermute | solution.py:262
  40.5 26.0 %collective-permute-start.8 = (bf16[2,384,384]{2,1,0:T(8,128)(2,1)S(1)}, bf16[2,384,384]{2,1,0:T(8,128)(2,1)}, u32[]{:S(2)}, u32[]{:S(2)}) collective-permute-start(bf16[2,384,384]{2,1,0:T(8,128)(2,1)S(1)} %pad_maximum_fusion.1), channel_id=1, source_target_pairs={{0,4},{4,0},{8,12},{12,8},{1,5},{5,1},{9,13},{13,9},{2,6},{6,2},{1... | collective-permute-start | bytes 1769480 | tf_op jit(solution)/shard_map/ppermute | solution.py:251
  54.0 1.4 collective-permute-start.2
  54.0 16.6 %collective-permute-start.13 = (bf16[2,384,384]{2,1,0:T(8,128)(2,1)}, bf16[2,384,384]{2,1,0:T(8,128)(2,1)}, u32[]{:S(2)}, u32[]{:S(2)}) collective-permute-start(bf16[2,384,384]{2,1,0:T(8,128)(2,1)} %collective-permute-done.12.refs_10_), channel_id=1, source_target_pairs={{0,16},{16,0},{1,17},{17,1},{2,18},{18,2},{3,19},{19,3},{4,20},{20... | collective-permute-start | bytes 1769480 | tf_op jit(solution)/shard_map/ppermute | solution.py:252
  55.4 11.1 %collective-permute-start.7 = (bf16[2,384,128]{2,1,0:T(8,128)(2,1)S(1)}, bf16[2,384,128]{2,1,0:T(8,128)(2,1)S(1)}, u32[]{:S(2)}, u32[]{:S(2)}) collective-permute-start(bf16[2,384,128]{2,1,0:T(8,128)(2,1)S(1)} %collective-permute-done.6.refs_6_), channel_id=1, source_target_pairs={{0,2},{2,0},{1,3},{3,1},{4,6},{6,4},{5,7},{7,5},{8,10},{10,8},{9,1... | collective-permute-start | bytes 589832 | tf_op jit(solution)/shard_map/ppermute | solution.py:264
  55.6 27.6 %collective-permute-start.17 = (bf16[2,384,384]{2,1,0:T(8,128)(2,1)}, bf16[2,384,384]{2,1,0:T(8,128)(2,1)}, u32[]{:S(2)}, u32[]{:S(2)}) collective-permute-start(bf16[2,384,384]{2,1,0:T(8,128)(2,1)} %collective-permute-done.16.refs_10_), channel_id=1, source_target_pairs={{0,16},{16,0},{1,17},{17,1},{2,18},{18,2},{3,19},{19,3},{4,20},{20... | collective-permute-start | bytes 1769480 | tf_op jit(solution)/shard_map/ppermute | solution.py:252
  56.6 39.3 %collective-permute-start.21 = (bf16[2,384,384]{2,1,0:T(8,128)(2,1)S(1)}, bf16[2,384,384]{2,1,0:T(8,128)(2,1)}, u32[]{:S(2)}, u32[]{:S(2)}) collective-permute-start(bf16[2,384,384]{2,1,0:T(8,128)(2,1)S(1)} %collective-permute-done.20.refs_10_), channel_id=1, source_target_pairs={{0,16},{16,0},{1,17},{17,1},{2,18},{18,2},{3,19},{19,3},{4,20},{20... | collective-permute-start | bytes 1769480 | tf_op jit(solution)/shard_map/ppermute | solution.py:252
  66.5 1.8 %collective-permute-start.4 = (bf16[2,384,128]{2,1,0:T(8,128)(2,1)S(1)}, bf16[2,384,128]{2,1,0:T(8,128)(2,1)S(1)}, u32[]{:S(2)}, u32[]{:S(2)}) collective-permute-start(bf16[2,384,128]{2,1,0:T(8,128)(2,1)S(1)} %collective-permute-done.3.refs_2_), channel_id=1, source_target_pairs={{0,2},{2,0},{1,3},{3,1},{4,6},{6,4},{5,7},{7,5},{8,10},{10,8},{9,1... | collective-permute-start | bytes 589832 | tf_op jit(solution)/shard_map/ppermute | solution.py:264
  66.5 41.4 %collective-permute-start.9 = (bf16[2,384,384]{2,1,0:T(8,128)(2,1)}, bf16[2,384,384]{2,1,0:T(8,128)(2,1)}, u32[]{:S(2)}, u32[]{:S(2)}) collective-permute-start(bf16[2,384,384]{2,1,0:T(8,128)(2,1)} %collective-permute-done.8.refs_10_), channel_id=1, source_target_pairs={{0,16},{16,0},{1,17},{17,1},{2,18},{18,2},{3,19},{19,3},{4,20},{20... | collective-permute-start | bytes 1769480 | tf_op jit(solution)/shard_map/ppermute | solution.py:252
  76.3 38.8 %collective-permute-start.14 = (bf16[2,256,384]{2,1,0:T(8,128)(2,1)}, bf16[2,256,384]{2,1,0:T(8,128)(2,1)S(1)}, u32[]{:S(2)}, u32[]{:S(2)}) collective-permute-start(bf16[2,256,384]{2,1,0:T(8,128)(2,1)} %get-tuple-element.28), channel_id=1, source_target_pairs={{0,1},{1,0},{2,3},{3,2},{4,5},{5,4},{6,7},{7,6},{8,9},{9,8},{10,11... | collective-permute-start | bytes 1179656 | tf_op jit(solution)/shard_map/ppermute | solution.py:269
  88.8 29.8 %collective-permute-start.18 = (bf16[2,256,384]{2,1,0:T(8,128)(2,1)}, bf16[2,256,384]{2,1,0:T(8,128)(2,1)}, u32[]{:S(2)}, u32[]{:S(2)}) collective-permute-start(bf16[2,256,384]{2,1,0:T(8,128)(2,1)} %get-tuple-element.30), channel_id=1, source_target_pairs={{0,1},{1,0},{2,3},{3,2},{4,5},{5,4},{6,7},{7,6},{8,9},{9,8},{10,11... | collective-permute-start | bytes 1179656 | tf_op jit(solution)/shard_map/ppermute | solution.py:269
  101.5 18.2 %collective-permute-start.22 = (bf16[2,256,384]{2,1,0:T(8,128)(2,1)}, bf16[2,256,384]{2,1,0:T(8,128)(2,1)S(1)}, u32[]{:S(2)}, u32[]{:S(2)}) collective-permute-start(bf16[2,256,384]{2,1,0:T(8,128)(2,1)} %get-tuple-element.32), channel_id=1, source_target_pairs={{0,1},{1,0},{2,3},{3,2},{4,5},{5,4},{6,7},{7,6},{8,9},{9,8},{10,11... | collective-permute-start | bytes 1179656 | tf_op jit(solution)/shard_map/ppermute | solution.py:269
  113.6 10.8 %collective-permute-start.10 = (bf16[2,256,384]{2,1,0:T(8,128)(2,1)}, bf16[2,256,384]{2,1,0:T(8,128)(2,1)S(1)}, u32[]{:S(2)}, u32[]{:S(2)}) collective-permute-start(bf16[2,256,384]{2,1,0:T(8,128)(2,1)} %get-tuple-element.26), channel_id=1, source_target_pairs={{0,1},{1,0},{2,3},{3,2},{4,5},{5,4},{6,7},{7,6},{8,9},{9,8},{10,11... | collective-permute-start | bytes 1179656 | tf_op jit(solution)/shard_map/ppermute | solution.py:269
  115.1 25.8 %collective-permute-start.15 = (bf16[256,384]{1,0:T(8,128)(2,1)S(1)}, bf16[256,384]{1,0:T(8,128)(2,1)S(1)}, u32[]{:S(2)}, u32[]{:S(2)}) collective-permute-start(bf16[256,384]{1,0:T(8,128)(2,1)S(1)} %fusion.5), channel_id=1, source_target_pairs={{0,8},{4,12},{8,0},{12,4},{1,9},{5,13},{9,1},{13,5},{2,10},{6,14},... | collective-permute-start | bytes 589832 | tf_op jit(solution)/shard_map/ppermute | solution.py:270
  119.6 25.6 %collective-permute-start.19 = (bf16[256,384]{1,0:T(8,128)(2,1)S(1)}, bf16[256,384]{1,0:T(8,128)(2,1)S(1)}, u32[]{:S(2)}, u32[]{:S(2)}) collective-permute-start(bf16[256,384]{1,0:T(8,128)(2,1)S(1)} %fusion.6), channel_id=1, source_target_pairs={{0,8},{4,12},{8,0},{12,4},{1,9},{5,13},{9,1},{13,5},{2,10},{6,14},... | collective-permute-start | bytes 589832 | tf_op jit(solution)/shard_map/ppermute | solution.py:270
  119.7 29.7 %collective-permute-start.23 = (bf16[256,384]{1,0:T(8,128)(2,1)S(1)}, bf16[256,384]{1,0:T(8,128)(2,1)S(1)}, u32[]{:S(2)}, u32[]{:S(2)}) collective-permute-start(bf16[256,384]{1,0:T(8,128)(2,1)S(1)} %fusion.7), channel_id=1, source_target_pairs={{0,8},{4,12},{8,0},{12,4},{1,9},{5,13},{9,1},{13,5},{2,10},{6,14},... | collective-permute-start | bytes 589832 | tf_op jit(solution)/shard_map/ppermute | solution.py:270
  124.5 28.0 %collective-permute-start.11 = (bf16[256,384]{1,0:T(8,128)(2,1)S(1)}, bf16[256,384]{1,0:T(8,128)(2,1)S(1)}, u32[]{:S(2)}, u32[]{:S(2)}) collective-permute-start(bf16[256,384]{1,0:T(8,128)(2,1)S(1)} %fusion.4), channel_id=1, source_target_pairs={{0,8},{4,12},{8,0},{12,4},{1,9},{5,13},{9,1},{13,5},{2,10},{6,14},... | collective-permute-start | bytes 589832 | tf_op jit(solution)/shard_map/ppermute | solution.py:270
  (14 other events, 224.3 us)

commit v3 on v2

--- a/solution.py
+++ b/solution.py
@@ -35,8 +35,8 @@
 
     if first:
         local_pool = kl_ref.shape[0]
-        k_s[:slice_len, :] = own_ref[0]
-        vt_s[:head_dim, :slice_len] = own_ref[1].T
+        k_s[:slice_len, :] = own_ref[:, 0, :]
+        vt_s[:head_dim, :slice_len] = own_ref[:, 1, :].T
         vt_s[head_dim:, :] = jnp.ones((vt_s.shape[0] - head_dim, vt_s.shape[1]), vt_s.dtype)
 
         @pl.loop(0, steps * BPS)
@@ -102,7 +102,7 @@
     whole = lambda a: pl.BlockSpec(a.shape, lambda g, *_: (0,) * a.ndim)
     pool = block_table.shape[1]
     if first:
-        keys = arrays[0].shape[1] + pool * arrays[1].shape[1]
+        keys = arrays[0].shape[0] + pool * arrays[1].shape[1]
         packed = [
             jax.ShapeDtypeStruct((keys, head_dim), jnp.bfloat16),
             jax.ShapeDtypeStruct((head_dim + 16, keys), jnp.bfloat16),
@@ -136,50 +136,86 @@
     return list(outs[: len(out_shape)]), list(outs[len(out_shape) :])
 
 
-def project_kernel(ids_ref, *refs, parts):
-    a_refs = refs[: 4 * parts]
-    w_refs = refs[4 * parts : 4 * parts + 4]
-    w_pairs = refs[4 * parts + 2 : 4 * parts + 4]
-    kept, sent, a_s, w_s = refs[4 * parts + 4 :]
-    rows, tokens = a_refs[0].shape[1:]
-    columns = kept.shape[2]
+def cut_kernel(ids_ref, w_ref, out_ref):
+    out_ref[0] = w_ref[...]
+
+
+def cut(ids, w_local, base, columns):
+    rows = w_local.shape[0] // 2
+    half = w_local.shape[1] // 2
+    return pl.pallas_call(
+        cut_kernel,
+        out_shape=jax.ShapeDtypeStruct((2, rows, columns), jnp.bfloat16),
+        grid_spec=pltpu.PrefetchScalarGridSpec(
+            num_scalar_prefetch=1,
+            grid=(2,),
+            in_specs=[
+                pl.BlockSpec(
+                    (pl.Element(rows), pl.Element(columns)),
+                    lambda n, ids: (
+                        pl.multiple_of(ids[3] * rows, 16),
+                        pl.multiple_of(n * half + base, 128),
+                    ),
+                )
+            ],
+            out_specs=pl.BlockSpec((1, rows, columns), lambda n, ids: (n, 0, 0)),
+        ),
+        name="cut",
+    )(ids, w_local)
+
+
+def project_kernel(ids_ref, *refs, inputs, first):
+    w_refs = refs[inputs : inputs + 2]
+    w_pairs = refs[inputs + 2 : inputs + 4]
+    kept, sent = refs[inputs + 4 : inputs + 6]
+    w_s = refs[-1]
+    half = kept.shape[1]
     ctx, head, group = ids_ref[1], ids_ref[2], ids_ref[3]
-    local_rows = parts * rows
-    for i in range(parts):
-        place = local_rows + lax.rem(i + group, parts) * rows
-        place = pl.ds(pl.multiple_of(place, rows), rows)
-        for which in range(4):
-            core = ctx if which % 2 == 0 else 1 - ctx
-            at = pl.multiple_of((which // 2 * 2 + core) * tokens, tokens)
-            at = pl.ds(at, tokens)
-            a_s[at, i * rows : (i + 1) * rows] = a_refs[4 * i + which][0].T
-            a_s[at, place] = a_refs[4 * i + which][1].T
-    for side in range(2):
-        at = slice(side * columns, (side + 1) * columns)
-        w_s[:local_rows, at] = w_refs[side][...]
-        half = head if side == 0 else 1 - head
+    local_rows = w_refs[0].shape[0]
+    if first:
+        a_s = refs[inputs + 6]
+        parts = inputs // 4
+        rows, tokens = refs[0].shape[1:]
+        for i in range(parts):
+            place = local_rows + lax.rem(i + group, parts) * rows
+            place = pl.ds(pl.multiple_of(place, rows), rows)
+            for which in range(4):
+                core = ctx if which % 2 == 0 else 1 - ctx
+                at = pl.multiple_of((which // 2 * 2 + core) * tokens, tokens)
+                at = pl.ds(at, tokens)
+                a_s[at, i * rows : (i + 1) * rows] = refs[4 * i + which][0].T
+                a_s[at, place] = refs[4 * i + which][1].T
+    else:
+        a_s = refs[0]
+    pair_rows = w_pairs[0].shape[1]
+    for side, out_ref in ((1, sent), (0, kept)):
+        which = head if side == 0 else 1 - head
         for j in range(2):
-            w_s[local_rows + j * rows : local_rows + (j + 1) * rows, at] = w_pairs[j][half]
-    out = jnp.dot(a_s[...], w_s[...], preferred_element_type=jnp.float32).astype(jnp.bfloat16)
-    for k in range(2):
-        at = slice(2 * k * tokens, 2 * (k + 1) * tokens)
-        sent[k] = out[at, columns:]
-        kept[k] = out[at, :columns]
-
-
-def project(ids, pieces, w_local, w_pairs, base, columns):
-    parts = len(pieces)
-    rows, tokens = pieces[0][0].shape[1:]
-    flat = [a for four in pieces for a in four]
+            w_s[j * pair_rows : (j + 1) * pair_rows, :] = w_pairs[j][which]
+        out = jnp.dot(
+            a_s[:, :local_rows], w_refs[side][...], preferred_element_type=jnp.float32
+        ) + jnp.dot(a_s[:, local_rows:], w_s[...], preferred_element_type=jnp.float32)
+        for k in range(2):
+            out_ref[k] = out[k * half : (k + 1) * half].astype(jnp.bfloat16)
+
+
+def project(ids, flat, w_local, w_pairs, base, columns, first):
     half = w_local.shape[1] // 2
     whole = lambda a: pl.BlockSpec(a.shape, lambda n, ids: (0,) * a.ndim)
     element = lambda f: pl.BlockSpec(
         (pl.Element(w_local.shape[0]), pl.Element(columns)), lambda n, ids: (0, f(ids))
     )
-    shape = jax.ShapeDtypeStruct((2, 2 * tokens, columns), jnp.bfloat16)
+    if first:
+        rows = 4 * flat[0].shape[2]
+        depth = w_local.shape[0] + 2 * w_pairs[0].shape[1]
+        made = [jax.ShapeDtypeStruct((rows, depth), jnp.bfloat16)]
+    else:
+        rows = flat[0].shape[0]
+        made = []
+    shape = jax.ShapeDtypeStruct((2, rows // 2, columns), jnp.bfloat16)
     return pl.pallas_call(
-        functools.partial(project_kernel, parts=parts),
-        out_shape=[shape, shape],
+        functools.partial(project_kernel, inputs=len(flat), first=first),
+        out_shape=[shape, shape] + made,
         grid_spec=pltpu.PrefetchScalarGridSpec(
             num_scalar_prefetch=1,
             grid=(1,),
@@ -189,11 +225,8 @@
                 element(lambda ids: pl.multiple_of((1 - ids[2]) * half + base, 128)),
             ]
             + [whole(w) for w in w_pairs],
-            out_specs=[whole(shape), whole(shape)],
-            scratch_shapes=[
-                pltpu.VMEM((4 * tokens, 2 * parts * rows), jnp.bfloat16),
-                pltpu.VMEM((2 * parts * rows, 2 * columns), jnp.bfloat16),
-            ],
+            out_specs=[whole(a) for a in [shape, shape] + made],
+            scratch_shapes=[pltpu.VMEM((2 * w_pairs[0].shape[1], columns), jnp.bfloat16)],
         ),
         compiler_params=pltpu.CompilerParams(dimension_semantics=("arbitrary",)),
         name="project",
@@ -235,19 +268,16 @@
     values_far = lax.ppermute(cache_values[0], "ctx", swap)
     own_queries = lax.dynamic_slice_in_dim(queries, ctx * tokens, tokens, 0)
     q = jnp.swapaxes(own_queries, 0, 1)
-    own = jnp.swapaxes(slice_kv, 0, 1)
-    blocks = [own, cache_keys[0], cache_values[0], keys_far, values_far]
+    blocks = [slice_kv, cache_keys[0], cache_values[0], keys_far, values_far]
     if pairs:
         parts = 2
         pair = [(z, z ^ 1) for z in range(section_count)]
         across = [(z, z ^ 2) for z in range(section_count)]
         widths = [out_columns * w // sum(chunk_parts) for w in chunk_parts]
         bases = [sum(widths[:j]) for j in range(len(widths))]
-        half_rows = w_local.shape[0] // 2
         w_pairs = []
         for base, columns in zip(bases, widths):
-            cut = lambda at: lax.dynamic_slice(w_local, (group * half_rows, at), (half_rows, columns))
-            sent = jnp.stack([cut(base), cut(out_columns + base)])
+            sent = cut(ids, w_local, base, columns)
             through_pair = lax.ppermute(sent, "section", pair)
             w_pairs.append((through_pair, lax.ppermute(through_pair, "group", swap)))
         arrays = blocks
@@ -262,10 +292,11 @@
             far = lax.ppermute(sent, "section", across)
             kept_twin = lax.ppermute(kept, "ctx", swap)
             far_twin = lax.ppermute(far, "ctx", swap)
-            pieces.append((kept, kept_twin, far, far_twin))
+            pieces += [kept, kept_twin, far, far_twin]
         out = []
         for j, (base, columns) in enumerate(zip(bases, widths)):
-            kept, sent = project(ids, pieces, w_local, w_pairs[j], base, columns)
+            kept, sent, *made = project(ids, pieces, w_local, w_pairs[j], base, columns, j == 0)
+            pieces = made or pieces
             other = lax.ppermute(sent, "head", swap)
             far = lax.ppermute(add_rounded(kept[1], other[1]), "section", across)
             out.append(add_rounded(kept[0], other[0], far))

time: 154 us -> 166 us (1.078)
  Pallas kernels: 39.6 us -> 49.4 us
  local copies, waits for them, and re-layouts: 4.6 us -> 2.68 us
  other arithmetic: 5.8 us -> 7.66 us
    pallas_call x4 -> x8, Pallas kernels: 22.5 us -> 32 us  [the longest x4 21.9 us: project(): pl.pallas_call(functools.partial(project_kernel, inputs=len(flat), first=...]
    ppermute x2, waiting for transfers between devices: 15 us -> 22.4 us  [on_device(): far = lax.ppermute(sent, 'section', across)]
    ppermute x4, starting transfers between devices: 4.85 us -> 11 us  [on_device(): w_pairs.append((through_pair, lax.ppermute(through_pair, 'group', swap)))]
    ppermute x4, starting transfers between devices: 12 us -> 7.9 us  [on_device(): through_pair = lax.ppermute(sent, 'section', pair)]
    convert_element_type x8, other arithmetic: 2.36 us -> 6.07 us  [add_rounded(): return total.astype(jnp.bfloat16)]
    ppermute x4, waiting for transfers between devices: 18.2 us -> 15.9 us  [on_device(): w_pairs.append((through_pair, lax.ppermute(through_pair, 'group', swap)))]
    another operation x4 -> x0, other arithmetic: 1.92 us -> none  [on_device(): sent = jnp.stack([cut(base), cut(out_columns + base)])]
    another operation x1 -> x0, local copies, waits for them, and re-layouts: 1.84 us -> none  [on_device(): sent = jnp.stack([cut(base), cut(out_columns + base)])]
  transfers between devices with their start and end apart: 24 -> 24, of which waited for: 13 -> 11; matrix products, arithmetic and copies ran while one was open for 6% -> 5% of each run, Pallas kernels for 26% -> 30%
where the time goes in v3:
time: 166 us; the launch traced here: 165 us
  waiting for transfers between devices  68.5 us (41%)
  Pallas kernels  49.4 us (30%)
  starting transfers between devices  37 us (22%)
  other arithmetic  7.66 us (5%)
  local copies, waits for them, and re-layouts  2.68 us (2%)
    ppermute x4, waiting for transfers between devices, on_device(): far = lax.ppermute(add_rounded(kept[1], other[1]), 'section', across)  22.4 us
    ppermute x2, waiting for transfers between devices, on_device(): far = lax.ppermute(sent, 'section', across)  22.4 us
    pallas_call x4, Pallas kernels, project(): pl.pallas_call(functools.partial(project_kernel, inputs=len(flat), first=...  21.9 us
    pallas_call x2, Pallas kernels, attend(): pl.pallas_call(functools.partial(attend_kernel, first=first, pieces=piece...  17.4 us
    ppermute x4, waiting for transfers between devices, on_device(): w_pairs.append((through_pair, lax.ppermute(through_pair, 'group', swap)))  15.9 us
    ppermute x4, starting transfers between devices, on_device(): w_pairs.append((through_pair, lax.ppermute(through_pair, 'group', swap)))  11 us
    pallas_call x4, Pallas kernels, cut(): pl.pallas_call(cut_kernel, out_shape=jax.ShapeDtypeStruct((2, rows, colum...  10.1 us
    ppermute x4, starting transfers between devices, on_device(): far = lax.ppermute(add_rounded(kept[1], other[1]), 'section', across)  9.73 us
  transfers between devices with their start and end apart: 24, of which 11 were waited for; matrix products, arithmetic and copies ran while one was open for 5% of the time, Pallas kernels for 30%

profile of v3, /device:TPU:0, one launch (start us, length us, event | category | flops | bytes accessed | tf_op | source)
XLA Modules:
  0.0 165.3 jit_solution(15390547539962488326)
XLA Ops:
  1.2 2.5 %cut.4 = bf16[2,384,384]{2,1,0:T(8,128)(2,1)} custom-call(s32[4]{0:T(128)} %pad_add_fusion.ids_ref, bf16[768,3072]{1,0:T(8,128)(2,1)} %bitcast.34), custom_call_target="tpu_custom_call" | custom-call | tf_op jit(solution)/shard_map/cut/pallas_call | solution.py:146
  3.7 3.0 %collective-permute-start.8 = (bf16[2,384,384]{2,1,0:T(8,128)(2,1)}, bf16[2,384,384]{2,1,0:T(8,128)(2,1)S(1)}, u32[]{:S(2)}, u32[]{:S(2)}) collective-permute-start(bf16[2,384,384]{2,1,0:T(8,128)(2,1)} %cut.4), channel_id=1, source_target_pairs={{0,4},{4,0},{8,12},{12,8},{1,5},{5,1},{9,13},{13,9},{2,6},{6,2},{1... | collective-permute-start | bytes 1769480 | tf_op jit(solution)/shard_map/ppermute | solution.py:281
  8.7 9.5 %attend.2 = (bf16[2,384,128]{2,1,0:T(8,128)(2,1)}, bf16[2,384,128]{2,1,0:T(8,128)(2,1)}, bf16[2304,128]{1,0:T(8,128)(2,1)}, bf16[144,2304]{1,0:T(8,128)(2,1)}) custom-call(s32[4]{0:T(128)} %pad_add_fusion.ids_ref, s32[4,16]{1,0:T(4,128)} %table_ref.3, s32[4]{0:T(128)} %index_ref.3, bf16[24,128,128]{2,1,0:T(8,128)(2,1)} %bitcast.46, ...), custom_call_target="tpu_custom_call" | custom-call | tf_op jit(solution)/shard_map/attend/pallas_call | solution.py:119
  18.2 7.9 %attend.3 = (bf16[2,384,128]{2,1,0:T(8,128)(2,1)}, bf16[2,384,128]{2,1,0:T(8,128)(2,1)}) custom-call(s32[4]{0:T(128)} %pad_add_fusion.ids_ref, s32[4,16]{1,0:T(4,128)} %table_ref.3, s32[4]{0:T(128)} %index_ref.3, bf16[24,128,128]{2,1,0:T(8,128)(2,1)} %bitcast.47, bf16[2304,128]{1,0:T(8,128)(2,1)} %get-tuple-element.22.refs_0_, ...), custom_call_target="tpu_custom_call" | custom-call | tf_op jit(solution)/shard_map/attend/pallas_call | solution.py:119
  28.6 3.0 %collective-permute-start.12 = (bf16[2,384,384]{2,1,0:T(8,128)(2,1)}, bf16[2,384,384]{2,1,0:T(8,128)(2,1)}, u32[]{:S(2)}, u32[]{:S(2)}) collective-permute-start(bf16[2,384,384]{2,1,0:T(8,128)(2,1)} %cut.5), channel_id=1, source_target_pairs={{0,4},{4,0},{8,12},{12,8},{1,5},{5,1},{9,13},{13,9},{2,6},{6,2},{1... | collective-permute-start | bytes 1769480 | tf_op jit(solution)/shard_map/ppermute | solution.py:281
  31.6 2.5 %cut.6 = bf16[2,384,384]{2,1,0:T(8,128)(2,1)} custom-call(s32[4]{0:T(128)} %pad_add_fusion.ids_ref, bf16[768,3072]{1,0:T(8,128)(2,1)} %bitcast.36), custom_call_target="tpu_custom_call" | custom-call | tf_op jit(solution)/shard_map/cut/pallas_call | solution.py:146
  34.1 2.6 %cut.7 = bf16[2,384,384]{2,1,0:T(8,128)(2,1)} custom-call(s32[4]{0:T(128)} %pad_add_fusion.ids_ref, bf16[768,3072]{1,0:T(8,128)(2,1)} %bitcast.37), custom_call_target="tpu_custom_call" | custom-call | tf_op jit(solution)/shard_map/cut/pallas_call | solution.py:146
  41.5 21.0 %collective-permute-done.3.refs_2_ = bf16[2,384,128]{2,1,0:T(8,128)(2,1)S(1)} collective-permute-done((bf16[2,384,128]{2,1,0:T(8,128)(2,1)}, bf16[2,384,128]{2,1,0:T(8,128)(2,1)S(1)}, u32[]{:S(2)}, u32[]{:S(2)}) %collective-permute-start.3) | collective-permute-done | bytes 196640 | tf_op jit(solution)/shard_map/ppermute | solution.py:292
  62.5 4.6 %collective-permute-start.9 = (bf16[2,384,384]{2,1,0:T(8,128)(2,1)S(1)}, bf16[2,384,384]{2,1,0:T(8,128)(2,1)}, u32[]{:S(2)}, u32[]{:S(2)}) collective-permute-start(bf16[2,384,384]{2,1,0:T(8,128)(2,1)S(1)} %collective-permute-done.8.refs_10_), channel_id=1, source_target_pairs={{0,16},{16,0},{1,17},{17,1},{2,18},{18,2},{3,19},{19,3},{4,20},{20... | collective-permute-start | bytes 1769480 | tf_op jit(solution)/shard_map/ppermute | solution.py:282
  69.2 7.4 %collective-permute-done.20.refs_3_ = bf16[2,384,384]{2,1,0:T(8,128)(2,1)S(1)} collective-permute-done((bf16[2,384,384]{2,1,0:T(8,128)(2,1)}, bf16[2,384,384]{2,1,0:T(8,128)(2,1)S(1)}, u32[]{:S(2)}, u32[]{:S(2)}) %collective-permute-start.20) | collective-permute-done | bytes 589856 | tf_op jit(solution)/shard_map/ppermute | solution.py:281
  76.7 4.5 %collective-permute-start.21 = (bf16[2,384,384]{2,1,0:T(8,128)(2,1)S(1)}, bf16[2,384,384]{2,1,0:T(8,128)(2,1)}, u32[]{:S(2)}, u32[]{:S(2)}) collective-permute-start(bf16[2,384,384]{2,1,0:T(8,128)(2,1)S(1)} %collective-permute-done.20.refs_3_), channel_id=1, source_target_pairs={{0,16},{16,0},{1,17},{17,1},{2,18},{18,2},{3,19},{19,3},{4,20},{20... | collective-permute-start | bytes 1769480 | tf_op jit(solution)/shard_map/ppermute | solution.py:282
  81.9 5.9 %project.4 = (bf16[2,256,384]{2,1,0:T(8,128)(2,1)}, bf16[2,256,384]{2,1,0:T(8,128)(2,1)}, bf16[512,1536]{1,0:T(8,128)(2,1)}) custom-call(s32[4]{0:T(128)} %pad_add_fusion.ids_ref, bf16[2,384,128]{2,1,0:T(8,128)(2,1)} %get-tuple-element.20.refs_0_, bf16[2,384,128]{2,1,0:T(8,128)(2,1)} %copy-done.13, bf16[2,384,128]{2,1,0:T(8,128)(2,1)} %copy-done.12, ...), custom_call_target="tpu_custom_call" | custom-call | tf_op jit(solution)/shard_map/project/pallas_call | solution.py:216
  89.4 4.6 %collective-permute-done.13.refs_4_ = bf16[2,384,384]{2,1,0:T(8,128)(2,1)} collective-permute-done((bf16[2,384,384]{2,1,0:T(8,128)(2,1)}, bf16[2,384,384]{2,1,0:T(8,128)(2,1)}, u32[]{:S(2)}, u32[]{:S(2)}) %collective-permute-start.13) | collective-permute-done | bytes 589856 | tf_op jit(solution)/shard_map/ppermute | solution.py:282
  94.0 5.3 %project.5 = (bf16[2,256,384]{2,1,0:T(8,128)(2,1)}, bf16[2,256,384]{2,1,0:T(8,128)(2,1)}) custom-call(s32[4]{0:T(128)} %pad_add_fusion.ids_ref, bf16[512,1536]{1,0:T(8,128)(2,1)} %get-tuple-element.28.refs_0_, bf16[768,3072]{1,0:T(8,128)(2,1)} %bitcast.40, bf16[768,3072]{1,0:T(8,128)(2,1)} %bitcast.41, bf16[2,384,384]{2,1,0:T(8,128)(2,1)} %collective-permute-done.12.refs_3_, ...), custom_call_target="tpu_custom_call" | custom-call | tf_op jit(solution)/shard_map/project/pallas_call | solution.py:216
  100.8 5.8 %collective-permute-done.17.refs_4_ = bf16[2,384,384]{2,1,0:T(8,128)(2,1)} collective-permute-done((bf16[2,384,384]{2,1,0:T(8,128)(2,1)S(1)}, bf16[2,384,384]{2,1,0:T(8,128)(2,1)}, u32[]{:S(2)}, u32[]{:S(2)}) %collective-permute-start.17) | collective-permute-done | bytes 589856 | tf_op jit(solution)/shard_map/ppermute | solution.py:282
  106.6 5.3 %project.6 = (bf16[2,256,384]{2,1,0:T(8,128)(2,1)}, bf16[2,256,384]{2,1,0:T(8,128)(2,1)}) custom-call(s32[4]{0:T(128)} %pad_add_fusion.ids_ref, bf16[512,1536]{1,0:T(8,128)(2,1)} %get-tuple-element.28.refs_0_, bf16[768,3072]{1,0:T(8,128)(2,1)} %bitcast.42, bf16[768,3072]{1,0:T(8,128)(2,1)} %bitcast.43, bf16[2,384,384]{2,1,0:T(8,128)(2,1)} %copy-done.2, ...), custom_call_target="tpu_custom_call" | custom-call | tf_op jit(solution)/shard_map/project/pallas_call | solution.py:216
  113.5 5.5 %collective-permute-done.21.refs_4_ = bf16[2,384,384]{2,1,0:T(8,128)(2,1)} collective-permute-done((bf16[2,384,384]{2,1,0:T(8,128)(2,1)S(1)}, bf16[2,384,384]{2,1,0:T(8,128)(2,1)}, u32[]{:S(2)}, u32[]{:S(2)}) %collective-permute-start.21) | collective-permute-done | bytes 589856 | tf_op jit(solution)/shard_map/ppermute | solution.py:282
  119.0 5.3 %project.7 = (bf16[2,256,384]{2,1,0:T(8,128)(2,1)}, bf16[2,256,384]{2,1,0:T(8,128)(2,1)}) custom-call(s32[4]{0:T(128)} %pad_add_fusion.ids_ref, bf16[512,1536]{1,0:T(8,128)(2,1)} %get-tuple-element.28.refs_0_, bf16[768,3072]{1,0:T(8,128)(2,1)} %bitcast.44, bf16[768,3072]{1,0:T(8,128)(2,1)} %bitcast.45, bf16[2,384,384]{2,1,0:T(8,128)(2,1)} %copy-done.3, ...), custom_call_target="tpu_custom_call" | custom-call | tf_op jit(solution)/shard_map/project/pallas_call | solution.py:216
  126.8 3.3 %collective-permute-start.11 = (bf16[256,384]{1,0:T(8,128)(2,1)S(1)}, bf16[256,384]{1,0:T(8,128)(2,1)S(1)}, u32[]{:S(2)}, u32[]{:S(2)}) collective-permute-start(bf16[256,384]{1,0:T(8,128)(2,1)S(1)} %fusion.4), channel_id=1, source_target_pairs={{0,8},{4,12},{8,0},{12,4},{1,9},{5,13},{9,1},{13,5},{2,10},{6,14},... | collective-permute-start | bytes 589832 | tf_op jit(solution)/shard_map/ppermute | solution.py:301
  132.2 3.0 %collective-permute-start.19 = (bf16[256,384]{1,0:T(8,128)(2,1)S(1)}, bf16[256,384]{1,0:T(8,128)(2,1)S(1)}, u32[]{:S(2)}, u32[]{:S(2)}) collective-permute-start(bf16[256,384]{1,0:T(8,128)(2,1)S(1)} %fusion.6), channel_id=1, source_target_pairs={{0,8},{4,12},{8,0},{12,4},{1,9},{5,13},{9,1},{13,5},{2,10},{6,14},... | collective-permute-start | bytes 589832 | tf_op jit(solution)/shard_map/ppermute | solution.py:301
  135.5 3.3 %collective-permute-start.23 = (bf16[256,384]{1,0:T(8,128)(2,1)S(1)}, bf16[256,384]{1,0:T(8,128)(2,1)S(1)}, u32[]{:S(2)}, u32[]{:S(2)}) collective-permute-start(bf16[256,384]{1,0:T(8,128)(2,1)S(1)} %fusion.7), channel_id=1, source_target_pairs={{0,8},{4,12},{8,0},{12,4},{1,9},{5,13},{9,1},{13,5},{2,10},{6,14},... | collective-permute-start | bytes 589832 | tf_op jit(solution)/shard_map/ppermute | solution.py:301
  138.8 13.7 %collective-permute-done.11 = bf16[256,384]{1,0:T(8,128)(2,1)S(1)} collective-permute-done((bf16[256,384]{1,0:T(8,128)(2,1)S(1)}, bf16[256,384]{1,0:T(8,128)(2,1)S(1)}, u32[]{:S(2)}, u32[]{:S(2)}) %collective-permute-start.11) | collective-permute-done | bytes 196640 | tf_op jit(solution)/shard_map/ppermute | solution.py:301
  153.5 3.2 %collective-permute-done.15 = bf16[256,384]{1,0:T(8,128)(2,1)S(1)} collective-permute-done((bf16[256,384]{1,0:T(8,128)(2,1)S(1)}, bf16[256,384]{1,0:T(8,128)(2,1)S(1)}, u32[]{:S(2)}, u32[]{:S(2)}) %collective-permute-start.15) | collective-permute-done | bytes 196640 | tf_op jit(solution)/shard_map/ppermute | solution.py:301
  157.8 3.2 %collective-permute-done.19 = bf16[256,384]{1,0:T(8,128)(2,1)S(1)} collective-permute-done((bf16[256,384]{1,0:T(8,128)(2,1)S(1)}, bf16[256,384]{1,0:T(8,128)(2,1)S(1)}, u32[]{:S(2)}, u32[]{:S(2)}) %collective-permute-start.19) | collective-permute-done | bytes 196640 | tf_op jit(solution)/shard_map/ppermute | solution.py:301
  (78 shorter events, 29.1 us)
Async XLA Ops:
  0.0 7.9 %collective-permute-start = (bf16[8,128,128]{2,1,0:T(8,128)(2,1)}, bf16[8,128,128]{2,1,0:T(8,128)(2,1)S(1)}, u32[]{:S(2)}, u32[]{:S(2)}) collective-permute-start(bf16[8,128,128]{2,1,0:T(8,128)(2,1)} %bitcast.48), channel_id=1, source_target_pairs={{0,2},{2,0},{1,3},{3,1},{4,6},{6,4},{5,7},{7,5},{8,10},{10,8},{9,1... | collective-permute-start | bytes 786440 | tf_op jit(solution)/shard_map/ppermute | solution.py:267
  0.5 7.4 %collective-permute-start.1 = (bf16[8,128,128]{2,1,0:T(8,128)(2,1)}, bf16[8,128,128]{2,1,0:T(8,128)(2,1)S(1)}, u32[]{:S(2)}, u32[]{:S(2)}) collective-permute-start(bf16[8,128,128]{2,1,0:T(8,128)(2,1)} %bitcast.50), channel_id=1, source_target_pairs={{0,2},{2,0},{1,3},{3,1},{4,6},{6,4},{5,7},{7,5},{8,10},{10,8},{9,1... | collective-permute-start | bytes 786440 | tf_op jit(solution)/shard_map/ppermute | solution.py:268
  3.7 58.8 %collective-permute-start.8 = (bf16[2,384,384]{2,1,0:T(8,128)(2,1)}, bf16[2,384,384]{2,1,0:T(8,128)(2,1)S(1)}, u32[]{:S(2)}, u32[]{:S(2)}) collective-permute-start(bf16[2,384,384]{2,1,0:T(8,128)(2,1)} %cut.4), channel_id=1, source_target_pairs={{0,4},{4,0},{8,12},{12,8},{1,5},{5,1},{9,13},{13,9},{2,6},{6,2},{1... | collective-permute-start | bytes 1769480 | tf_op jit(solution)/shard_map/ppermute | solution.py:281
  26.1 12.0 %collective-permute-start.6 = (bf16[2,384,128]{2,1,0:T(8,128)(2,1)}, bf16[2,384,128]{2,1,0:T(8,128)(2,1)S(1)}, u32[]{:S(2)}, u32[]{:S(2)}) collective-permute-start(bf16[2,384,128]{2,1,0:T(8,128)(2,1)} %get-tuple-element.25), channel_id=1, source_target_pairs={{0,8},{4,12},{8,0},{12,4},{1,9},{5,13},{9,1},{13,5},{2,10},{6,14},... | collective-permute-start | bytes 589832 | tf_op jit(solution)/shard_map/ppermute | solution.py:292
  26.1 13.5 %collective-permute-start.5 = (bf16[2,384,128]{2,1,0:T(8,128)(2,1)}, bf16[2,384,128]{2,1,0:T(8,128)(2,1)}, u32[]{:S(2)}, u32[]{:S(2)}) collective-permute-start(bf16[2,384,128]{2,1,0:T(8,128)(2,1)} %get-tuple-element.24.refs_4_), channel_id=1, source_target_pairs={{0,2},{2,0},{1,3},{3,1},{4,6},{6,4},{5,7},{7,5},{8,10},{10,8},{9,1... | collective-permute-start | bytes 589832 | tf_op jit(solution)/shard_map/ppermute | solution.py:293
  28.6 38.6 %collective-permute-start.12 = (bf16[2,384,384]{2,1,0:T(8,128)(2,1)}, bf16[2,384,384]{2,1,0:T(8,128)(2,1)}, u32[]{:S(2)}, u32[]{:S(2)}) collective-permute-start(bf16[2,384,384]{2,1,0:T(8,128)(2,1)} %cut.5), channel_id=1, source_target_pairs={{0,4},{4,0},{8,12},{12,8},{1,5},{5,1},{9,13},{13,9},{2,6},{6,2},{1... | collective-permute-start | bytes 1769480 | tf_op jit(solution)/shard_map/ppermute | solution.py:281
  34.1 34.5 %collective-permute-start.16 = (bf16[2,384,384]{2,1,0:T(8,128)(2,1)}, bf16[2,384,384]{2,1,0:T(8,128)(2,1)S(1)}, u32[]{:S(2)}, u32[]{:S(2)}) collective-permute-start(bf16[2,384,384]{2,1,0:T(8,128)(2,1)} %cut.6), channel_id=1, source_target_pairs={{0,4},{4,0},{8,12},{12,8},{1,5},{5,1},{9,13},{13,9},{2,6},{6,2},{1... | collective-permute-start | bytes 1769480 | tf_op jit(solution)/shard_map/ppermute | solution.py:281
  38.1 24.4 %collective-permute-start.3 = (bf16[2,384,128]{2,1,0:T(8,128)(2,1)}, bf16[2,384,128]{2,1,0:T(8,128)(2,1)S(1)}, u32[]{:S(2)}, u32[]{:S(2)}) collective-permute-start(bf16[2,384,128]{2,1,0:T(8,128)(2,1)} %get-tuple-element.21), channel_id=1, source_target_pairs={{0,8},{4,12},{8,0},{12,4},{1,9},{5,13},{9,1},{13,5},{2,10},{6,14},... | collective-permute-start | bytes 589832 | tf_op jit(solution)/shard_map/ppermute | solution.py:292
  39.6 37.1 %collective-permute-start.20 = (bf16[2,384,384]{2,1,0:T(8,128)(2,1)}, bf16[2,384,384]{2,1,0:T(8,128)(2,1)S(1)}, u32[]{:S(2)}, u32[]{:S(2)}) collective-permute-start(bf16[2,384,384]{2,1,0:T(8,128)(2,1)} %cut.7), channel_id=1, source_target_pairs={{0,4},{4,0},{8,12},{12,8},{1,5},{5,1},{9,13},{13,9},{2,6},{6,2},{1... | collective-permute-start | bytes 1769480 | tf_op jit(solution)/shard_map/ppermute | solution.py:281
  62.5 4.6 %collective-permute-start.2 = (bf16[2,384,128]{2,1,0:T(8,128)(2,1)S(1)}, bf16[2,384,128]{2,1,0:T(8,128)(2,1)S(1)}, u32[]{:S(2)}, u32[]{:S(2)}) collective-permute-start(bf16[2,384,128]{2,1,0:T(8,128)(2,1)S(1)} %copy-done.10), channel_id=1, source_target_pairs={{0,2},{2,0},{1,3},{3,1},{4,6},{6,4},{5,7},{7,5},{8,10},{10,8},{9,1... | collective-permute-start | bytes 589832 | tf_op jit(solution)/shard_map/ppermute | solution.py:293
  62.5 19.4 %collective-permute-start.9 = (bf16[2,384,384]{2,1,0:T(8,128)(2,1)S(1)}, bf16[2,384,384]{2,1,0:T(8,128)(2,1)}, u32[]{:S(2)}, u32[]{:S(2)}) collective-permute-start(bf16[2,384,384]{2,1,0:T(8,128)(2,1)S(1)} %collective-permute-done.8.refs_10_), channel_id=1, source_target_pairs={{0,16},{16,0},{1,17},{17,1},{2,18},{18,2},{3,19},{19,3},{4,20},{20... | collective-permute-start | bytes 1769480 | tf_op jit(solution)/shard_map/ppermute | solution.py:282
  67.1 9.6 %collective-permute-start.7 = (bf16[2,384,128]{2,1,0:T(8,128)(2,1)}, bf16[2,384,128]{2,1,0:T(8,128)(2,1)S(1)}, u32[]{:S(2)}, u32[]{:S(2)}) collective-permute-start(bf16[2,384,128]{2,1,0:T(8,128)(2,1)} %copy-done.11), channel_id=1, source_target_pairs={{0,2},{2,0},{1,3},{3,1},{4,6},{6,4},{5,7},{7,5},{8,10},{10,8},{9,1... | collective-permute-start | bytes 589832 | tf_op jit(solution)/shard_map/ppermute | solution.py:294
  67.2 26.8 %collective-permute-start.13 = (bf16[2,384,384]{2,1,0:T(8,128)(2,1)}, bf16[2,384,384]{2,1,0:T(8,128)(2,1)}, u32[]{:S(2)}, u32[]{:S(2)}) collective-permute-start(bf16[2,384,384]{2,1,0:T(8,128)(2,1)} %collective-permute-done.12.refs_3_), channel_id=1, source_target_pairs={{0,16},{16,0},{1,17},{17,1},{2,18},{18,2},{3,19},{19,3},{4,20},{20... | collective-permute-start | bytes 1769480 | tf_op jit(solution)/shard_map/ppermute | solution.py:282
  68.6 38.1 %collective-permute-start.17 = (bf16[2,384,384]{2,1,0:T(8,128)(2,1)S(1)}, bf16[2,384,384]{2,1,0:T(8,128)(2,1)}, u32[]{:S(2)}, u32[]{:S(2)}) collective-permute-start(bf16[2,384,384]{2,1,0:T(8,128)(2,1)S(1)} %collective-permute-done.16.refs_3_), channel_id=1, source_target_pairs={{0,16},{16,0},{1,17},{17,1},{2,18},{18,2},{3,19},{19,3},{4,20},{20... | collective-permute-start | bytes 1769480 | tf_op jit(solution)/shard_map/ppermute | solution.py:282
  76.7 4.5 %collective-permute-start.4 = (bf16[2,384,128]{2,1,0:T(8,128)(2,1)S(1)}, bf16[2,384,128]{2,1,0:T(8,128)(2,1)S(1)}, u32[]{:S(2)}, u32[]{:S(2)}) collective-permute-start(bf16[2,384,128]{2,1,0:T(8,128)(2,1)S(1)} %collective-permute-done.3.refs_2_), channel_id=1, source_target_pairs={{0,2},{2,0},{1,3},{3,1},{4,6},{6,4},{5,7},{7,5},{8,10},{10,8},{9,1... | collective-permute-start | bytes 589832 | tf_op jit(solution)/shard_map/ppermute | solution.py:294
  76.7 42.3 %collective-permute-start.21 = (bf16[2,384,384]{2,1,0:T(8,128)(2,1)S(1)}, bf16[2,384,384]{2,1,0:T(8,128)(2,1)}, u32[]{:S(2)}, u32[]{:S(2)}) collective-permute-start(bf16[2,384,384]{2,1,0:T(8,128)(2,1)S(1)} %collective-permute-done.20.refs_3_), channel_id=1, source_target_pairs={{0,16},{16,0},{1,17},{17,1},{2,18},{18,2},{3,19},{19,3},{4,20},{20... | collective-permute-start | bytes 1769480 | tf_op jit(solution)/shard_map/ppermute | solution.py:282
  87.8 38.0 %collective-permute-start.10 = (bf16[2,256,384]{2,1,0:T(8,128)(2,1)}, bf16[2,256,384]{2,1,0:T(8,128)(2,1)}, u32[]{:S(2)}, u32[]{:S(2)}) collective-permute-start(bf16[2,256,384]{2,1,0:T(8,128)(2,1)} %get-tuple-element.27), channel_id=1, source_target_pairs={{0,1},{1,0},{2,3},{3,2},{4,5},{5,4},{6,7},{7,6},{8,9},{9,8},{10,11... | collective-permute-start | bytes 1179656 | tf_op jit(solution)/shard_map/ppermute | solution.py:300
  99.3 30.8 %collective-permute-start.14 = (bf16[2,256,384]{2,1,0:T(8,128)(2,1)}, bf16[2,256,384]{2,1,0:T(8,128)(2,1)}, u32[]{:S(2)}, u32[]{:S(2)}) collective-permute-start(bf16[2,256,384]{2,1,0:T(8,128)(2,1)} %get-tuple-element.30), channel_id=1, source_target_pairs={{0,1},{1,0},{2,3},{3,2},{4,5},{5,4},{6,7},{7,6},{8,9},{9,8},{10,11... | collective-permute-start | bytes 1179656 | tf_op jit(solution)/shard_map/ppermute | solution.py:300
  112.0 19.3 %collective-permute-start.18 = (bf16[2,256,384]{2,1,0:T(8,128)(2,1)}, bf16[2,256,384]{2,1,0:T(8,128)(2,1)}, u32[]{:S(2)}, u32[]{:S(2)}) collective-permute-start(bf16[2,256,384]{2,1,0:T(8,128)(2,1)} %get-tuple-element.32), channel_id=1, source_target_pairs={{0,1},{1,0},{2,3},{3,2},{4,5},{5,4},{6,7},{7,6},{8,9},{9,8},{10,11... | collective-permute-start | bytes 1179656 | tf_op jit(solution)/shard_map/ppermute | solution.py:300
  124.3 11.1 %collective-permute-start.22 = (bf16[2,256,384]{2,1,0:T(8,128)(2,1)}, bf16[2,256,384]{2,1,0:T(8,128)(2,1)S(1)}, u32[]{:S(2)}, u32[]{:S(2)}) collective-permute-start(bf16[2,256,384]{2,1,0:T(8,128)(2,1)} %get-tuple-element.34), channel_id=1, source_target_pairs={{0,1},{1,0},{2,3},{3,2},{4,5},{5,4},{6,7},{7,6},{8,9},{9,8},{10,11... | collective-permute-start | bytes 1179656 | tf_op jit(solution)/shard_map/ppermute | solution.py:300
  126.8 25.7 %collective-permute-start.11 = (bf16[256,384]{1,0:T(8,128)(2,1)S(1)}, bf16[256,384]{1,0:T(8,128)(2,1)S(1)}, u32[]{:S(2)}, u32[]{:S(2)}) collective-permute-start(bf16[256,384]{1,0:T(8,128)(2,1)S(1)} %fusion.4), channel_id=1, source_target_pairs={{0,8},{4,12},{8,0},{12,4},{1,9},{5,13},{9,1},{13,5},{2,10},{6,14},... | collective-permute-start | bytes 589832 | tf_op jit(solution)/shard_map/ppermute | solution.py:301
  131.1 25.6 %collective-permute-start.15 = (bf16[256,384]{1,0:T(8,128)(2,1)S(1)}, bf16[256,384]{1,0:T(8,128)(2,1)S(1)}, u32[]{:S(2)}, u32[]{:S(2)}) collective-permute-start(bf16[256,384]{1,0:T(8,128)(2,1)S(1)} %fusion.5), channel_id=1, source_target_pairs={{0,8},{4,12},{8,0},{12,4},{1,9},{5,13},{9,1},{13,5},{2,10},{6,14},... | collective-permute-start | bytes 589832 | tf_op jit(solution)/shard_map/ppermute | solution.py:301
  132.2 28.7 %collective-permute-start.19 = (bf16[256,384]{1,0:T(8,128)(2,1)S(1)}, bf16[256,384]{1,0:T(8,128)(2,1)S(1)}, u32[]{:S(2)}, u32[]{:S(2)}) collective-permute-start(bf16[256,384]{1,0:T(8,128)(2,1)S(1)} %fusion.6), channel_id=1, source_target_pairs={{0,8},{4,12},{8,0},{12,4},{1,9},{5,13},{9,1},{13,5},{2,10},{6,14},... | collective-permute-start | bytes 589832 | tf_op jit(solution)/shard_map/ppermute | solution.py:301
  135.5 28.8 %collective-permute-start.23 = (bf16[256,384]{1,0:T(8,128)(2,1)S(1)}, bf16[256,384]{1,0:T(8,128)(2,1)S(1)}, u32[]{:S(2)}, u32[]{:S(2)}) collective-permute-start(bf16[256,384]{1,0:T(8,128)(2,1)S(1)} %fusion.7), channel_id=1, source_target_pairs={{0,8},{4,12},{8,0},{12,4},{1,9},{5,13},{9,1},{13,5},{2,10},{6,14},... | collective-permute-start | bytes 589832 | tf_op jit(solution)/shard_map/ppermute | solution.py:301
  (16 other events, 184.4 us)

commit v4 on v3

--- a/solution.py
+++ b/solution.py
@@ -12,7 +12,7 @@
 BPS = 4
 
 negative_floor = -1e30
-chunk_parts = (3, 3, 3, 3)
+chunk_parts = (3, 4, 3, 2)
 
 
 def attend_kernel(ids_ref, table_ref, index_ref, q_ref, *refs, first, pieces, block_len):
@@ -136,29 +136,33 @@
     return list(outs[: len(out_shape)]), list(outs[len(out_shape) :])
 
 
-def cut_kernel(ids_ref, w_ref, out_ref):
-    out_ref[0] = w_ref[...]
+def cut_kernel(ids_ref, w_ref, out_ref, sems, *, base):
+    rows, columns = out_ref.shape[1:]
+    at = pl.ds(pl.multiple_of(ids_ref[3] * rows, rows), rows)
+    half = w_ref.shape[1] // 2
+    copies = [
+        pltpu.make_async_copy(
+            w_ref.at[at, pl.ds(n * half + base, columns)], out_ref.at[n], sems.at[n]
+        )
+        for n in range(2)
+    ]
+    for copy in copies:
+        copy.start()
+    for copy in copies:
+        copy.wait()
 
 
 def cut(ids, w_local, base, columns):
     rows = w_local.shape[0] // 2
-    half = w_local.shape[1] // 2
     return pl.pallas_call(
-        cut_kernel,
+        functools.partial(cut_kernel, base=base),
         out_shape=jax.ShapeDtypeStruct((2, rows, columns), jnp.bfloat16),
         grid_spec=pltpu.PrefetchScalarGridSpec(
             num_scalar_prefetch=1,
-            grid=(2,),
-            in_specs=[
-                pl.BlockSpec(
-                    (pl.Element(rows), pl.Element(columns)),
-                    lambda n, ids: (
-                        pl.multiple_of(ids[3] * rows, 16),
-                        pl.multiple_of(n * half + base, 128),
-                    ),
-                )
-            ],
-            out_specs=pl.BlockSpec((1, rows, columns), lambda n, ids: (n, 0, 0)),
+            grid=(1,),
+            in_specs=[pl.BlockSpec(memory_space=pl.ANY)],
+            out_specs=pl.BlockSpec((2, rows, columns), lambda n, ids: (0, 0, 0)),
+            scratch_shapes=[pltpu.SemaphoreType.DMA((2,))],
         ),
         name="cut",
     )(ids, w_local)

time: 166 us -> 159 us (0.958)
  starting transfers between devices: 37 us -> 23.4 us
  waiting for transfers between devices: 68.5 us -> 73.6 us
    ppermute x2, waiting for transfers between devices: 22.4 us -> 33.1 us  [on_device(): far = lax.ppermute(sent, 'section', across)]
    ppermute x4, waiting for transfers between devices: 7.43 us -> 0.01 us  [on_device(): through_pair = lax.ppermute(sent, 'section', pair)]
    ppermute x4, starting transfers between devices: 9.73 us -> 3.83 us  [on_device(): far = lax.ppermute(add_rounded(kept[1], other[1]), 'section', across)]
    ppermute x4, starting transfers between devices: 11 us -> 5.19 us  [on_device(): w_pairs.append((through_pair, lax.ppermute(through_pair, 'group', swap)))]
    ppermute x4, waiting for transfers between devices: 22.4 us -> 17.1 us  [on_device(): far = lax.ppermute(add_rounded(kept[1], other[1]), 'section', across)]
    ppermute x4, waiting for transfers between devices: 0.23 us -> 4.9 us  [on_device(): other = lax.ppermute(sent, 'head', swap)]
    ppermute x4, starting transfers between devices: 7.9 us -> 4.96 us  [on_device(): through_pair = lax.ppermute(sent, 'section', pair)]
    ppermute x2, starting transfers between devices: 1.47 us -> 3.28 us  [on_device(): far = lax.ppermute(sent, 'section', across)]
  transfers between devices with their start and end apart: 24 -> 24, of which waited for: 11 -> 11; matrix products, arithmetic and copies ran while one was open for 5% -> 5% of each run, Pallas kernels for 30% -> 31%
where the time goes in v4:
time: 159 us; the launch traced here: 158 us
  waiting for transfers between devices  73.6 us (46%)
  Pallas kernels  48.9 us (31%)
  starting transfers between devices  23.4 us (15%)
  other arithmetic  8.51 us (5%)
  local copies, waits for them, and re-layouts  3.49 us (2%)
    ppermute x2, waiting for transfers between devices, on_device(): far = lax.ppermute(sent, 'section', across)  33.1 us
    pallas_call x4, Pallas kernels, project(): pl.pallas_call(functools.partial(project_kernel, inputs=len(flat), first=...  21.2 us
    pallas_call x2, Pallas kernels, attend(): pl.pallas_call(functools.partial(attend_kernel, first=first, pieces=piece...  17.4 us
    ppermute x4, waiting for transfers between devices, on_device(): w_pairs.append((through_pair, lax.ppermute(through_pair, 'group', swap)))  17.1 us
    ppermute x4, waiting for transfers between devices, on_device(): far = lax.ppermute(add_rounded(kept[1], other[1]), 'section', across)  17.1 us
    pallas_call x4, Pallas kernels, cut(): pl.pallas_call(functools.partial(cut_kernel, base=base), out_shape=jax.Sh...  10.3 us
    convert_element_type x8, other arithmetic, add_rounded(): return total.astype(jnp.bfloat16)  6.95 us
    ppermute x4, starting transfers between devices, on_device(): w_pairs.append((through_pair, lax.ppermute(through_pair, 'group', swap)))  5.19 us
  transfers between devices with their start and end apart: 24, of which 11 were waited for; matrix products, arithmetic and copies ran while one was open for 5% of the time, Pallas kernels for 31%

profile of v4, /device:TPU:0, one launch (start us, length us, event | category | flops | bytes accessed | tf_op | source)
XLA Modules:
  0.0 158.0 jit_solution(10527598408502745627)
XLA Ops:
  1.1 2.5 %cut.4 = bf16[2,384,384]{2,1,0:T(8,128)(2,1)} custom-call(s32[4]{0:T(128)} %pad_add_fusion.ids_ref, bf16[768,3072]{1,0:T(8,128)(2,1)} %bitcast.34), custom_call_target="tpu_custom_call" | custom-call | tf_op jit(solution)/shard_map/cut/pallas_call | solution.py:157
  3.7 2.6 %collective-permute-start.8 = (bf16[2,384,384]{2,1,0:T(8,128)(2,1)}, bf16[2,384,384]{2,1,0:T(8,128)(2,1)}, u32[]{:S(2)}, u32[]{:S(2)}) collective-permute-start(bf16[2,384,384]{2,1,0:T(8,128)(2,1)} %cut.4), channel_id=1, source_target_pairs={{0,4},{4,0},{8,12},{12,8},{1,5},{5,1},{9,13},{13,9},{2,6},{6,2},{1... | collective-permute-start | bytes 1769480 | tf_op jit(solution)/shard_map/ppermute | solution.py:285
  6.3 2.5 %cut.7 = bf16[2,384,256]{2,1,0:T(8,128)(2,1)} custom-call(s32[4]{0:T(128)} %pad_add_fusion.ids_ref, bf16[768,3072]{1,0:T(8,128)(2,1)} %bitcast.35), custom_call_target="tpu_custom_call" | custom-call | tf_op jit(solution)/shard_map/cut/pallas_call | solution.py:157
  8.9 2.7 %cut.5 = bf16[2,384,512]{2,1,0:T(8,128)(2,1)} custom-call(s32[4]{0:T(128)} %pad_add_fusion.ids_ref, bf16[768,3072]{1,0:T(8,128)(2,1)} %bitcast.36), custom_call_target="tpu_custom_call" | custom-call | tf_op jit(solution)/shard_map/cut/pallas_call | solution.py:157
  11.6 2.1 %collective-permute-start.12 = (bf16[2,384,512]{2,1,0:T(8,128)(2,1)}, bf16[2,384,512]{2,1,0:T(8,128)(2,1)S(1)}, u32[]{:S(2)}, u32[]{:S(2)}) collective-permute-start(bf16[2,384,512]{2,1,0:T(8,128)(2,1)} %cut.5), channel_id=1, source_target_pairs={{0,4},{4,0},{8,12},{12,8},{1,5},{5,1},{9,13},{13,9},{2,6},{6,2},{1... | collective-permute-start | bytes 2359304 | tf_op jit(solution)/shard_map/ppermute | solution.py:285
  13.7 2.6 %cut.6 = bf16[2,384,384]{2,1,0:T(8,128)(2,1)} custom-call(s32[4]{0:T(128)} %pad_add_fusion.ids_ref, bf16[768,3072]{1,0:T(8,128)(2,1)} %bitcast.37), custom_call_target="tpu_custom_call" | custom-call | tf_op jit(solution)/shard_map/cut/pallas_call | solution.py:157
  18.3 9.6 %attend.2 = (bf16[2,384,128]{2,1,0:T(8,128)(2,1)}, bf16[2,384,128]{2,1,0:T(8,128)(2,1)}, bf16[2304,128]{1,0:T(8,128)(2,1)}, bf16[144,2304]{1,0:T(8,128)(2,1)}) custom-call(s32[4]{0:T(128)} %pad_add_fusion.ids_ref, s32[4,16]{1,0:T(4,128)} %table_ref.3, s32[4]{0:T(128)} %index_ref.3, bf16[24,128,128]{2,1,0:T(8,128)(2,1)} %bitcast.46, ...), custom_call_target="tpu_custom_call" | custom-call | tf_op jit(solution)/shard_map/attend/pallas_call | solution.py:119
  27.9 7.9 %attend.3 = (bf16[2,384,128]{2,1,0:T(8,128)(2,1)}, bf16[2,384,128]{2,1,0:T(8,128)(2,1)}) custom-call(s32[4]{0:T(128)} %pad_add_fusion.ids_ref, s32[4,16]{1,0:T(4,128)} %table_ref.3, s32[4]{0:T(128)} %index_ref.3, bf16[24,128,128]{2,1,0:T(8,128)(2,1)} %bitcast.47, bf16[2304,128]{1,0:T(8,128)(2,1)} %get-tuple-element.22.refs_0_, ...), custom_call_target="tpu_custom_call" | custom-call | tf_op jit(solution)/shard_map/attend/pallas_call | solution.py:119
  36.2 25.8 %collective-permute-done.6.refs_6_ = bf16[2,384,128]{2,1,0:T(8,128)(2,1)S(1)} collective-permute-done((bf16[2,384,128]{2,1,0:T(8,128)(2,1)}, bf16[2,384,128]{2,1,0:T(8,128)(2,1)S(1)}, u32[]{:S(2)}, u32[]{:S(2)}) %collective-permute-start.6) | collective-permute-done | bytes 196640 | tf_op jit(solution)/shard_map/ppermute | solution.py:296
  62.0 3.3 %collective-permute-start.3 = (bf16[2,384,128]{2,1,0:T(8,128)(2,1)S(1)}, bf16[2,384,128]{2,1,0:T(8,128)(2,1)S(1)}, u32[]{:S(2)}, u32[]{:S(2)}) collective-permute-start(bf16[2,384,128]{2,1,0:T(8,128)(2,1)S(1)} %copy-done.18), channel_id=1, source_target_pairs={{0,8},{4,12},{8,0},{12,4},{1,9},{5,13},{9,1},{13,5},{2,10},{6,14},... | collective-permute-start | bytes 589832 | tf_op jit(solution)/shard_map/ppermute | solution.py:296
  66.9 7.3 %collective-permute-done.3.refs_2_ = bf16[2,384,128]{2,1,0:T(8,128)(2,1)S(1)} collective-permute-done((bf16[2,384,128]{2,1,0:T(8,128)(2,1)S(1)}, bf16[2,384,128]{2,1,0:T(8,128)(2,1)S(1)}, u32[]{:S(2)}, u32[]{:S(2)}) %collective-permute-start.3) | collective-permute-done | bytes 196640 | tf_op jit(solution)/shard_map/ppermute | solution.py:296
  80.1 1.7 %collective-permute-done.9.refs_11_ = bf16[2,384,384]{2,1,0:T(8,128)(2,1)} collective-permute-done((bf16[2,384,384]{2,1,0:T(8,128)(2,1)}, bf16[2,384,384]{2,1,0:T(8,128)(2,1)}, u32[]{:S(2)}, u32[]{:S(2)}) %collective-permute-start.9) | collective-permute-done | bytes 589856 | tf_op jit(solution)/shard_map/ppermute | solution.py:286
  81.8 5.9 %project.4 = (bf16[2,256,384]{2,1,0:T(8,128)(2,1)}, bf16[2,256,384]{2,1,0:T(8,128)(2,1)}, bf16[512,1536]{1,0:T(8,128)(2,1)}) custom-call(s32[4]{0:T(128)} %pad_add_fusion.ids_ref, bf16[2,384,128]{2,1,0:T(8,128)(2,1)} %get-tuple-element.20.refs_0_, bf16[2,384,128]{2,1,0:T(8,128)(2,1)} %copy-done.15, bf16[2,384,128]{2,1,0:T(8,128)(2,1)} %copy-done.14, ...), custom_call_target="tpu_custom_call" | custom-call | tf_op jit(solution)/shard_map/project/pallas_call | solution.py:220
  87.7 2.5 %collective-permute-done.21.refs_4_ = bf16[2,384,256]{2,1,0:T(8,128)(2,1)} collective-permute-done((bf16[2,384,256]{2,1,0:T(8,128)(2,1)S(1)}, bf16[2,384,256]{2,1,0:T(8,128)(2,1)}, u32[]{:S(2)}, u32[]{:S(2)}) %collective-permute-start.21) | collective-permute-done | bytes 393248 | tf_op jit(solution)/shard_map/ppermute | solution.py:286
  90.2 4.3 %project.7 = (bf16[2,256,256]{2,1,0:T(8,128)(2,1)}, bf16[2,256,256]{2,1,0:T(8,128)(2,1)}) custom-call(s32[4]{0:T(128)} %pad_add_fusion.ids_ref, bf16[512,1536]{1,0:T(8,128)(2,1)} %get-tuple-element.28.refs_0_, bf16[768,3072]{1,0:T(8,128)(2,1)} %bitcast.40, bf16[768,3072]{1,0:T(8,128)(2,1)} %bitcast.41, bf16[2,384,256]{2,1,0:T(8,128)(2,1)} %copy-done.4, ...), custom_call_target="tpu_custom_call" | custom-call | tf_op jit(solution)/shard_map/project/pallas_call | solution.py:220
  96.6 6.3 %collective-permute-done.17.refs_4_ = bf16[2,384,384]{2,1,0:T(8,128)(2,1)} collective-permute-done((bf16[2,384,384]{2,1,0:T(8,128)(2,1)}, bf16[2,384,384]{2,1,0:T(8,128)(2,1)}, u32[]{:S(2)}, u32[]{:S(2)}) %collective-permute-start.17) | collective-permute-done | bytes 589856 | tf_op jit(solution)/shard_map/ppermute | solution.py:286
  102.9 5.4 %project.6 = (bf16[2,256,384]{2,1,0:T(8,128)(2,1)}, bf16[2,256,384]{2,1,0:T(8,128)(2,1)}) custom-call(s32[4]{0:T(128)} %pad_add_fusion.ids_ref, bf16[512,1536]{1,0:T(8,128)(2,1)} %get-tuple-element.28.refs_0_, bf16[768,3072]{1,0:T(8,128)(2,1)} %bitcast.42, bf16[768,3072]{1,0:T(8,128)(2,1)} %bitcast.43, bf16[2,384,384]{2,1,0:T(8,128)(2,1)} %collective-permute-done.16.refs_3_, ...), custom_call_target="tpu_custom_call" | custom-call | tf_op jit(solution)/shard_map/project/pallas_call | solution.py:220
  111.4 6.6 %collective-permute-done.13.refs_4_ = bf16[2,384,512]{2,1,0:T(8,128)(2,1)S(1)} collective-permute-done((bf16[2,384,512]{2,1,0:T(8,128)(2,1)S(1)}, bf16[2,384,512]{2,1,0:T(8,128)(2,1)S(1)}, u32[]{:S(2)}, u32[]{:S(2)}) %collective-permute-start.13) | collective-permute-done | bytes 786464 | tf_op jit(solution)/shard_map/ppermute | solution.py:286
  118.9 5.6 %project.5 = (bf16[2,256,512]{2,1,0:T(8,128)(2,1)}, bf16[2,256,512]{2,1,0:T(8,128)(2,1)}) custom-call(s32[4]{0:T(128)} %pad_add_fusion.ids_ref, bf16[512,1536]{1,0:T(8,128)(2,1)} %get-tuple-element.28.refs_0_, bf16[768,3072]{1,0:T(8,128)(2,1)} %bitcast.44, bf16[768,3072]{1,0:T(8,128)(2,1)} %bitcast.45, bf16[2,384,512]{2,1,0:T(8,128)(2,1)} %copy-done.1, ...), custom_call_target="tpu_custom_call" | custom-call | tf_op jit(solution)/shard_map/project/pallas_call | solution.py:220
  128.5 2.6 %collective-permute-start.19 = (bf16[256,384]{1,0:T(8,128)(2,1)S(1)}, bf16[256,384]{1,0:T(8,128)(2,1)S(1)}, u32[]{:S(2)}, u32[]{:S(2)}) collective-permute-start(bf16[256,384]{1,0:T(8,128)(2,1)S(1)} %fusion.6), channel_id=1, source_target_pairs={{0,8},{4,12},{8,0},{12,4},{1,9},{5,13},{9,1},{13,5},{2,10},{6,14},... | collective-permute-start | bytes 589832 | tf_op jit(solution)/shard_map/ppermute | solution.py:305
  132.2 4.9 %collective-permute-done.14 = bf16[2,256,512]{2,1,0:T(8,128)(2,1)S(1)} collective-permute-done((bf16[2,256,512]{2,1,0:T(8,128)(2,1)}, bf16[2,256,512]{2,1,0:T(8,128)(2,1)S(1)}, u32[]{:S(2)}, u32[]{:S(2)}) %collective-permute-start.14) | collective-permute-done | bytes 524320 | tf_op jit(solution)/shard_map/ppermute | solution.py:304
  137.9 9.7 %collective-permute-done.11 = bf16[256,384]{1,0:T(8,128)(2,1)S(1)} collective-permute-done((bf16[256,384]{1,0:T(8,128)(2,1)S(1)}, bf16[256,384]{1,0:T(8,128)(2,1)S(1)}, u32[]{:S(2)}, u32[]{:S(2)}) %collective-permute-start.11) | collective-permute-done | bytes 196640 | tf_op jit(solution)/shard_map/ppermute | solution.py:305
  148.6 3.2 %collective-permute-done.19 = bf16[256,384]{1,0:T(8,128)(2,1)S(1)} collective-permute-done((bf16[256,384]{1,0:T(8,128)(2,1)S(1)}, bf16[256,384]{1,0:T(8,128)(2,1)S(1)}, u32[]{:S(2)}, u32[]{:S(2)}) %collective-permute-start.19) | collective-permute-done | bytes 196640 | tf_op jit(solution)/shard_map/ppermute | solution.py:305
  152.8 4.2 %collective-permute-done.15 = bf16[256,512]{1,0:T(8,128)(2,1)S(1)} collective-permute-done((bf16[256,512]{1,0:T(8,128)(2,1)S(1)}, bf16[256,512]{1,0:T(8,128)(2,1)S(1)}, u32[]{:S(2)}, u32[]{:S(2)}) %collective-permute-start.15) | collective-permute-done | bytes 262176 | tf_op jit(solution)/shard_map/ppermute | solution.py:305
  (84 shorter events, 26.2 us)
Async XLA Ops:
  0.0 16.2 %collective-permute-start = (bf16[8,128,128]{2,1,0:T(8,128)(2,1)}, bf16[8,128,128]{2,1,0:T(8,128)(2,1)S(1)}, u32[]{:S(2)}, u32[]{:S(2)}) collective-permute-start(bf16[8,128,128]{2,1,0:T(8,128)(2,1)} %bitcast.48), channel_id=1, source_target_pairs={{0,2},{2,0},{1,3},{3,1},{4,6},{6,4},{5,7},{7,5},{8,10},{10,8},{9,1... | collective-permute-start | bytes 786440 | tf_op jit(solution)/shard_map/ppermute | solution.py:271
  3.7 61.6 %collective-permute-start.8 = (bf16[2,384,384]{2,1,0:T(8,128)(2,1)}, bf16[2,384,384]{2,1,0:T(8,128)(2,1)}, u32[]{:S(2)}, u32[]{:S(2)}) collective-permute-start(bf16[2,384,384]{2,1,0:T(8,128)(2,1)} %cut.4), channel_id=1, source_target_pairs={{0,4},{4,0},{8,12},{12,8},{1,5},{5,1},{9,13},{13,9},{2,6},{6,2},{1... | collective-permute-start | bytes 1769480 | tf_op jit(solution)/shard_map/ppermute | solution.py:285
  8.8 27.0 %collective-permute-start.20 = (bf16[2,384,256]{2,1,0:T(8,128)(2,1)}, bf16[2,384,256]{2,1,0:T(8,128)(2,1)S(1)}, u32[]{:S(2)}, u32[]{:S(2)}) collective-permute-start(bf16[2,384,256]{2,1,0:T(8,128)(2,1)} %cut.7), channel_id=1, source_target_pairs={{0,4},{4,0},{8,12},{12,8},{1,5},{5,1},{9,13},{13,9},{2,6},{6,2},{1... | collective-permute-start | bytes 1179656 | tf_op jit(solution)/shard_map/ppermute | solution.py:285
  11.6 64.7 %collective-permute-start.12 = (bf16[2,384,512]{2,1,0:T(8,128)(2,1)}, bf16[2,384,512]{2,1,0:T(8,128)(2,1)S(1)}, u32[]{:S(2)}, u32[]{:S(2)}) collective-permute-start(bf16[2,384,512]{2,1,0:T(8,128)(2,1)} %cut.5), channel_id=1, source_target_pairs={{0,4},{4,0},{8,12},{12,8},{1,5},{5,1},{9,13},{13,9},{2,6},{6,2},{1... | collective-permute-start | bytes 2359304 | tf_op jit(solution)/shard_map/ppermute | solution.py:285
  13.7 3.9 %collective-permute-start.1 = (bf16[8,128,128]{2,1,0:T(8,128)(2,1)S(1)}, bf16[8,128,128]{2,1,0:T(8,128)(2,1)S(1)}, u32[]{:S(2)}, u32[]{:S(2)}) collective-permute-start(bf16[8,128,128]{2,1,0:T(8,128)(2,1)S(1)} %bitcast.51), channel_id=1, source_target_pairs={{0,2},{2,0},{1,3},{3,1},{4,6},{6,4},{5,7},{7,5},{8,10},{10,8},{9,1... | collective-permute-start | bytes 786440 | tf_op jit(solution)/shard_map/ppermute | solution.py:272
  16.3 59.5 %collective-permute-start.16 = (bf16[2,384,384]{2,1,0:T(8,128)(2,1)}, bf16[2,384,384]{2,1,0:T(8,128)(2,1)}, u32[]{:S(2)}, u32[]{:S(2)}) collective-permute-start(bf16[2,384,384]{2,1,0:T(8,128)(2,1)} %cut.6), channel_id=1, source_target_pairs={{0,4},{4,0},{8,12},{12,8},{1,5},{5,1},{9,13},{13,9},{2,6},{6,2},{1... | collective-permute-start | bytes 1769480 | tf_op jit(solution)/shard_map/ppermute | solution.py:285
  35.7 26.3 %collective-permute-start.6 = (bf16[2,384,128]{2,1,0:T(8,128)(2,1)}, bf16[2,384,128]{2,1,0:T(8,128)(2,1)S(1)}, u32[]{:S(2)}, u32[]{:S(2)}) collective-permute-start(bf16[2,384,128]{2,1,0:T(8,128)(2,1)} %get-tuple-element.25), channel_id=1, source_target_pairs={{0,8},{4,12},{8,0},{12,4},{1,9},{5,13},{9,1},{13,5},{2,10},{6,14},... | collective-permute-start | bytes 589832 | tf_op jit(solution)/shard_map/ppermute | solution.py:296
  35.7 31.1 %collective-permute-start.5 = (bf16[2,384,128]{2,1,0:T(8,128)(2,1)}, bf16[2,384,128]{2,1,0:T(8,128)(2,1)S(1)}, u32[]{:S(2)}, u32[]{:S(2)}) collective-permute-start(bf16[2,384,128]{2,1,0:T(8,128)(2,1)} %get-tuple-element.24.refs_4_), channel_id=1, source_target_pairs={{0,2},{2,0},{1,3},{3,1},{4,6},{6,4},{5,7},{7,5},{8,10},{10,8},{9,1... | collective-permute-start | bytes 589832 | tf_op jit(solution)/shard_map/ppermute | solution.py:297
  62.0 12.2 %collective-permute-start.3 = (bf16[2,384,128]{2,1,0:T(8,128)(2,1)S(1)}, bf16[2,384,128]{2,1,0:T(8,128)(2,1)S(1)}, u32[]{:S(2)}, u32[]{:S(2)}) collective-permute-start(bf16[2,384,128]{2,1,0:T(8,128)(2,1)S(1)} %copy-done.18), channel_id=1, source_target_pairs={{0,8},{4,12},{8,0},{12,4},{1,9},{5,13},{9,1},{13,5},{2,10},{6,14},... | collective-permute-start | bytes 589832 | tf_op jit(solution)/shard_map/ppermute | solution.py:296
  65.3 16.5 %collective-permute-start.9 = (bf16[2,384,384]{2,1,0:T(8,128)(2,1)}, bf16[2,384,384]{2,1,0:T(8,128)(2,1)}, u32[]{:S(2)}, u32[]{:S(2)}) collective-permute-start(bf16[2,384,384]{2,1,0:T(8,128)(2,1)} %collective-permute-done.8.refs_10_), channel_id=1, source_target_pairs={{0,16},{16,0},{1,17},{17,1},{2,18},{18,2},{3,19},{19,3},{4,20},{20... | collective-permute-start | bytes 1769480 | tf_op jit(solution)/shard_map/ppermute | solution.py:286
  66.8 7.4 %collective-permute-start.2 = (bf16[2,384,128]{2,1,0:T(8,128)(2,1)S(1)}, bf16[2,384,128]{2,1,0:T(8,128)(2,1)S(1)}, u32[]{:S(2)}, u32[]{:S(2)}) collective-permute-start(bf16[2,384,128]{2,1,0:T(8,128)(2,1)S(1)} %copy-done.11), channel_id=1, source_target_pairs={{0,2},{2,0},{1,3},{3,1},{4,6},{6,4},{5,7},{7,5},{8,10},{10,8},{9,1... | collective-permute-start | bytes 589832 | tf_op jit(solution)/shard_map/ppermute | solution.py:297
  74.2 3.7 %collective-permute-start.7 = (bf16[2,384,128]{2,1,0:T(8,128)(2,1)S(1)}, bf16[2,384,128]{2,1,0:T(8,128)(2,1)S(1)}, u32[]{:S(2)}, u32[]{:S(2)}) collective-permute-start(bf16[2,384,128]{2,1,0:T(8,128)(2,1)S(1)} %collective-permute-done.6.refs_6_), channel_id=1, source_target_pairs={{0,2},{2,0},{1,3},{3,1},{4,6},{6,4},{5,7},{7,5},{8,10},{10,8},{9,1... | collective-permute-start | bytes 589832 | tf_op jit(solution)/shard_map/ppermute | solution.py:298
  74.2 16.0 %collective-permute-start.21 = (bf16[2,384,256]{2,1,0:T(8,128)(2,1)S(1)}, bf16[2,384,256]{2,1,0:T(8,128)(2,1)}, u32[]{:S(2)}, u32[]{:S(2)}) collective-permute-start(bf16[2,384,256]{2,1,0:T(8,128)(2,1)S(1)} %collective-permute-done.20.refs_3_), channel_id=1, source_target_pairs={{0,16},{16,0},{1,17},{17,1},{2,18},{18,2},{3,19},{19,3},{4,20},{20... | collective-permute-start | bytes 1179656 | tf_op jit(solution)/shard_map/ppermute | solution.py:286
  75.8 27.1 %collective-permute-start.17 = (bf16[2,384,384]{2,1,0:T(8,128)(2,1)}, bf16[2,384,384]{2,1,0:T(8,128)(2,1)}, u32[]{:S(2)}, u32[]{:S(2)}) collective-permute-start(bf16[2,384,384]{2,1,0:T(8,128)(2,1)} %collective-permute-done.16.refs_3_), channel_id=1, source_target_pairs={{0,16},{16,0},{1,17},{17,1},{2,18},{18,2},{3,19},{19,3},{4,20},{20... | collective-permute-start | bytes 1769480 | tf_op jit(solution)/shard_map/ppermute | solution.py:286
  76.3 41.7 %collective-permute-start.13 = (bf16[2,384,512]{2,1,0:T(8,128)(2,1)S(1)}, bf16[2,384,512]{2,1,0:T(8,128)(2,1)S(1)}, u32[]{:S(2)}, u32[]{:S(2)}) collective-permute-start(bf16[2,384,512]{2,1,0:T(8,128)(2,1)S(1)} %collective-permute-done.12.refs_3_), channel_id=1, source_target_pairs={{0,16},{16,0},{1,17},{17,1},{2,18},{18,2},{3,19},{19,3},{4,20},{20... | collective-permute-start | bytes 2359304 | tf_op jit(solution)/shard_map/ppermute | solution.py:286
  77.9 1.5 collective-permute-start.4
  94.5 15.2 %collective-permute-start.22 = (bf16[2,256,256]{2,1,0:T(8,128)(2,1)}, bf16[2,256,256]{2,1,0:T(8,128)(2,1)}, u32[]{:S(2)}, u32[]{:S(2)}) collective-permute-start(bf16[2,256,256]{2,1,0:T(8,128)(2,1)} %get-tuple-element.34), channel_id=1, source_target_pairs={{0,1},{1,0},{2,3},{3,2},{4,5},{5,4},{6,7},{7,6},{8,9},{9,8},{10,11... | collective-permute-start | bytes 786440 | tf_op jit(solution)/shard_map/ppermute | solution.py:304
  96.0 29.9 %collective-permute-start.10 = (bf16[2,256,384]{2,1,0:T(8,128)(2,1)}, bf16[2,256,384]{2,1,0:T(8,128)(2,1)}, u32[]{:S(2)}, u32[]{:S(2)}) collective-permute-start(bf16[2,256,384]{2,1,0:T(8,128)(2,1)} %get-tuple-element.27), channel_id=1, source_target_pairs={{0,1},{1,0},{2,3},{3,2},{4,5},{5,4},{6,7},{7,6},{8,9},{9,8},{10,11... | collective-permute-start | bytes 1179656 | tf_op jit(solution)/shard_map/ppermute | solution.py:304
  108.2 19.2 %collective-permute-start.18 = (bf16[2,256,384]{2,1,0:T(8,128)(2,1)}, bf16[2,256,384]{2,1,0:T(8,128)(2,1)}, u32[]{:S(2)}, u32[]{:S(2)}) collective-permute-start(bf16[2,256,384]{2,1,0:T(8,128)(2,1)} %get-tuple-element.32), channel_id=1, source_target_pairs={{0,1},{1,0},{2,3},{3,2},{4,5},{5,4},{6,7},{7,6},{8,9},{9,8},{10,11... | collective-permute-start | bytes 1179656 | tf_op jit(solution)/shard_map/ppermute | solution.py:304
  111.3 19.8 %collective-permute-start.23 = (bf16[256,256]{1,0:T(8,128)(2,1)}, bf16[256,256]{1,0:T(8,128)(2,1)}, u32[]{:S(2)}, u32[]{:S(2)}) collective-permute-start(bf16[256,256]{1,0:T(8,128)(2,1)} %fusion.7), channel_id=1, source_target_pairs={{0,8},{4,12},{8,0},{12,4},{1,9},{5,13},{9,1},{13,5},{2,10},{6,14},... | collective-permute-start | bytes 393224 | tf_op jit(solution)/shard_map/ppermute | solution.py:305
  124.5 12.6 %collective-permute-start.14 = (bf16[2,256,512]{2,1,0:T(8,128)(2,1)}, bf16[2,256,512]{2,1,0:T(8,128)(2,1)S(1)}, u32[]{:S(2)}, u32[]{:S(2)}) collective-permute-start(bf16[2,256,512]{2,1,0:T(8,128)(2,1)} %get-tuple-element.30), channel_id=1, source_target_pairs={{0,1},{1,0},{2,3},{3,2},{4,5},{5,4},{6,7},{7,6},{8,9},{9,8},{10,11... | collective-permute-start | bytes 1572872 | tf_op jit(solution)/shard_map/ppermute | solution.py:304
  127.0 20.6 %collective-permute-start.11 = (bf16[256,384]{1,0:T(8,128)(2,1)S(1)}, bf16[256,384]{1,0:T(8,128)(2,1)S(1)}, u32[]{:S(2)}, u32[]{:S(2)}) collective-permute-start(bf16[256,384]{1,0:T(8,128)(2,1)S(1)} %fusion.5), channel_id=1, source_target_pairs={{0,8},{4,12},{8,0},{12,4},{1,9},{5,13},{9,1},{13,5},{2,10},{6,14},... | collective-permute-start | bytes 589832 | tf_op jit(solution)/shard_map/ppermute | solution.py:305
  128.5 23.3 %collective-permute-start.19 = (bf16[256,384]{1,0:T(8,128)(2,1)S(1)}, bf16[256,384]{1,0:T(8,128)(2,1)S(1)}, u32[]{:S(2)}, u32[]{:S(2)}) collective-permute-start(bf16[256,384]{1,0:T(8,128)(2,1)S(1)} %fusion.6), channel_id=1, source_target_pairs={{0,8},{4,12},{8,0},{12,4},{1,9},{5,13},{9,1},{13,5},{2,10},{6,14},... | collective-permute-start | bytes 589832 | tf_op jit(solution)/shard_map/ppermute | solution.py:305
  137.2 19.8 %collective-permute-start.15 = (bf16[256,512]{1,0:T(8,128)(2,1)S(1)}, bf16[256,512]{1,0:T(8,128)(2,1)S(1)}, u32[]{:S(2)}, u32[]{:S(2)}) collective-permute-start(bf16[256,512]{1,0:T(8,128)(2,1)S(1)} %fusion.3), channel_id=1, source_target_pairs={{0,8},{4,12},{8,0},{12,4},{1,9},{5,13},{9,1},{13,5},{2,10},{6,14},... | collective-permute-start | bytes 786440 | tf_op jit(solution)/shard_map/ppermute | solution.py:305
  (19 other events, 264.1 us)

commit v5 on v3

--- a/solution.py
+++ b/solution.py
@@ -12,7 +12,7 @@
 BPS = 4
 
 negative_floor = -1e30
-chunk_parts = (3, 3, 3, 3)
+chunk_parts = (3, 4, 3, 2)
 
 
 def attend_kernel(ids_ref, table_ref, index_ref, q_ref, *refs, first, pieces, block_len):
@@ -136,34 +136,6 @@
     return list(outs[: len(out_shape)]), list(outs[len(out_shape) :])
 
 
-def cut_kernel(ids_ref, w_ref, out_ref):
-    out_ref[0] = w_ref[...]
-
-
-def cut(ids, w_local, base, columns):
-    rows = w_local.shape[0] // 2
-    half = w_local.shape[1] // 2
-    return pl.pallas_call(
-        cut_kernel,
-        out_shape=jax.ShapeDtypeStruct((2, rows, columns), jnp.bfloat16),
-        grid_spec=pltpu.PrefetchScalarGridSpec(
-            num_scalar_prefetch=1,
-            grid=(2,),
-            in_specs=[
-                pl.BlockSpec(
-                    (pl.Element(rows), pl.Element(columns)),
-                    lambda n, ids: (
-                        pl.multiple_of(ids[3] * rows, 16),
-                        pl.multiple_of(n * half + base, 128),
-                    ),
-                )
-            ],
-            out_specs=pl.BlockSpec((1, rows, columns), lambda n, ids: (n, 0, 0)),
-        ),
-        name="cut",
-    )(ids, w_local)
-
-
 def project_kernel(ids_ref, *refs, inputs, first):
     w_refs = refs[inputs : inputs + 2]
     w_pairs = refs[inputs + 2 : inputs + 4]
@@ -275,9 +247,11 @@
         across = [(z, z ^ 2) for z in range(section_count)]
         widths = [out_columns * w // sum(chunk_parts) for w in chunk_parts]
         bases = [sum(widths[:j]) for j in range(len(widths))]
+        half_rows = w_local.shape[0] // 2
         w_pairs = []
         for base, columns in zip(bases, widths):
-            sent = cut(ids, w_local, base, columns)
+            cut = lambda at: lax.dynamic_slice(w_local, (group * half_rows, at), (half_rows, columns))
+            sent = jnp.stack([cut(base), cut(out_columns + base)])
             through_pair = lax.ppermute(sent, "section", pair)
             w_pairs.append((through_pair, lax.ppermute(through_pair, "group", swap)))
         arrays = blocks

time: 166 us -> 157 us (0.946)
  starting transfers between devices: 37 us -> 23.1 us
  Pallas kernels: 49.4 us -> 38.7 us
  waiting for transfers between devices: 68.5 us -> 75.3 us
  local copies, waits for them, and re-layouts: 2.68 us -> 7.04 us
  other arithmetic: 7.66 us -> 12 us
    ppermute x2, waiting for transfers between devices: 22.4 us -> 35.1 us  [on_device(): far = lax.ppermute(sent, 'section', across)]
    pallas_call x4 -> x0, Pallas kernels: 10.1 us -> none  [cut(): pl.pallas_call(cut_kernel, out_shape=jax.ShapeDtypeStruct((2, rows, colum...]
    ppermute x4, waiting for transfers between devices: 7.43 us -> 0.01 us  [on_device(): through_pair = lax.ppermute(sent, 'section', pair)]
    ppermute x4, starting transfers between devices: 9.73 us -> 3.83 us  [on_device(): far = lax.ppermute(add_rounded(kept[1], other[1]), 'section', across)]
    ppermute x4, starting transfers between devices: 11 us -> 5.19 us  [on_device(): w_pairs.append((through_pair, lax.ppermute(through_pair, 'group', swap)))]
    ppermute x4, waiting for transfers between devices: 22.4 us -> 17.1 us  [on_device(): far = lax.ppermute(add_rounded(kept[1], other[1]), 'section', across)]
    ppermute x4, waiting for transfers between devices: 0.23 us -> 4.48 us  [on_device(): other = lax.ppermute(sent, 'head', swap)]
    another operation x0 -> x3, local copies, waits for them, and re-layouts: none -> 3.57 us  [on_device(): sent = jnp.stack([cut(base), cut(out_columns + base)])]
  transfers between devices with their start and end apart: 24 -> 24, of which waited for: 11 -> 11; matrix products, arithmetic and copies ran while one was open for 5% -> 10% of each run, Pallas kernels for 30% -> 25%
where the time goes in v5:
time: 157 us; the launch traced here: 156 us
  waiting for transfers between devices  75.3 us (48%)
  Pallas kernels  38.7 us (25%)
  starting transfers between devices  23.1 us (15%)
  other arithmetic  12 us (8%)
  local copies, waits for them, and re-layouts  7.04 us (4%)
    ppermute x2, waiting for transfers between devices, on_device(): far = lax.ppermute(sent, 'section', across)  35.1 us
    pallas_call x4, Pallas kernels, project(): pl.pallas_call(functools.partial(project_kernel, inputs=len(flat), first=...  21.1 us
    pallas_call x2, Pallas kernels, attend(): pl.pallas_call(functools.partial(attend_kernel, first=first, pieces=piece...  17.6 us
    ppermute x4, waiting for transfers between devices, on_device(): w_pairs.append((through_pair, lax.ppermute(through_pair, 'group', swap)))  17.2 us
    ppermute x4, waiting for transfers between devices, on_device(): far = lax.ppermute(add_rounded(kept[1], other[1]), 'section', across)  17.1 us
    convert_element_type x8, other arithmetic, add_rounded(): return total.astype(jnp.bfloat16)  6.95 us
    ppermute x4, starting transfers between devices, on_device(): w_pairs.append((through_pair, lax.ppermute(through_pair, 'group', swap)))  5.19 us
    ppermute x4, starting transfers between devices, on_device(): through_pair = lax.ppermute(sent, 'section', pair)  5.03 us
  transfers between devices with their start and end apart: 24, of which 11 were waited for; matrix products, arithmetic and copies ran while one was open for 10% of the time, Pallas kernels for 25%

profile of v5, /device:TPU:0, one launch (start us, length us, event | category | flops | bytes accessed | tf_op | source)
XLA Modules:
  0.0 156.3 jit_solution(7073978075848786346)
XLA Ops:
  2.8 3.0 %collective-permute-start.8 = (bf16[2,384,384]{2,1,0:T(8,128)(2,1)}, bf16[2,384,384]{2,1,0:T(8,128)(2,1)}, u32[]{:S(2)}, u32[]{:S(2)}) collective-permute-start(bf16[2,384,384]{2,1,0:T(8,128)(2,1)} %pad_maximum_fusion.2), channel_id=1, source_target_pairs={{0,4},{4,0},{8,12},{12,8},{1,5},{5,1},{9,13},{13,9},{2,6},{6,2},{1... | collective-permute-start | bytes 1769480 | tf_op jit(solution)/shard_map/ppermute | solution.py:255
  9.8 2.0 %collective-permute-start.12 = (bf16[2,384,512]{2,1,0:T(8,128)(2,1)}, bf16[2,384,512]{2,1,0:T(8,128)(2,1)S(1)}, u32[]{:S(2)}, u32[]{:S(2)}) collective-permute-start(bf16[2,384,512]{2,1,0:T(8,128)(2,1)} %pad_maximum_fusion), channel_id=1, source_target_pairs={{0,4},{4,0},{8,12},{12,8},{1,5},{5,1},{9,13},{13,9},{2,6},{6,2},{1... | collective-permute-start | bytes 2359304 | tf_op jit(solution)/shard_map/ppermute | solution.py:255
  15.1 9.5 %attend.2 = (bf16[2,384,128]{2,1,0:T(8,128)(2,1)}, bf16[2,384,128]{2,1,0:T(8,128)(2,1)}, bf16[2304,128]{1,0:T(8,128)(2,1)}, bf16[144,2304]{1,0:T(8,128)(2,1)}) custom-call(s32[4]{0:T(128)} %pad_add_fusion.ids_ref, s32[4,16]{1,0:T(4,128)} %table_ref.3, s32[4]{0:T(128)} %index_ref.3, bf16[24,128,128]{2,1,0:T(8,128)(2,1)} %bitcast.61, ...), custom_call_target="tpu_custom_call" | custom-call | tf_op jit(solution)/shard_map/attend/pallas_call | solution.py:119
  24.7 8.0 %attend.3 = (bf16[2,384,128]{2,1,0:T(8,128)(2,1)}, bf16[2,384,128]{2,1,0:T(8,128)(2,1)}) custom-call(s32[4]{0:T(128)} %pad_add_fusion.ids_ref, s32[4,16]{1,0:T(4,128)} %table_ref.3, s32[4]{0:T(128)} %index_ref.3, bf16[24,128,128]{2,1,0:T(8,128)(2,1)} %bitcast.62, bf16[2304,128]{1,0:T(8,128)(2,1)} %get-tuple-element.22.refs_0_, ...), custom_call_target="tpu_custom_call" | custom-call | tf_op jit(solution)/shard_map/attend/pallas_call | solution.py:119
  32.8 28.2 %collective-permute-done.6.refs_6_ = bf16[2,384,128]{2,1,0:T(8,128)(2,1)S(1)} collective-permute-done((bf16[2,384,128]{2,1,0:T(8,128)(2,1)}, bf16[2,384,128]{2,1,0:T(8,128)(2,1)S(1)}, u32[]{:S(2)}, u32[]{:S(2)}) %collective-permute-start.6) | collective-permute-done | bytes 196640 | tf_op jit(solution)/shard_map/ppermute | solution.py:266
  61.1 3.3 %collective-permute-start.3 = (bf16[2,384,128]{2,1,0:T(8,128)(2,1)S(1)}, bf16[2,384,128]{2,1,0:T(8,128)(2,1)S(1)}, u32[]{:S(2)}, u32[]{:S(2)}) collective-permute-start(bf16[2,384,128]{2,1,0:T(8,128)(2,1)S(1)} %copy-done.16), channel_id=1, source_target_pairs={{0,8},{4,12},{8,0},{12,4},{1,9},{5,13},{9,1},{13,5},{2,10},{6,14},... | collective-permute-start | bytes 589832 | tf_op jit(solution)/shard_map/ppermute | solution.py:266
  64.4 1.5 collective-permute-start.9
  66.0 6.9 %collective-permute-done.3.refs_2_ = bf16[2,384,128]{2,1,0:T(8,128)(2,1)S(1)} collective-permute-done((bf16[2,384,128]{2,1,0:T(8,128)(2,1)S(1)}, bf16[2,384,128]{2,1,0:T(8,128)(2,1)S(1)}, u32[]{:S(2)}, u32[]{:S(2)}) %collective-permute-start.3) | collective-permute-done | bytes 196640 | tf_op jit(solution)/shard_map/ppermute | solution.py:266
  72.9 1.6 %collective-permute-start.21 = (bf16[2,384,256]{2,1,0:T(8,128)(2,1)S(1)}, bf16[2,384,256]{2,1,0:T(8,128)(2,1)}, u32[]{:S(2)}, u32[]{:S(2)}) collective-permute-start(bf16[2,384,256]{2,1,0:T(8,128)(2,1)S(1)} %collective-permute-done.20.refs_3_), channel_id=1, source_target_pairs={{0,16},{16,0},{1,17},{17,1},{2,18},{18,2},{3,19},{19,3},{4,20},{20... | collective-permute-start | bytes 1179656 | tf_op jit(solution)/shard_map/ppermute | solution.py:256
  75.0 1.6 %collective-permute-start.13 = (bf16[2,384,512]{2,1,0:T(8,128)(2,1)S(1)}, bf16[2,384,512]{2,1,0:T(8,128)(2,1)S(1)}, u32[]{:S(2)}, u32[]{:S(2)}) collective-permute-start(bf16[2,384,512]{2,1,0:T(8,128)(2,1)S(1)} %collective-permute-done.12.refs_3_), channel_id=1, source_target_pairs={{0,16},{16,0},{1,17},{17,1},{2,18},{18,2},{3,19},{19,3},{4,20},{20... | collective-permute-start | bytes 2359304 | tf_op jit(solution)/shard_map/ppermute | solution.py:256
  78.8 2.1 %collective-permute-done.9.refs_11_ = bf16[2,384,384]{2,1,0:T(8,128)(2,1)} collective-permute-done((bf16[2,384,384]{2,1,0:T(8,128)(2,1)}, bf16[2,384,384]{2,1,0:T(8,128)(2,1)}, u32[]{:S(2)}, u32[]{:S(2)}) %collective-permute-start.9) | collective-permute-done | bytes 589856 | tf_op jit(solution)/shard_map/ppermute | solution.py:256
  80.9 5.9 %project.4 = (bf16[2,256,384]{2,1,0:T(8,128)(2,1)}, bf16[2,256,384]{2,1,0:T(8,128)(2,1)}, bf16[512,1536]{1,0:T(8,128)(2,1)}) custom-call(s32[4]{0:T(128)} %pad_add_fusion.ids_ref, bf16[2,384,128]{2,1,0:T(8,128)(2,1)} %get-tuple-element.20.refs_0_, bf16[2,384,128]{2,1,0:T(8,128)(2,1)} %copy-done.13, bf16[2,384,128]{2,1,0:T(8,128)(2,1)} %copy-done.12, ...), custom_call_target="tpu_custom_call" | custom-call | tf_op jit(solution)/shard_map/project/pallas_call | solution.py:188
  86.8 2.5 %collective-permute-done.21.refs_4_ = bf16[2,384,256]{2,1,0:T(8,128)(2,1)} collective-permute-done((bf16[2,384,256]{2,1,0:T(8,128)(2,1)S(1)}, bf16[2,384,256]{2,1,0:T(8,128)(2,1)}, u32[]{:S(2)}, u32[]{:S(2)}) %collective-permute-start.21) | collective-permute-done | bytes 393248 | tf_op jit(solution)/shard_map/ppermute | solution.py:256
  89.3 4.3 %project.7 = (bf16[2,256,256]{2,1,0:T(8,128)(2,1)}, bf16[2,256,256]{2,1,0:T(8,128)(2,1)}) custom-call(s32[4]{0:T(128)} %pad_add_fusion.ids_ref, bf16[512,1536]{1,0:T(8,128)(2,1)} %get-tuple-element.28.refs_0_, bf16[768,3072]{1,0:T(8,128)(2,1)} %bitcast.55, bf16[768,3072]{1,0:T(8,128)(2,1)} %bitcast.56, bf16[2,384,256]{2,1,0:T(8,128)(2,1)} %copy-done.4, ...), custom_call_target="tpu_custom_call" | custom-call | tf_op jit(solution)/shard_map/project/pallas_call | solution.py:188
  95.6 6.3 %collective-permute-done.17.refs_4_ = bf16[2,384,384]{2,1,0:T(8,128)(2,1)} collective-permute-done((bf16[2,384,384]{2,1,0:T(8,128)(2,1)}, bf16[2,384,384]{2,1,0:T(8,128)(2,1)}, u32[]{:S(2)}, u32[]{:S(2)}) %collective-permute-start.17) | collective-permute-done | bytes 589856 | tf_op jit(solution)/shard_map/ppermute | solution.py:256
  101.9 5.4 %project.6 = (bf16[2,256,384]{2,1,0:T(8,128)(2,1)}, bf16[2,256,384]{2,1,0:T(8,128)(2,1)}) custom-call(s32[4]{0:T(128)} %pad_add_fusion.ids_ref, bf16[512,1536]{1,0:T(8,128)(2,1)} %get-tuple-element.28.refs_0_, bf16[768,3072]{1,0:T(8,128)(2,1)} %bitcast.57, bf16[768,3072]{1,0:T(8,128)(2,1)} %bitcast.58, bf16[2,384,384]{2,1,0:T(8,128)(2,1)} %collective-permute-done.16.refs_3_, ...), custom_call_target="tpu_custom_call" | custom-call | tf_op jit(solution)/shard_map/project/pallas_call | solution.py:188
  108.8 1.6 %fusion.7 = bf16[256,256]{1,0:T(8,128)(2,1)} fusion(bf16[2,256,256]{2,1,0:T(8,128)(2,1)} %collective-permute-done.22, bf16[2,256,256]{2,1,0:T(8,128)(2,1)S(1)} %copy-done.8), kind=kLoop, calls=%fused_computation.29 | loop fusion | flops 262144 | bytes 393216 | tf_op jit(solution)/shard_map/convert_element_type | solution.py:215
  110.5 6.2 %collective-permute-done.13.refs_4_ = bf16[2,384,512]{2,1,0:T(8,128)(2,1)S(1)} collective-permute-done((bf16[2,384,512]{2,1,0:T(8,128)(2,1)S(1)}, bf16[2,384,512]{2,1,0:T(8,128)(2,1)S(1)}, u32[]{:S(2)}, u32[]{:S(2)}) %collective-permute-start.13) | collective-permute-done | bytes 786464 | tf_op jit(solution)/shard_map/ppermute | solution.py:256
  117.6 5.6 %project.5 = (bf16[2,256,512]{2,1,0:T(8,128)(2,1)}, bf16[2,256,512]{2,1,0:T(8,128)(2,1)}) custom-call(s32[4]{0:T(128)} %pad_add_fusion.ids_ref, bf16[512,1536]{1,0:T(8,128)(2,1)} %get-tuple-element.28.refs_0_, bf16[768,3072]{1,0:T(8,128)(2,1)} %bitcast.59, bf16[768,3072]{1,0:T(8,128)(2,1)} %bitcast.60, bf16[2,384,512]{2,1,0:T(8,128)(2,1)} %copy-done.1, ...), custom_call_target="tpu_custom_call" | custom-call | tf_op jit(solution)/shard_map/project/pallas_call | solution.py:188
  127.2 2.6 %collective-permute-start.19 = (bf16[256,384]{1,0:T(8,128)(2,1)S(1)}, bf16[256,384]{1,0:T(8,128)(2,1)S(1)}, u32[]{:S(2)}, u32[]{:S(2)}) collective-permute-start(bf16[256,384]{1,0:T(8,128)(2,1)S(1)} %fusion.6), channel_id=1, source_target_pairs={{0,8},{4,12},{8,0},{12,4},{1,9},{5,13},{9,1},{13,5},{2,10},{6,14},... | collective-permute-start | bytes 589832 | tf_op jit(solution)/shard_map/ppermute | solution.py:275
  130.9 4.5 %collective-permute-done.14 = bf16[2,256,512]{2,1,0:T(8,128)(2,1)S(1)} collective-permute-done((bf16[2,256,512]{2,1,0:T(8,128)(2,1)}, bf16[2,256,512]{2,1,0:T(8,128)(2,1)S(1)}, u32[]{:S(2)}, u32[]{:S(2)}) %collective-permute-start.14) | collective-permute-done | bytes 524320 | tf_op jit(solution)/shard_map/ppermute | solution.py:274
  136.1 10.2 %collective-permute-done.11 = bf16[256,384]{1,0:T(8,128)(2,1)S(1)} collective-permute-done((bf16[256,384]{1,0:T(8,128)(2,1)S(1)}, bf16[256,384]{1,0:T(8,128)(2,1)S(1)}, u32[]{:S(2)}, u32[]{:S(2)}) %collective-permute-start.11) | collective-permute-done | bytes 196640 | tf_op jit(solution)/shard_map/ppermute | solution.py:275
  147.3 3.2 %collective-permute-done.19 = bf16[256,384]{1,0:T(8,128)(2,1)S(1)} collective-permute-done((bf16[256,384]{1,0:T(8,128)(2,1)S(1)}, bf16[256,384]{1,0:T(8,128)(2,1)S(1)}, u32[]{:S(2)}, u32[]{:S(2)}) %collective-permute-start.19) | collective-permute-done | bytes 196640 | tf_op jit(solution)/shard_map/ppermute | solution.py:275
  151.6 3.7 %collective-permute-done.15 = bf16[256,512]{1,0:T(8,128)(2,1)S(1)} collective-permute-done((bf16[256,512]{1,0:T(8,128)(2,1)S(1)}, bf16[256,512]{1,0:T(8,128)(2,1)S(1)}, u32[]{:S(2)}, u32[]{:S(2)}) %collective-permute-start.15) | collective-permute-done | bytes 262176 | tf_op jit(solution)/shard_map/ppermute | solution.py:275
  (83 shorter events, 26.4 us)
Async XLA Ops:
  0.0 12.7 %collective-permute-start = (bf16[8,128,128]{2,1,0:T(8,128)(2,1)}, bf16[8,128,128]{2,1,0:T(8,128)(2,1)S(1)}, u32[]{:S(2)}, u32[]{:S(2)}) collective-permute-start(bf16[8,128,128]{2,1,0:T(8,128)(2,1)} %bitcast.63), channel_id=1, source_target_pairs={{0,2},{2,0},{1,3},{3,1},{4,6},{6,4},{5,7},{7,5},{8,10},{10,8},{9,1... | collective-permute-start | bytes 786440 | tf_op jit(solution)/shard_map/ppermute | solution.py:239
  0.5 14.6 %collective-permute-start.1 = (bf16[8,128,128]{2,1,0:T(8,128)(2,1)}, bf16[8,128,128]{2,1,0:T(8,128)(2,1)}, u32[]{:S(2)}, u32[]{:S(2)}) collective-permute-start(bf16[8,128,128]{2,1,0:T(8,128)(2,1)} %bitcast.65), channel_id=1, source_target_pairs={{0,2},{2,0},{1,3},{3,1},{4,6},{6,4},{5,7},{7,5},{8,10},{10,8},{9,1... | collective-permute-start | bytes 786440 | tf_op jit(solution)/shard_map/ppermute | solution.py:240
  2.8 61.6 %collective-permute-start.8 = (bf16[2,384,384]{2,1,0:T(8,128)(2,1)}, bf16[2,384,384]{2,1,0:T(8,128)(2,1)}, u32[]{:S(2)}, u32[]{:S(2)}) collective-permute-start(bf16[2,384,384]{2,1,0:T(8,128)(2,1)} %pad_maximum_fusion.2), channel_id=1, source_target_pairs={{0,4},{4,0},{8,12},{12,8},{1,5},{5,1},{9,13},{13,9},{2,6},{6,2},{1... | collective-permute-start | bytes 1769480 | tf_op jit(solution)/shard_map/ppermute | solution.py:255
  7.7 25.2 %collective-permute-start.20 = (bf16[2,384,256]{2,1,0:T(8,128)(2,1)}, bf16[2,384,256]{2,1,0:T(8,128)(2,1)S(1)}, u32[]{:S(2)}, u32[]{:S(2)}) collective-permute-start(bf16[2,384,256]{2,1,0:T(8,128)(2,1)} %pad_maximum_fusion.4), channel_id=1, source_target_pairs={{0,4},{4,0},{8,12},{12,8},{1,5},{5,1},{9,13},{13,9},{2,6},{6,2},{1... | collective-permute-start | bytes 1179656 | tf_op jit(solution)/shard_map/ppermute | solution.py:255
  9.8 65.2 %collective-permute-start.12 = (bf16[2,384,512]{2,1,0:T(8,128)(2,1)}, bf16[2,384,512]{2,1,0:T(8,128)(2,1)S(1)}, u32[]{:S(2)}, u32[]{:S(2)}) collective-permute-start(bf16[2,384,512]{2,1,0:T(8,128)(2,1)} %pad_maximum_fusion), channel_id=1, source_target_pairs={{0,4},{4,0},{8,12},{12,8},{1,5},{5,1},{9,13},{13,9},{2,6},{6,2},{1... | collective-permute-start | bytes 2359304 | tf_op jit(solution)/shard_map/ppermute | solution.py:255
  13.4 61.0 %collective-permute-start.16 = (bf16[2,384,384]{2,1,0:T(8,128)(2,1)}, bf16[2,384,384]{2,1,0:T(8,128)(2,1)}, u32[]{:S(2)}, u32[]{:S(2)}) collective-permute-start(bf16[2,384,384]{2,1,0:T(8,128)(2,1)} %pad_maximum_fusion.3), channel_id=1, source_target_pairs={{0,4},{4,0},{8,12},{12,8},{1,5},{5,1},{9,13},{13,9},{2,6},{6,2},{1... | collective-permute-start | bytes 1769480 | tf_op jit(solution)/shard_map/ppermute | solution.py:255
  32.7 28.3 %collective-permute-start.6 = (bf16[2,384,128]{2,1,0:T(8,128)(2,1)}, bf16[2,384,128]{2,1,0:T(8,128)(2,1)S(1)}, u32[]{:S(2)}, u32[]{:S(2)}) collective-permute-start(bf16[2,384,128]{2,1,0:T(8,128)(2,1)} %get-tuple-element.25), channel_id=1, source_target_pairs={{0,8},{4,12},{8,0},{12,4},{1,9},{5,13},{9,1},{13,5},{2,10},{6,14},... | collective-permute-start | bytes 589832 | tf_op jit(solution)/shard_map/ppermute | solution.py:266
  32.8 33.1 %collective-permute-start.5 = (bf16[2,384,128]{2,1,0:T(8,128)(2,1)}, bf16[2,384,128]{2,1,0:T(8,128)(2,1)S(1)}, u32[]{:S(2)}, u32[]{:S(2)}) collective-permute-start(bf16[2,384,128]{2,1,0:T(8,128)(2,1)} %get-tuple-element.24.refs_4_), channel_id=1, source_target_pairs={{0,2},{2,0},{1,3},{3,1},{4,6},{6,4},{5,7},{7,5},{8,10},{10,8},{9,1... | collective-permute-start | bytes 589832 | tf_op jit(solution)/shard_map/ppermute | solution.py:267
  61.1 11.8 %collective-permute-start.3 = (bf16[2,384,128]{2,1,0:T(8,128)(2,1)S(1)}, bf16[2,384,128]{2,1,0:T(8,128)(2,1)S(1)}, u32[]{:S(2)}, u32[]{:S(2)}) collective-permute-start(bf16[2,384,128]{2,1,0:T(8,128)(2,1)S(1)} %copy-done.16), channel_id=1, source_target_pairs={{0,8},{4,12},{8,0},{12,4},{1,9},{5,13},{9,1},{13,5},{2,10},{6,14},... | collective-permute-start | bytes 589832 | tf_op jit(solution)/shard_map/ppermute | solution.py:266
  64.4 16.5 %collective-permute-start.9 = (bf16[2,384,384]{2,1,0:T(8,128)(2,1)}, bf16[2,384,384]{2,1,0:T(8,128)(2,1)}, u32[]{:S(2)}, u32[]{:S(2)}) collective-permute-start(bf16[2,384,384]{2,1,0:T(8,128)(2,1)} %collective-permute-done.8.refs_10_), channel_id=1, source_target_pairs={{0,16},{16,0},{1,17},{17,1},{2,18},{18,2},{3,19},{19,3},{4,20},{20... | collective-permute-start | bytes 1769480 | tf_op jit(solution)/shard_map/ppermute | solution.py:256
  65.9 7.0 %collective-permute-start.2 = (bf16[2,384,128]{2,1,0:T(8,128)(2,1)S(1)}, bf16[2,384,128]{2,1,0:T(8,128)(2,1)S(1)}, u32[]{:S(2)}, u32[]{:S(2)}) collective-permute-start(bf16[2,384,128]{2,1,0:T(8,128)(2,1)S(1)} %copy-done.9), channel_id=1, source_target_pairs={{0,2},{2,0},{1,3},{3,1},{4,6},{6,4},{5,7},{7,5},{8,10},{10,8},{9,1... | collective-permute-start | bytes 589832 | tf_op jit(solution)/shard_map/ppermute | solution.py:267
  72.9 3.7 %collective-permute-start.7 = (bf16[2,384,128]{2,1,0:T(8,128)(2,1)S(1)}, bf16[2,384,128]{2,1,0:T(8,128)(2,1)S(1)}, u32[]{:S(2)}, u32[]{:S(2)}) collective-permute-start(bf16[2,384,128]{2,1,0:T(8,128)(2,1)S(1)} %collective-permute-done.6.refs_6_), channel_id=1, source_target_pairs={{0,2},{2,0},{1,3},{3,1},{4,6},{6,4},{5,7},{7,5},{8,10},{10,8},{9,1... | collective-permute-start | bytes 589832 | tf_op jit(solution)/shard_map/ppermute | solution.py:268
  72.9 16.4 %collective-permute-start.21 = (bf16[2,384,256]{2,1,0:T(8,128)(2,1)S(1)}, bf16[2,384,256]{2,1,0:T(8,128)(2,1)}, u32[]{:S(2)}, u32[]{:S(2)}) collective-permute-start(bf16[2,384,256]{2,1,0:T(8,128)(2,1)S(1)} %collective-permute-done.20.refs_3_), channel_id=1, source_target_pairs={{0,16},{16,0},{1,17},{17,1},{2,18},{18,2},{3,19},{19,3},{4,20},{20... | collective-permute-start | bytes 1179656 | tf_op jit(solution)/shard_map/ppermute | solution.py:256
  74.5 27.5 %collective-permute-start.17 = (bf16[2,384,384]{2,1,0:T(8,128)(2,1)}, bf16[2,384,384]{2,1,0:T(8,128)(2,1)}, u32[]{:S(2)}, u32[]{:S(2)}) collective-permute-start(bf16[2,384,384]{2,1,0:T(8,128)(2,1)} %collective-permute-done.16.refs_3_), channel_id=1, source_target_pairs={{0,16},{16,0},{1,17},{17,1},{2,18},{18,2},{3,19},{19,3},{4,20},{20... | collective-permute-start | bytes 1769480 | tf_op jit(solution)/shard_map/ppermute | solution.py:256
  75.0 41.7 %collective-permute-start.13 = (bf16[2,384,512]{2,1,0:T(8,128)(2,1)S(1)}, bf16[2,384,512]{2,1,0:T(8,128)(2,1)S(1)}, u32[]{:S(2)}, u32[]{:S(2)}) collective-permute-start(bf16[2,384,512]{2,1,0:T(8,128)(2,1)S(1)} %collective-permute-done.12.refs_3_), channel_id=1, source_target_pairs={{0,16},{16,0},{1,17},{17,1},{2,18},{18,2},{3,19},{19,3},{4,20},{20... | collective-permute-start | bytes 2359304 | tf_op jit(solution)/shard_map/ppermute | solution.py:256
  76.6 1.5 collective-permute-start.4
  93.6 15.2 %collective-permute-start.22 = (bf16[2,256,256]{2,1,0:T(8,128)(2,1)}, bf16[2,256,256]{2,1,0:T(8,128)(2,1)}, u32[]{:S(2)}, u32[]{:S(2)}) collective-permute-start(bf16[2,256,256]{2,1,0:T(8,128)(2,1)} %get-tuple-element.34), channel_id=1, source_target_pairs={{0,1},{1,0},{2,3},{3,2},{4,5},{5,4},{6,7},{7,6},{8,9},{9,8},{10,11... | collective-permute-start | bytes 786440 | tf_op jit(solution)/shard_map/ppermute | solution.py:274
  95.1 29.5 %collective-permute-start.10 = (bf16[2,256,384]{2,1,0:T(8,128)(2,1)}, bf16[2,256,384]{2,1,0:T(8,128)(2,1)}, u32[]{:S(2)}, u32[]{:S(2)}) collective-permute-start(bf16[2,256,384]{2,1,0:T(8,128)(2,1)} %get-tuple-element.27), channel_id=1, source_target_pairs={{0,1},{1,0},{2,3},{3,2},{4,5},{5,4},{6,7},{7,6},{8,9},{9,8},{10,11... | collective-permute-start | bytes 1179656 | tf_op jit(solution)/shard_map/ppermute | solution.py:274
  107.3 18.8 %collective-permute-start.18 = (bf16[2,256,384]{2,1,0:T(8,128)(2,1)}, bf16[2,256,384]{2,1,0:T(8,128)(2,1)}, u32[]{:S(2)}, u32[]{:S(2)}) collective-permute-start(bf16[2,256,384]{2,1,0:T(8,128)(2,1)} %get-tuple-element.32), channel_id=1, source_target_pairs={{0,1},{1,0},{2,3},{3,2},{4,5},{5,4},{6,7},{7,6},{8,9},{9,8},{10,11... | collective-permute-start | bytes 1179656 | tf_op jit(solution)/shard_map/ppermute | solution.py:274
  110.4 19.4 %collective-permute-start.23 = (bf16[256,256]{1,0:T(8,128)(2,1)}, bf16[256,256]{1,0:T(8,128)(2,1)}, u32[]{:S(2)}, u32[]{:S(2)}) collective-permute-start(bf16[256,256]{1,0:T(8,128)(2,1)} %fusion.7), channel_id=1, source_target_pairs={{0,8},{4,12},{8,0},{12,4},{1,9},{5,13},{9,1},{13,5},{2,10},{6,14},... | collective-permute-start | bytes 393224 | tf_op jit(solution)/shard_map/ppermute | solution.py:275
  123.1 12.2 %collective-permute-start.14 = (bf16[2,256,512]{2,1,0:T(8,128)(2,1)}, bf16[2,256,512]{2,1,0:T(8,128)(2,1)S(1)}, u32[]{:S(2)}, u32[]{:S(2)}) collective-permute-start(bf16[2,256,512]{2,1,0:T(8,128)(2,1)} %get-tuple-element.30), channel_id=1, source_target_pairs={{0,1},{1,0},{2,3},{3,2},{4,5},{5,4},{6,7},{7,6},{8,9},{9,8},{10,11... | collective-permute-start | bytes 1572872 | tf_op jit(solution)/shard_map/ppermute | solution.py:274
  125.7 20.7 %collective-permute-start.11 = (bf16[256,384]{1,0:T(8,128)(2,1)S(1)}, bf16[256,384]{1,0:T(8,128)(2,1)S(1)}, u32[]{:S(2)}, u32[]{:S(2)}) collective-permute-start(bf16[256,384]{1,0:T(8,128)(2,1)S(1)} %fusion.5), channel_id=1, source_target_pairs={{0,8},{4,12},{8,0},{12,4},{1,9},{5,13},{9,1},{13,5},{2,10},{6,14},... | collective-permute-start | bytes 589832 | tf_op jit(solution)/shard_map/ppermute | solution.py:275
  127.2 23.4 %collective-permute-start.19 = (bf16[256,384]{1,0:T(8,128)(2,1)S(1)}, bf16[256,384]{1,0:T(8,128)(2,1)S(1)}, u32[]{:S(2)}, u32[]{:S(2)}) collective-permute-start(bf16[256,384]{1,0:T(8,128)(2,1)S(1)} %fusion.6), channel_id=1, source_target_pairs={{0,8},{4,12},{8,0},{12,4},{1,9},{5,13},{9,1},{13,5},{2,10},{6,14},... | collective-permute-start | bytes 589832 | tf_op jit(solution)/shard_map/ppermute | solution.py:275
  135.4 19.8 %collective-permute-start.15 = (bf16[256,512]{1,0:T(8,128)(2,1)S(1)}, bf16[256,512]{1,0:T(8,128)(2,1)S(1)}, u32[]{:S(2)}, u32[]{:S(2)}) collective-permute-start(bf16[256,512]{1,0:T(8,128)(2,1)S(1)} %fusion.3), channel_id=1, source_target_pairs={{0,8},{4,12},{8,0},{12,4},{1,9},{5,13},{9,1},{13,5},{2,10},{6,14},... | collective-permute-start | bytes 786440 | tf_op jit(solution)/shard_map/ppermute | solution.py:275
  (17 other events, 260.2 us)
